TPU v7x, 32 devices: a whole 2x2x4 slice. The times are simulated.
32 devices in a mesh: fsdp: 8 (over y, x, core), rep: 4 (over z).
Axes of the slice: x: 2, y: 2, z: 4, core: 2. Of those that a mesh axis runs over, the one named last changes fastest.
Arguments:
- layer_input: bfloat16 [128, 512, 768], P(('fsdp', 'rep')), may hold values from -6 to 6
- segment_length_pairs: int32 [128, 2], P(('fsdp', 'rep')), may hold values from 16 to 496, as said below
- query_key_value_weight: bfloat16 [3, 768, 768], P(None, 'fsdp', 'rep'), may hold values from -0.21875 to 0.21875
- output_weight: bfloat16 [768, 768], P('fsdp', 'rep'), may hold values from -0.875 to 0.875
- attention_bias: bfloat16 [3, 768], P(None, 'fsdp'), may hold values from -1.5 to 1.5
- adapter_down: bfloat16 [2, 768, 8], P(None, 'fsdp'), may hold values from -0.21875 to 0.21875
- adapter_up: bfloat16 [2, 8, 768], replicated, may hold values from -1 to 1
- layernorm_gain: bfloat16 [2, 768], P(None, 'fsdp'), may hold values from 0.5 to 1.5
- layernorm_bias: bfloat16 [2, 768], P(None, 'fsdp'), may hold values from -1.5 to 1.5
- feedforward_in_weight: bfloat16 [768, 3072], P('fsdp', 'rep'), may hold values from -0.21875 to 0.21875
- feedforward_in_bias: bfloat16 [3072], P('fsdp'), may hold values from -1.5 to 1.5
- feedforward_out_weight: bfloat16 [3072, 768], P('fsdp', 'rep'), may hold values from -0.21875 to 0.21875
- feedforward_out_bias: bfloat16 [768], P('fsdp'), may hold values from -1.5 to 1.5
- output_cotangent: bfloat16 [128, 512, 768], P(('fsdp', 'rep')), may hold values from -6 to 6
Outputs:
- hidden_out: bfloat16 [128, 512, 768], P(('fsdp', 'rep'))
- hidden_grad: bfloat16 [128, 512, 768], P(('fsdp', 'rep'))
- adapter_up_gradient: float32 [2, 8, 768], replicated
Inputs may be any that keep to these rules, and one draw needn't show every extreme that they name: Item i uses slots 0 to segment_length_pairs[i,0] + segment_length_pairs[i,1] - 1 of its 512; that total is at most 512, and exactly 512 for every item whose index is a multiple of 4. The first segment is at most 256. Item 0 has a first segment of 16 and a second of 496; item 1 has a second segment of 16.
All inputs are finite; a program needn't handle non-finite values.
Results may differ from a plain program's by a relative error of at most 0.017.
Values may be sent and summed in bfloat16 or wider, within the bound.
No kernel may reach another device: no remote copies, remote signals or barrier semaphores. Data moves between devices by JAX's collectives and lax.ppermute only.
A program may use at most 320 MiB of HBM per device.

v0:
```python
import math

import jax
import jax.numpy as jnp
from jax import lax
from jax.sharding import PartitionSpec as P

MODEL_WIDTH = 768
H = 12
HD = 64
ADAPTER_RANK = 8
ADAPTER_ALPHA = 16
L = 512
MB = 2


def collect_frozen(frozen_args):
    (
        qkv_part,
        out_part,
        in_part,
        back_part,
        attn_part,
        down_part,
        gain_part,
        shift_part,
        in_bias_part,
        back_bias_part,
    ) = frozen_args
    columns = (
        lax.all_gather(qkv_part, "rep", axis=2, tiled=True),
        lax.all_gather(out_part, "rep", axis=1, tiled=True),
        lax.all_gather(in_part, "rep", axis=1, tiled=True),
        lax.all_gather(back_part, "rep", axis=1, tiled=True),
    )
    return (
        lax.all_gather(columns[0], "fsdp", axis=1, tiled=True),
        lax.all_gather(columns[1], "fsdp", axis=0, tiled=True),
        lax.all_gather(columns[2], "fsdp", axis=0, tiled=True),
        lax.all_gather(columns[3], "fsdp", axis=0, tiled=True),
        lax.all_gather(attn_part, "fsdp", axis=1, tiled=True),
        lax.all_gather(down_part, "fsdp", axis=1, tiled=True),
        lax.all_gather(gain_part, "fsdp", axis=1, tiled=True),
        lax.all_gather(shift_part, "fsdp", axis=1, tiled=True),
        lax.all_gather(in_bias_part, "fsdp", axis=0, tiled=True),
        lax.all_gather(back_bias_part, "fsdp", axis=0, tiled=True),
    )


def adapter_sum(adapter_grad_term):
    return lax.psum(adapter_grad_term, ("fsdp", "rep"))


def exact_gelu(values):
    return jax.nn.gelu(values, approximate=False)


def layer_norm_rows(values):
    centered = values - jnp.mean(values, axis=-1, keepdims=True)
    spread = jnp.mean(centered * centered, axis=-1, keepdims=True)
    inverse = lax.rsqrt(spread + 1e-05)
    return (centered * inverse, inverse)


def norm_back(output_gradient, normed, inverse, gain):
    scaled = output_gradient * gain
    return inverse * (
        scaled
        - jnp.mean(scaled, axis=-1, keepdims=True)
        - normed * jnp.mean(scaled * normed, axis=-1, keepdims=True)
    )


def attention_scores(query_bf, key_bf, valid_keys):
    head_scale = 1.0 / math.sqrt(HD)
    raw_scores = (
        jnp.einsum("ilhe,imhe->ihlm", query_bf, key_bf, preferred_element_type=jnp.float32)
        * head_scale
    )
    return jnp.where(valid_keys[:, None, None, :], raw_scores, -1e30)


def forward_sweep(input_bundle, valid_keys, weight_bundle, adapter_up):
    (
        qkv_full,
        out_full,
        in_full,
        back_full,
        attention_offset,
        down_matrix_whole,
        norm_gains,
        norm_shifts,
        in_shift,
        back_shift,
    ) = weight_bundle
    item_count = valid_keys.shape[0]
    row_count = input_bundle.shape[0]
    adapter_scale = ADAPTER_ALPHA / ADAPTER_RANK
    attention_single = attention_offset.astype(jnp.float32)
    adapter_reduced = jnp.einsum(
        "td,kdr->tkr", input_bundle, down_matrix_whole, preferred_element_type=jnp.float32
    ).astype(jnp.bfloat16)
    projected_rows = jnp.einsum(
        "td,kde->tke", input_bundle, qkv_full, preferred_element_type=jnp.float32
    )
    adapter_term = jnp.einsum(
        "lsn,snb->lsb", adapter_reduced, adapter_up, preferred_element_type=jnp.float32
    )
    head_shape = (item_count, L, H, HD)
    query_bf = (
        (projected_rows[:, 0] + attention_single[0] + adapter_scale * adapter_term[:, 0])
        .astype(jnp.bfloat16)
        .reshape(head_shape)
    )
    key_bf = projected_rows[:, 1].astype(jnp.bfloat16).reshape(head_shape)
    value_bf = (
        (projected_rows[:, 2] + attention_single[1] + adapter_scale * adapter_term[:, 1])
        .astype(jnp.bfloat16)
        .reshape(head_shape)
    )
    scores = attention_scores(query_bf, key_bf, valid_keys)
    row_max = jnp.max(scores, axis=-1, keepdims=True)
    log_total = row_max + jnp.log(jnp.sum(jnp.exp(scores - row_max), axis=-1, keepdims=True))
    probs_bf = jnp.exp(scores - log_total).astype(jnp.bfloat16)
    mixed_bf = (
        jnp.einsum("ihlm,imhe->ilhe", probs_bf, value_bf, preferred_element_type=jnp.float32)
        .astype(jnp.bfloat16)
        .reshape(row_count, MODEL_WIDTH)
    )
    first_sum = (
        input_bundle.astype(jnp.float32)
        + jnp.dot(mixed_bf, out_full, preferred_element_type=jnp.float32)
        + attention_single[2]
    )
    normed_one, inverse_one = layer_norm_rows(first_sum)
    gain_float = norm_gains.astype(jnp.float32)
    shift_float = norm_shifts.astype(jnp.float32)
    hidden_one = normed_one * gain_float[0] + shift_float[0]
    ffn_inner = jnp.dot(
        hidden_one.astype(jnp.bfloat16), in_full, preferred_element_type=jnp.float32
    ) + in_shift.astype(jnp.float32)
    activation = exact_gelu(ffn_inner).astype(jnp.bfloat16)
    second_sum = (
        hidden_one
        + jnp.dot(activation, back_full, preferred_element_type=jnp.float32)
        + back_shift.astype(jnp.float32)
    )
    normed_two, inverse_two = layer_norm_rows(second_sum)
    layer_output = (normed_two * gain_float[1] + shift_float[1]).astype(jnp.bfloat16)
    saved_values = (
        adapter_reduced,
        query_bf,
        key_bf,
        value_bf,
        log_total,
        normed_one,
        inverse_one,
        ffn_inner,
        normed_two,
        inverse_two,
    )
    return (saved_values, layer_output)


def reverse_sweep(output_gradient, saved_values, valid_keys, weight_bundle, adapter_up):
    (
        qkv_full,
        out_full,
        in_full,
        back_full,
        attention_offset,
        down_matrix_whole,
        norm_gains,
        norm_shifts,
        in_shift,
        back_shift,
    ) = weight_bundle
    (
        adapter_reduced,
        query_bf,
        key_bf,
        value_bf,
        log_total,
        normed_one,
        inverse_one,
        ffn_inner,
        normed_two,
        inverse_two,
    ) = saved_values
    item_count = valid_keys.shape[0]
    row_count = output_gradient.shape[0]
    adapter_scale = ADAPTER_ALPHA / ADAPTER_RANK
    head_scale = 1.0 / math.sqrt(HD)
    gain_float = norm_gains.astype(jnp.float32)
    grad_second = norm_back(
        output_gradient.astype(jnp.float32), normed_two, inverse_two, gain_float[1]
    )
    grad_act = jnp.einsum(
        "td,fd->tf", grad_second.astype(jnp.bfloat16), back_full, preferred_element_type=jnp.float32
    )
    gelu_value, gelu_pull = jax.vjp(exact_gelu, ffn_inner)
    grad_inner = gelu_pull(grad_act)[0].astype(jnp.bfloat16)
    grad_hidden = grad_second + jnp.einsum(
        "tf,df->td", grad_inner, in_full, preferred_element_type=jnp.float32
    )
    grad_first = norm_back(grad_hidden, normed_one, inverse_one, gain_float[0])
    grad_mixed = jnp.einsum(
        "td,ed->te", grad_first.astype(jnp.bfloat16), out_full, preferred_element_type=jnp.float32
    )
    grad_mixed = grad_mixed.astype(jnp.bfloat16).reshape(item_count, L, H, HD)
    scores = attention_scores(query_bf, key_bf, valid_keys)
    attn_weights = jnp.exp(scores - log_total)
    probs_bf = attn_weights.astype(jnp.bfloat16)
    grad_probs = jnp.einsum(
        "ilhe,imhe->ihlm", grad_mixed, value_bf, preferred_element_type=jnp.float32
    )
    value_gradient = jnp.einsum(
        "ihlm,ilhe->imhe", probs_bf, grad_mixed, preferred_element_type=jnp.float32
    ).astype(jnp.bfloat16)
    row_inner = jnp.sum(attn_weights * grad_probs, axis=-1, keepdims=True)
    grad_scores = (attn_weights * (grad_probs - row_inner)).astype(jnp.bfloat16)
    query_gradient = (
        jnp.einsum("ihlm,imhe->ilhe", grad_scores, key_bf, preferred_element_type=jnp.float32)
        * head_scale
    ).astype(jnp.bfloat16)
    grad_key = (
        jnp.einsum("ihlm,ilhe->imhe", grad_scores, query_bf, preferred_element_type=jnp.float32)
        * head_scale
    ).astype(jnp.bfloat16)
    query_gradient = query_gradient.reshape(row_count, MODEL_WIDTH)
    grad_key = grad_key.reshape(row_count, MODEL_WIDTH)
    value_gradient = value_gradient.reshape(row_count, MODEL_WIDTH)
    grad_proj = jnp.stack([query_gradient, grad_key, value_gradient], axis=1)
    input_gradient = grad_first + jnp.einsum(
        "tke,kde->td", grad_proj, qkv_full, preferred_element_type=jnp.float32
    )
    adapter_gradient = jnp.stack([query_gradient, value_gradient], axis=1)
    adapter_grad_term = adapter_scale * jnp.einsum(
        "hiu,his->ius", adapter_reduced, adapter_gradient, preferred_element_type=jnp.float32
    )
    grad_u = (
        adapter_scale
        * jnp.einsum(
            "pqf,qnf->pqn", adapter_gradient, adapter_up, preferred_element_type=jnp.float32
        )
    ).astype(jnp.bfloat16)
    input_gradient = input_gradient + jnp.einsum(
        "tkr,kdr->td", grad_u, down_matrix_whole, preferred_element_type=jnp.float32
    )
    return (input_gradient.astype(jnp.bfloat16), adapter_grad_term)


def per_device(
    layer_input,
    segment_length_pairs,
    query_key_value_weight,
    output_weight,
    attention_bias,
    adapter_down,
    adapter_up,
    layernorm_gain,
    layernorm_bias,
    feedforward_in_weight,
    feedforward_in_bias,
    feedforward_out_weight,
    feedforward_out_bias,
    output_cotangent,
):
    frozen_args = (
        query_key_value_weight,
        output_weight,
        feedforward_in_weight,
        feedforward_out_weight,
        attention_bias,
        adapter_down,
        layernorm_gain,
        layernorm_bias,
        feedforward_in_bias,
        feedforward_out_bias,
    )
    per_micro = layer_input.shape[0] // MB
    row_count = per_micro * L
    token_count = layer_input.shape[0] * L * lax.axis_size("fsdp") * lax.axis_size("rep")
    positions = jnp.arange(L, dtype=jnp.int32)
    layer_outputs = []
    input_gradients = []
    gradient_total = jnp.zeros((2, ADAPTER_RANK, MODEL_WIDTH), jnp.float32)
    for micro_index in range(MB):
        weight_bundle = collect_frozen(frozen_args)
        first_item = micro_index * per_micro
        input_bundle = layer_input[first_item : first_item + per_micro].reshape(
            row_count, MODEL_WIDTH
        )
        valid_counts = (
            segment_length_pairs[first_item : first_item + per_micro, 0]
            + segment_length_pairs[first_item : first_item + per_micro, 1]
        )
        valid_keys = positions[None, :] < valid_counts[:, None]
        saved_values, layer_output = forward_sweep(
            input_bundle, valid_keys, weight_bundle, adapter_up
        )
        weight_bundle = collect_frozen(frozen_args)
        gradient_rows = output_cotangent[first_item : first_item + per_micro].reshape(
            row_count, MODEL_WIDTH
        )
        input_gradient, adapter_grad_term = reverse_sweep(
            gradient_rows, saved_values, valid_keys, weight_bundle, adapter_up
        )
        gradient_total = gradient_total + adapter_grad_term
        layer_outputs.append(layer_output.reshape(per_micro, L, MODEL_WIDTH))
        input_gradients.append(input_gradient.reshape(per_micro, L, MODEL_WIDTH))
    gradient_total = adapter_sum(gradient_total)
    adapter_up_gradient = gradient_total / math.sqrt(token_count)
    return (
        jnp.concatenate(layer_outputs, axis=0),
        jnp.concatenate(input_gradients, axis=0),
        adapter_up_gradient,
    )


def solution(mesh):
    in_specs = (
        P(("fsdp", "rep"), None, None),
        P(("fsdp", "rep"), None),
        P(None, "fsdp", "rep"),
        P("fsdp", "rep"),
        P(None, "fsdp"),
        P(None, "fsdp", None),
        P(),
        P(None, "fsdp"),
        P(None, "fsdp"),
        P("fsdp", "rep"),
        P("fsdp"),
        P("fsdp", "rep"),
        P("fsdp"),
        P(("fsdp", "rep"), None, None),
    )
    out_specs = (P(("fsdp", "rep"), None, None), P(("fsdp", "rep"), None, None), P())
    return jax.shard_map(
        per_device, mesh=mesh, in_specs=in_specs, out_specs=out_specs, check_vma=False
    )
```

profile of v0, /device:TPU:0, one launch (start us, length us, event | category | flops | bytes accessed | tf_op | source)
XLA Modules:
  0.0 779.1 jit_solution(15271656868781157294)
XLA Ops:
  8.4 21.9 %all_gather.28 = bf16[3,96,768]{1,0,2:T(4,128)(2,1)} all-gather(bf16[3,96,192]{1,0,2:T(4,128)(2,1)S(1)} %copy.229), channel_id=1, replica_groups=mesh['fsdp'=8,'rep'=4] {'rep'}, dimensions={2}, use_global_device_ids=true | all-gather | bytes 552960 | tf_op jit(solution)/shard_map/all_gather | solution.py:31
  33.4 13.6 %all_gather.32 = bf16[96,768]{0,1:T(8,128)(2,1)S(1)} all-gather(bf16[96,192]{0,1:T(8,128)(2,1)S(1)} %copy.244), channel_id=1, replica_groups=mesh['fsdp'=8,'rep'=4] {'rep'}, dimensions={1}, use_global_device_ids=true | all-gather | bytes 184320 | tf_op jit(solution)/shard_map/all_gather | solution.py:32
  47.8 17.4 %all_gather.36 = bf16[96,3072]{1,0:T(8,128)(2,1)} all-gather(bf16[96,768]{1,0:T(8,128)(2,1)} %param.23), channel_id=1, replica_groups=mesh['fsdp'=8,'rep'=4] {'rep'}, dimensions={1}, use_global_device_ids=true | all-gather | bytes 737280 | tf_op jit(solution)/shard_map/all_gather | solution.py:33
  65.3 16.5 %all_gather.39 = bf16[384,768]{0,1:T(8,128)(2,1)} all-gather(bf16[384,192]{0,1:T(8,128)(2,1)} %param.25), channel_id=1, replica_groups=mesh['fsdp'=8,'rep'=4] {'rep'}, dimensions={1}, use_global_device_ids=true | all-gather | bytes 737280 | tf_op jit(solution)/shard_map/all_gather | solution.py:34
  83.4 12.1 %all-reduce = bf16[768]{0:T(1024)(128)(2,1)S(1)} all-reduce(bf16[768]{0:T(1024)(128)(2,1)S(1)} %dynamic-update-slice), channel_id=1, replica_groups=mesh['fsdp'=8,'rep'=4] {'fsdp'}, use_global_device_ids=true, to_apply=%add | all-reduce | flops 768 | bytes 3072
  96.1 8.7 %all-gather.1 = bf16[8,96,2]{1,2,0:T(2,128)(2,1)S(1)} all-gather(bf16[1,96,2]{1,2,0:T(2,128)(2,1)S(1)} %bitcast.229), channel_id=1, replica_groups=mesh['fsdp'=8,'rep'=4] {'fsdp'}, dimensions={0}, use_global_device_ids=true | all-gather | bytes 3456 | tf_op jit(solution)/shard_map/all_gather | solution.py:43
  104.9 8.1 %all-gather.2 = bf16[8,96,2]{1,2,0:T(2,128)(2,1)S(1)} all-gather(bf16[1,96,2]{1,2,0:T(2,128)(2,1)S(1)} %bitcast.230), channel_id=1, replica_groups=mesh['fsdp'=8,'rep'=4] {'fsdp'}, dimensions={0}, use_global_device_ids=true | all-gather | bytes 3456 | tf_op jit(solution)/shard_map/all_gather | solution.py:44
  113.0 9.0 %all-gather = bf16[8,96,3]{1,2,0:T(4,128)(2,1)S(1)} all-gather(bf16[1,96,3]{1,2,0:T(4,128)(2,1)S(1)} %bitcast.228), channel_id=1, replica_groups=mesh['fsdp'=8,'rep'=4] {'fsdp'}, dimensions={0}, use_global_device_ids=true | all-gather | bytes 5184 | tf_op jit(solution)/shard_map/all_gather | solution.py:41
  124.8 8.2 %all-gather.3 = bf16[8,1,384]{2,1,0:T(2,128)(2,1)S(1)} all-gather(bf16[1,1,384]{2,1,0:T(2,128)(2,1)S(1)} %reshape.269), channel_id=1, replica_groups=mesh['fsdp'=8,'rep'=4] {'fsdp'}, dimensions={0}, use_global_device_ids=true | all-gather | bytes 6912 | tf_op jit(solution)/shard_map/all_gather | solution.py:45
  133.1 9.6 %all_gather.31 = bf16[2,768,8]{2,0,1:T(2,128)(2,1)S(1)} all-gather(bf16[2,96,8]{2,0,1:T(2,128)(2,1)S(1)} %copy.233), channel_id=1, replica_groups=mesh['fsdp'=8,'rep'=4] {'fsdp'}, dimensions={1}, use_global_device_ids=true | all-gather | bytes 27648 | tf_op jit(solution)/shard_map/all_gather | solution.py:42
  252.1 11.1 %fusion = (f32[2,12,512]{2,1,0:T(8,128)S(1)}, f32[2,12,512,512]{2,3,1,0:T(8,128)}) fusion(pred[2,512]{1,0:T(4,128)(4,1)S(1)} %get-tuple-element.62, bf16[2,512,12,64]{1,0,3,2:T(2,128)(2,1)S(1)} %convert_element_type.205, bf16[2,512,12,64]{1,0,3,2:T(2,128)(2,1)S(1)} %get-tuple-element.36), kind=kOutput, calls=%fused_computation.10 | convolution fusion | flops 824168448 | bytes 28361728 | tf_op jit(solution)/shard_map/ilhe,imhe->ihlm/dot_general | solution.py:77
  263.2 12.8 %exponential_reduce_fusion.1 = f32[2,12,512]{2,1,0:T(8,128)S(1)} fusion(f32[2,12,512,512]{2,3,1,0:T(8,128)} %get-tuple-element.45, f32[2,12,512]{2,1,0:T(8,128)S(1)} %get-tuple-element.44, pred[2,512]{1,0:T(4,128)(4,1)S(1)} %get-tuple-element.62), kind=kLoop, calls=%fused_computation.8 | loop fusion | flops 25153536 | bytes 25265152 | tf_op jit(solution)/shard_map/reduce_sum | solution.py:123
  280.5 11.9 %fusion.66 = bf16[2,512,12,64]{1,3,2,0:T(8,128)(2,1)S(1)} fusion(bf16[2,512,12,64]{1,0,3,2:T(2,128)(2,1)S(1)} %get-tuple-element.38, f32[2,12,512,512]{2,3,1,0:T(8,128)} %get-tuple-element.45, f32[2,12,512]{2,1,0:T(8,128)S(1)} %log_add_fusion.1, pred[2,512]{1,0:T(4,128)(4,1)S(1)} %get-tuple-element.62), kind=kOutput, calls=%fused_computation.152 | convolution fusion | flops 831258624 | bytes 28361728 | tf_op jit(solution)/shard_map/ihlm,imhe->ilhe/dot_general | solution.py:126
  301.6 11.1 %fusion.1 = (f32[2,12,512]{2,1,0:T(8,128)S(1)}, f32[2,12,512,512]{2,3,1,0:T(8,128)}) fusion(pred[2,512]{1,0:T(4,128)(4,1)S(1)} %get-tuple-element.61, bf16[2,512,12,64]{1,0,3,2:T(2,128)(2,1)S(1)} %convert_element_type.220, bf16[2,512,12,64]{1,0,3,2:T(2,128)(2,1)S(1)} %copy-done.7), kind=kOutput, calls=%fused_computation.11 | convolution fusion | flops 824168448 | bytes 28361728 | tf_op jit(solution)/shard_map/ilhe,imhe->ihlm/dot_general | solution.py:77
  312.7 11.2 %exponential_reduce_fusion = f32[2,12,512]{2,1,0:T(8,128)S(1)} fusion(f32[2,12,512,512]{2,3,1,0:T(8,128)} %get-tuple-element.43, f32[2,12,512]{2,1,0:T(8,128)S(1)} %get-tuple-element.42, pred[2,512]{1,0:T(4,128)(4,1)S(1)} %get-tuple-element.61), kind=kLoop, calls=%fused_computation.5 | loop fusion | flops 25153536 | bytes 25265152 | tf_op jit(solution)/shard_map/reduce_sum | solution.py:123
  324.0 11.6 %fusion.67 = bf16[2,512,12,64]{1,3,2,0:T(8,128)(2,1)S(1)} fusion(bf16[2,512,12,64]{1,0,3,2:T(2,128)(2,1)S(1)} %copy-done.29, f32[2,12,512,512]{2,3,1,0:T(8,128)} %get-tuple-element.43, f32[2,12,512]{2,1,0:T(8,128)S(1)} %log_add_fusion, pred[2,512]{1,0:T(4,128)(4,1)S(1)} %get-tuple-element.61), kind=kOutput, calls=%fused_computation.153 | convolution fusion | flops 831258624 | bytes 28361728 | tf_op jit(solution)/shard_map/ihlm,imhe->ilhe/dot_general | solution.py:126
  341.6 8.3 %fusion.48 = f32[1024,3072]{1,0:T(8,128)S(1)} fusion(bf16[768,3072]{1,0:T(8,128)(2,1)} %all-gather.13.cloned.1.call-done, f32[1024,768]{1,0:T(8,128)} %copy-done.38, f32[1024]{0:T(1024)S(1)} %add_rsqrt_fusion.1, f32[1024]{0:T(1024)S(1)} %broadcast_multiply_fusion.8, f32[768]{0:T(1024)S(1)} %get-tuple-element.17, f32[768]{0:T(1024)S(1)} %get-tuple-element.63), kind=kOutput, calls=%fused_computation.136 | convolution fusion | flops 4835770368 | bytes 20461568 | tf_op jit(solution)/shard_map/dot_general | solution.py:139
  354.5 59.2 %fusion.4 = (f32[1024,3072]{1,0:T(8,128)}, f32[1024,3072]{1,0:T(8,128)}, f32[1024,3072]{1,0:T(8,128)}) fusion(f32[3072]{0:T(1024)S(1)} %bitcast.223, f32[1024,3072]{1,0:T(8,128)S(1)} %fusion.48, bf16[768,3072]{1,0:T(8,128)(2,1)S(1)} %copy-done.81, f32[1024,768]{1,0:T(8,128)S(1)} %copy-done.35, f32[768]{0:T(1024)S(1)} %get-tuple-element.17, ...), kind=kOutput, calls=%fused_computation.16 | convolution fusion | flops 5232132096 | bytes 58222592 | tf_op jit(solution)/shard_map/dot_general | solution.py:139
  413.7 12.6 %fusion.147 = (f32[1024]{0:T(1024)S(1)}, f32[1024,768]{1,0:T(8,128)S(1)}) fusion(f32[768]{0:T(1024)S(1)} %copy-done.66, bf16[3072,768]{0,1:T(8,128)(2,1)} %all-gather.15.cloned.1.call-done, f32[1024,3072]{1,0:T(8,128)} %get-tuple-element.34, f32[1024,3072]{1,0:T(8,128)} %get-tuple-element.50, f32[3072]{0:T(1024)S(1)} %bitcast.224, ...), kind=kOutput, calls=%fused_computation.262 | convolution fusion | flops 4849925120 | bytes 36209664 | tf_op jit(solution)/shard_map/dot_general | solution.py:145
  427.0 16.0 %fusion.148 = (f32[1024]{0:T(1024)S(1)}, f32[1024,768]{1,0:T(8,128)S(1)}) fusion(f32[768]{0:T(1024)S(1)} %copy-done.66, bf16[3072,768]{0,1:T(8,128)(2,1)} %all-gather.15.cloned.1.call-done, f32[1024,3072]{1,0:T(8,128)} %get-tuple-element.35, f32[1024,3072]{1,0:T(8,128)} %copy-done.88, f32[3072]{0:T(1024)S(1)} %bitcast.225, f32[768]{0:T(1024)S(1)} %get-tuple-element.17, ...), kind=kOutput, calls=%fused_computation.263 | convolution fusion | flops 4849925120 | bytes 36209664 | tf_op jit(solution)/shard_map/dot_general | solution.py:145
  451.9 22.1 %fusion.140 = (f32[1024]{0:T(1024)S(1)}, f32[1024]{0:T(1024)S(1)}, f32[1024,768]{1,0:T(8,128)}) fusion(f32[1024]{0:T(1024)S(1)} %add_rsqrt_fusion.3, f32[1024,768]{1,0:T(8,128)} %copy-done.34, f32[1024]{0:T(1024)S(1)} %broadcast_multiply_fusion.10, f32[768]{0:T(1024)S(1)} %get-tuple-element.63, f32[1024,768]{1,0:T(8,128)} %get-tuple-element.31, ...), kind=kOutput, calls=%fused_computation.255 | convolution fusion | flops 9717151744 | bytes 44071936 | tf_op jit(solution)/shard_map/tf,df->td/dot_general | solution.py:203
  482.9 12.8 %fusion.68 = bf16[2,512,12,64]{1,3,2,0:T(8,128)(2,1)} fusion(bf16[2,512,12,64]{1,0,3,2:T(2,128)(2,1)S(1)} %reshape.254, f32[2,12,512,512]{2,3,1,0:T(8,128)} %get-tuple-element.45, f32[2,12,512]{2,1,0:T(8,128)S(1)} %copy-done.48, pred[2,512]{1,0:T(4,128)(4,1)S(1)} %copy-done.56), kind=kOutput, calls=%fused_computation.154 | convolution fusion | flops 831258624 | bytes 28361728 | tf_op jit(solution)/shard_map/ihlm,ilhe->imhe/dot_general | solution.py:217
  495.7 19.7 %multiply_reduce_fusion.1 = (f32[2,12,512]{2,1,0:T(8,128)S(1)}, f32[2,12,512,512]{2,3,1,0:T(8,128)}) fusion(f32[2,12,512,512]{2,3,1,0:T(8,128)} %get-tuple-element.45, f32[2,12,512]{2,1,0:T(8,128)S(1)} %copy-done.48, pred[2,512]{1,0:T(4,128)(4,1)S(1)} %copy-done.56, bf16[2,512,12,64]{1,0,3,2:T(2,128)(2,1)S(1)} %copy-done.32, ...), kind=kOutput, calls=%fused_computation.3 | convolution fusion | flops 836751360 | bytes 53576704 | tf_op jit(solution)/shard_map/ilhe,imhe->ihlm/dot_general | solution.py:214
  515.4 21.6 %multiply_convert_fusion.1 = bf16[2,12,512,512]{2,3,1,0:T(8,128)(2,1)} fusion(f32[2,12,512,512]{2,3,1,0:T(8,128)} %get-tuple-element.60, f32[2,12,512,512]{2,3,1,0:T(8,128)} %get-tuple-element.45, f32[2,12,512]{2,1,0:T(8,128)S(1)} %get-tuple-element.59, f32[2,12,512]{2,1,0:T(8,128)S(1)} %copy-done.48, pred[2,512]{1,0:T(4,128)(4,1)S(1)} %copy-done.56), kind=kLoop, calls=%fused_computation.2 | loop fusion | flops 37748736 | bytes 63013888 | tf_op jit(solution)/shard_map/convert_element_type | solution.py:221
  537.0 9.9 %fusion.71 = bf16[2,512,12,64]{1,3,2,0:T(8,128)(2,1)} fusion(bf16[2,12,512,512]{2,3,1,0:T(8,128)(2,1)} %multiply_convert_fusion.1, bf16[2,512,12,64]{1,0,3,2:T(2,128)(2,1)S(1)} %copy-done.10), kind=kOutput, calls=%fused_computation.157 | convolution fusion | flops 806879232 | bytes 15728640 | tf_op jit(solution)/shard_map/ihlm,ilhe->imhe/dot_general | solution.py:227
  553.6 22.5 %fusion.141 = (f32[1024]{0:T(1024)S(1)}, f32[1024]{0:T(1024)S(1)}, f32[1024,768]{1,0:T(8,128)}) fusion(f32[1024]{0:T(1024)S(1)} %copy-done.71, f32[1024,768]{1,0:T(8,128)} %copy-done.38, f32[1024]{0:T(1024)S(1)} %copy-done.65, f32[768]{0:T(1024)S(1)} %get-tuple-element.63, f32[1024,768]{1,0:T(8,128)} %get-tuple-element.28, ...), kind=kOutput, calls=%fused_computation.256 | convolution fusion | flops 9717151744 | bytes 44071936 | tf_op jit(solution)/shard_map/tf,df->td/dot_general | solution.py:203
  586.1 12.6 %fusion.69 = bf16[2,512,12,64]{1,3,2,0:T(8,128)(2,1)} fusion(bf16[2,512,12,64]{1,0,3,2:T(2,128)(2,1)} %reshape.256, f32[2,12,512,512]{2,3,1,0:T(8,128)} %get-tuple-element.43, f32[2,12,512]{2,1,0:T(8,128)S(1)} %copy-done.46, pred[2,512]{1,0:T(4,128)(4,1)S(1)} %copy-done.54), kind=kOutput, calls=%fused_computation.155 | convolution fusion | flops 831258624 | bytes 28361728 | tf_op jit(solution)/shard_map/ihlm,ilhe->imhe/dot_general | solution.py:217
  598.7 21.5 %multiply_reduce_fusion = (f32[2,12,512]{2,1,0:T(8,128)S(1)}, f32[2,12,512,512]{2,3,1,0:T(8,128)}) fusion(f32[2,12,512,512]{2,3,1,0:T(8,128)} %get-tuple-element.43, f32[2,12,512]{2,1,0:T(8,128)S(1)} %copy-done.46, pred[2,512]{1,0:T(4,128)(4,1)S(1)} %copy-done.54, bf16[2,512,12,64]{1,0,3,2:T(2,128)(2,1)S(1)} %copy-done.30, bf16[2,512,12,64]{1,0,3,2:T(2,128)(2,1)} %reshape.256), kind=kOutput, calls=%fused_computation.1 | convolution fusion | flops 836751360 | bytes 53576704 | tf_op jit(solution)/shard_map/ilhe,imhe->ihlm/dot_general | solution.py:214
  620.2 21.8 %multiply_convert_fusion = bf16[2,12,512,512]{2,3,1,0:T(8,128)(2,1)} fusion(f32[2,12,512,512]{2,3,1,0:T(8,128)} %get-tuple-element.57, f32[2,12,512,512]{2,3,1,0:T(8,128)} %get-tuple-element.43, f32[2,12,512]{2,1,0:T(8,128)S(1)} %get-tuple-element.56, f32[2,12,512]{2,1,0:T(8,128)S(1)} %copy-done.46, pred[2,512]{1,0:T(4,128)(4,1)S(1)} %copy-done.54), kind=kLoop, calls=%fused_computation | loop fusion | flops 37748736 | bytes 63013888 | tf_op jit(solution)/shard_map/convert_element_type | solution.py:221
  642.1 9.8 %fusion.73 = bf16[2,512,12,64]{1,3,2,0:T(8,128)(2,1)} fusion(bf16[2,12,512,512]{2,3,1,0:T(8,128)(2,1)} %multiply_convert_fusion, bf16[2,512,12,64]{1,0,3,2:T(2,128)(2,1)S(1)} %copy-done.8), kind=kOutput, calls=%fused_computation.159 | convolution fusion | flops 806879232 | bytes 15728640 | tf_op jit(solution)/shard_map/ihlm,ilhe->imhe/dot_general | solution.py:227
  712.4 38.5 %psum.7 = f32[2,8,768]{2,1,0:T(8,128)S(1)} all-reduce(f32[2,8,768]{2,1,0:T(8,128)S(1)} %fusion.101), channel_id=1, replica_groups=mesh['fsdp'=8,'rep'=4] {'fsdp','rep'}, use_global_device_ids=true, to_apply=%region_22.23 | all-reduce | flops 12288 | bytes 98304 | tf_op jit(solution)/shard_map/psum | solution.py:51
  755.5 8.4 %fusion.37 = bf16[1024,768]{1,0:T(8,128)(2,1)S(1)} fusion(f32[1024,768,1]{1,0,2:T(8,128)} %fusion.103, bf16[3,768,768]{2,1,0:T(8,128)(2,1)} %all-gather.9.cloned.1.call-done, bf16[1024,1,768]{2,0,1:T(8,128)(2,1)S(1)} %copy-done.27, bf16[1024,1,768]{2,0,1:T(8,128)(2,1)} %copy.272, bf16[1024,1,768]{2,0,1:T(8,128)(2,1)S(1)} %copy-done.28, ...), kind=kOutput, calls=%fused_computation.83 | convolution fusion | flops 3635675136 | bytes 19283968 | tf_op jit(solution)/shard_map/tke,kde->td/dot_general | solution.py:234
  (316 shorter events, 251.1 us)
Async XLA Ops:
  7.2 140.3 %copy-start = (bf16[2,8,768]{2,1,0:T(8,128)(2,1)S(1)}, bf16[2,8,768]{2,1,0:T(8,128)(2,1)}, u32[]{:S(2)}) copy-start(bf16[2,8,768]{2,1,0:T(8,128)(2,1)} %param.20) | copy-start | bytes 73732
  7.2 173.5 %all-gather.9.cloned.1.call-start = ((), (), s32[]{:S(2)}) async-start(), calls=%async_computation | async-start | bytes 3981312 | tf_op jit(solution)/shard_map/all_gather | solution.py:37
  8.3 73.5 %copy-start.67 = (s32[4,2]{0,1:T(2,128)S(1)}, s32[4,2]{0,1:T(2,128)}, u32[]{:S(2)}) copy-start(s32[4,2]{0,1:T(2,128)} %param.15) | copy-start | bytes 100
  8.3 73.6 %copy-start.78 = (bf16[384]{0:T(512)(128)(2,1)S(1)}, bf16[384]{0:T(512)(128)(2,1)}, u32[]{:S(2)}) copy-start(bf16[384]{0:T(512)(128)(2,1)} %param.24) | copy-start | bytes 2308
  8.3 73.6 %copy-start.87 = (u32[32]{0:T(128)S(1)}, u32[32]{0:T(128)}, u32[]{:S(2)}) copy-start(u32[32]{0:T(128)} %constant.101) | copy-start | bytes 388
  8.3 74.9 %copy-start.86 = (bf16[96]{0:T(256)(128)(2,1)S(1)}, bf16[96]{0:T(256)(128)(2,1)}, u32[]{:S(2)}) copy-start(bf16[96]{0:T(256)(128)(2,1)} %param.26) | copy-start | bytes 580
  8.4 87.8 %copy-start.79 = (bf16[2,96]{1,0:T(2,128)(2,1)S(1)}, bf16[2,96]{1,0:T(2,128)(2,1)}, u32[]{:S(2)}) copy-start(bf16[2,96]{1,0:T(2,128)(2,1)} %param.21) | copy-start | bytes 1156
  8.4 96.5 %copy-start.80 = (bf16[2,96]{1,0:T(2,128)(2,1)S(1)}, bf16[2,96]{1,0:T(2,128)(2,1)}, u32[]{:S(2)}) copy-start(bf16[2,96]{1,0:T(2,128)(2,1)} %param.22) | copy-start | bytes 1156
  8.4 104.6 %copy-start.77 = (bf16[3,96]{1,0:T(4,128)(2,1)S(1)}, bf16[3,96]{1,0:T(4,128)(2,1)}, u32[]{:S(2)}) copy-start(bf16[3,96]{1,0:T(4,128)(2,1)} %param.18) | copy-start | bytes 1732
  8.4 114.5 %copy-start.1 = (bf16[4,512,768]{2,1,0:T(8,128)(2,1)S(1)}, bf16[4,512,768]{2,1,0:T(8,128)(2,1)}, u32[]{:S(2)}) copy-start(bf16[4,512,768]{2,1,0:T(8,128)(2,1)} %param.27) | copy-start | bytes 9437188
  32.4 263.2 %all-gather.11.cloned.1.call-start = ((), (), s32[]{:S(2)}) async-start(), calls=%async_computation.1 | async-start | bytes 1327104 | tf_op jit(solution)/shard_map/all_gather | solution.py:38
  47.8 85.2 %copy-start.76 = (bf16[2,96,8]{1,2,0:T(8,128)(2,1)S(1)}, bf16[2,96,8]{1,2,0:T(8,128)(2,1)}, u32[]{:S(2)}) copy-start(bf16[2,96,8]{1,2,0:T(8,128)(2,1)} %param.19) | copy-start | bytes 9220
  47.8 293.8 %all-gather.13.cloned.1.call-start = ((), (), s32[]{:S(2)}) async-start(), calls=%async_computation.2 | async-start | bytes 5308416 | tf_op jit(solution)/shard_map/all_gather | solution.py:39
  65.3 348.4 %all-gather.15.cloned.1.call-start = ((), (), s32[]{:S(2)}) async-start(), calls=%async_computation.3 | async-start | bytes 5308416 | tf_op jit(solution)/shard_map/all_gather | solution.py:40
  145.7 18.3 %copy-start.51 = (bf16[1024,2,8]{0,2,1:T(8,128)(2,1)}, bf16[1024,2,8]{0,2,1:T(8,128)(2,1)S(1)}, u32[]{:S(2)}) copy-start(bf16[1024,2,8]{0,2,1:T(8,128)(2,1)S(1)} %fusion.99) | copy-start | bytes 98308
  180.7 99.8 %copy-start.55 = (pred[2,512]{1,0:T(4,128)(4,1)}, pred[2,512]{1,0:T(4,128)(4,1)S(1)}, u32[]{:S(2)}) copy-start(pred[2,512]{1,0:T(4,128)(4,1)S(1)} %get-tuple-element.62) | copy-start | bytes 3076
  180.7 143.3 %copy-start.53 = (pred[2,512]{1,0:T(4,128)(4,1)}, pred[2,512]{1,0:T(4,128)(4,1)S(1)}, u32[]{:S(2)}) copy-start(pred[2,512]{1,0:T(4,128)(4,1)S(1)} %get-tuple-element.61) | copy-start | bytes 3076
  210.4 89.1 %copy-start.3 = (bf16[2,512,12,64]{1,0,3,2:T(2,128)(2,1)}, bf16[2,512,12,64]{1,0,3,2:T(2,128)(2,1)S(1)}, u32[]{:S(2)}) copy-start(bf16[2,512,12,64]{1,0,3,2:T(2,128)(2,1)S(1)} %convert_element_type.220) | copy-start | bytes 4718596
  234.5 17.6 %copy-start.5 = (bf16[2,512,12,64]{1,0,3,2:T(2,128)(2,1)}, bf16[2,512,12,64]{1,0,3,2:T(2,128)(2,1)S(1)}, u32[]{:S(2)}) copy-start(bf16[2,512,12,64]{1,0,3,2:T(2,128)(2,1)S(1)} %convert_element_type.205) | copy-start | bytes 4718596
  299.0 175.0 %copy-start.60 = (f32[1024]{0:T(1024)}, f32[1024]{0:T(1024)S(1)}, u32[]{:S(2)}) copy-start(f32[1024]{0:T(1024)S(1)} %broadcast_multiply_fusion.10) | copy-start | bytes 12292
  299.6 174.5 %copy-start.68 = (f32[1024]{0:T(1024)}, f32[1024]{0:T(1024)S(1)}, u32[]{:S(2)}) copy-start(f32[1024]{0:T(1024)S(1)} %add_rsqrt_fusion.3) | copy-start | bytes 12292
  354.5 59.2 %copy-start.66 = (f32[768]{0:T(1024)S(1)}, f32[768]{0:T(1024)}, u32[]{:S(2)}) copy-start(f32[768]{0:T(1024)} %convert_element_type.214) | copy-start | bytes 9220
  451.9 22.8 %copy-start.36 = (f32[1024,768]{1,0:T(8,128)S(1)}, f32[1024,768]{1,0:T(8,128)}, u32[]{:S(2)}) copy-start(f32[1024,768]{1,0:T(8,128)} %copy-done.34) | copy-start | bytes 9437188
  515.4 21.6 %copy-start.10 = (bf16[2,512,12,64]{1,0,3,2:T(2,128)(2,1)S(1)}, bf16[2,512,12,64]{1,0,3,2:T(2,128)(2,1)}, u32[]{:S(2)}) copy-start(bf16[2,512,12,64]{1,0,3,2:T(2,128)(2,1)} %copy-done.9) | copy-start | bytes 4718596
  553.6 22.5 %copy-start.85 = (bf16[768,768]{1,0:T(8,128)(2,1)S(1)}, bf16[768,768]{1,0:T(8,128)(2,1)}, u32[]{:S(2)}) copy-start(bf16[768,768]{1,0:T(8,128)(2,1)} %all-gather.11.cloned.1.call-done) | copy-start | bytes 3538948
  620.2 21.8 %copy-start.8 = (bf16[2,512,12,64]{1,0,3,2:T(2,128)(2,1)S(1)}, bf16[2,512,12,64]{1,0,3,2:T(2,128)(2,1)}, u32[]{:S(2)}) copy-start(bf16[2,512,12,64]{1,0,3,2:T(2,128)(2,1)} %get-tuple-element.37) | copy-start | bytes 4718596
  705.1 48.4 %copy-start.61 = (f32[1024]{0:T(1024)S(1)}, f32[1024]{0:T(1024)}, u32[]{:S(2)}) copy-start(f32[1024]{0:T(1024)} %copy-done.60) | copy-start | bytes 12292
  705.1 48.3 %copy-start.69 = (f32[1024]{0:T(1024)S(1)}, f32[1024]{0:T(1024)}, u32[]{:S(2)}) copy-start(f32[1024]{0:T(1024)} %copy-done.68) | copy-start | bytes 12292
  705.2 48.3 %copy-start.73 = (f32[1024]{0:T(1024)S(1)}, f32[1024]{0:T(1024)}, u32[]{:S(2)}) copy-start(f32[1024]{0:T(1024)} %copy-done.72) | copy-start | bytes 12292
  705.2 48.3 %copy-start.75 = (f32[1024]{0:T(1024)S(1)}, f32[1024]{0:T(1024)}, u32[]{:S(2)}) copy-start(f32[1024]{0:T(1024)} %copy-done.74) | copy-start | bytes 12292
  709.9 41.7 %copy-start.15 = (bf16[1024,768]{1,0:T(8,128)(2,1)S(1)}, bf16[1024,768]{1,0:T(8,128)(2,1)}, u32[]{:S(2)}) copy-start(bf16[1024,768]{1,0:T(8,128)(2,1)} %get-tuple-element.29) | copy-start | bytes 4718596
  709.9 41.7 %copy-start.16 = (bf16[1024,768]{1,0:T(8,128)(2,1)S(1)}, bf16[1024,768]{1,0:T(8,128)(2,1)}, u32[]{:S(2)}) copy-start(bf16[1024,768]{1,0:T(8,128)(2,1)} %get-tuple-element.30) | copy-start | bytes 4718596
  (61 other events, 364.8 us)
Sparse Core Ops, SparseCore 0:
  32.5 33.4 all-gather.8
  67.9 24.0 all-gather.10
  93.9 38.7 all-gather.12
  134.4 39.6 all-gather.14
where the time goes:
time: 784 us; the launch traced here: 779 us
  matrix products  345 us (44%)
  blocking collectives  163 us (21%)
  local copies, waits for them, and re-layouts  154 us (20%)
  other arithmetic  101 us (13%)
  between operations  15.9 us (2%)
    dot_general x2, matrix products, forward_sweep(): jnp.dot(hidden_one.astype(jnp.bfloat16), in_full, preferred_element_type=...  67.6 us
    dot_general x2, matrix products, reverse_sweep(): jnp.einsum('tf,df->td', grad_inner, in_full, preferred_element_type=jnp.f...  44.6 us
    convert_element_type x2, other arithmetic, reverse_sweep(): grad_scores = (attn_weights * (grad_probs - row_inner)).astype(jnp.bfloat16)  43.4 us
    dot_general x2, matrix products, reverse_sweep(): jnp.einsum('ilhe,imhe->ihlm', grad_mixed, value_bf, preferred_element_typ...  41.2 us
    psum x1, blocking collectives, adapter_sum(): return lax.psum(adapter_grad_term, ('fsdp', 'rep'))  38.5 us
    dot_general x2, matrix products, forward_sweep(): jnp.dot(activation, back_full, preferred_element_type=jnp.float32)  28.6 us
    dot_general x2, matrix products, reverse_sweep(): jnp.einsum('ihlm,ilhe->imhe', probs_bf, grad_mixed, preferred_element_typ...  25.4 us
    another operation x12, local copies, waits for them, and re-layouts, reverse_sweep(): grad_proj = jnp.stack([query_gradient, grad_key, value_gradient], axis=1)  24.3 us
  transfers between devices with their start and end apart: 4, of which 0 were waited for; matrix products, arithmetic and copies ran while one was open for 34% of the time, Pallas kernels for 0%

commit v1 on v0

v1 whole, which is shorter than its diff:
```python
import math

import jax
import jax.numpy as jnp
from jax import lax
from jax.experimental import pallas as pl
from jax.experimental.pallas import tpu as pltpu
from jax.sharding import Mesh, PartitionSpec as P

D = 768
HD = 64
RANK = 8
L = 512
FF = 3072
F32 = jnp.float32
BF = jnp.bfloat16

NF = 8
NR = 4
FB = D // NF
RB = D // NR
GH = RB // HD
VMEM = 60 << 20

DOWN0 = 64
ATTN0 = 80
GAIN0 = 83
SHIFT0 = 85
INB0 = 87
BACKB0 = 91


def mm(a, b):
    return jnp.dot(a, b, preferred_element_type=F32)


def mm_nt(a, b):
    return lax.dot_general(a, b, (((1,), (1,)), ((), ())), preferred_element_type=F32)


def lanes(rows):
    return lax.broadcasted_iota(jnp.int32, (rows, 128), 1)


def params(n):
    return pltpu.CompilerParams(dimension_semantics=("arbitrary",) * n, vmem_limit_bytes=VMEM)


def whole_spec(*shape):
    return pl.BlockSpec(shape, lambda *_: (0,) * len(shape), pipeline_mode=pl.Buffered(1))


def pack_first(w, attn, down, gain, shift, in_bias, back_bias):
    small = jnp.concatenate(
        [down[0], down[1], attn.T, gain.T, shift.T, in_bias.reshape(FF // D, FB).T, back_bias[:, None]], axis=1
    )
    small = jnp.pad(small, ((0, 0), (0, 64 - small.shape[1])))
    return jnp.stack(
        [
            w[0, :, :128],
            w[1, :, :128],
            w[2, :, :128],
            jnp.concatenate([w[0, :, 128:], w[1, :, 128:]], axis=1),
            jnp.concatenate([w[2, :, 128:], small], axis=1),
        ]
    )


def pack_rest(wo, wi, wb):
    b = wb.reshape(4, FB, RB)
    tiles = [wi[:, 128 * j : 128 * j + 128] for j in range(6)]
    tiles += [wo[:, :128]] + [b[j, :, :128] for j in range(4)]
    halves = [wo[:, 128:]] + [b[j, :, 128:] for j in range(4)]
    halves.append(halves[-1])
    tiles += [jnp.concatenate(halves[2 * j : 2 * j + 2], axis=1) for j in range(3)]
    return jnp.stack(tiles)


def small_body(meta, a_ref, b_ref, up_ref, upb_ref, sm_ref, vec_ref, inb_ref, scr):
    for j in range(4):
        scr[pl.ds(pl.multiple_of(meta[j], 32), FB), :] = a_ref[j, 0]
        scr[pl.ds(pl.multiple_of(meta[4 + j], 32), FB), :] = b_ref[j, 0]
    sm = scr[...]
    lane = lanes(D)
    sm_ref[...] = jnp.where(jnp.logical_and(lane >= DOWN0, lane < DOWN0 + 2 * RANK), sm, jnp.zeros((), BF))
    t = sm.astype(F32).T
    row = lambda i: t[i : i + 1]
    zero = jnp.zeros((1, D), F32)
    vec_ref[...] = jnp.concatenate(
        [row(ATTN0 + 2), row(GAIN0), row(SHIFT0), row(BACKB0), row(GAIN0 + 1), row(SHIFT0 + 1), zero, zero], axis=0
    )
    inb_ref[...] = t[INB0 : INB0 + 4]
    z = meta[8]
    zb = jnp.zeros((RANK, D), F32)
    for k in range(2):
        b = up_ref[k].astype(F32) * 2.0
        body = [jnp.zeros((DOWN0, D), F32)] + ([b, zb] if k == 0 else [zb, b])
        bias = jnp.broadcast_to(row(ATTN0 + k), (RANK, D))
        keep = lax.broadcasted_iota(jnp.int32, (RANK, D), 0) == 0
        body.append(jnp.where(keep, bias, 0.0))
        body.append(jnp.zeros((128 - DOWN0 - 3 * RANK, D), F32))
        full = jnp.concatenate(body, axis=0).astype(BF)
        for r in range(NR):
            part = full[:, RB * r : RB * r + RB]
            upb_ref[r ^ z, k] = jnp.concatenate([part, jnp.zeros((128, 256 - RB), BF)], axis=1)


def small_params(meta, a, b, up):
    tile = pl.BlockSpec((4, 1, FB, 128), lambda i, *_: (0, 4, 0, 0))
    return pl.pallas_call(
        small_body,
        grid_spec=pltpu.PrefetchScalarGridSpec(
            num_scalar_prefetch=1,
            grid=(1,),
            in_specs=[tile, tile, whole_spec(2, RANK, D)],
            out_specs=[whole_spec(NR, 2, 128, 256), whole_spec(D, 128), whole_spec(8, D), whole_spec(4, D)],
            scratch_shapes=[pltpu.VMEM((D, 128), BF)],
        ),
        out_shape=[
            jax.ShapeDtypeStruct((NR, 2, 128, 256), BF),
            jax.ShapeDtypeStruct((D, 128), BF),
            jax.ShapeDtypeStruct((8, D), F32),
            jax.ShapeDtypeStruct((4, D), F32),
        ],
        compiler_params=params(1),
        name="small_params",
    )(meta, a, b, up)


def attn_fwd_body(meta, x_ref, a_ref, b_ref, upb_ref, *refs):
    w_ref, q_ref, k_ref, v_ref, p_ref, o_ref, li_ref, u_ref = refs[-8:]
    i = pl.program_id(0)

    @pl.when(i == 0)
    def _():
        left = lanes(FB) < 64
        for src, base in ((a_ref, 0), (b_ref, 4)):
            for j in range(4):
                rows = pl.ds(pl.multiple_of(meta[base + j], 32), FB)
                for k in range(3):
                    w_ref[0, k, rows, :128] = src[j, k]
                t3 = src[j, 3]
                t4 = src[j, 4]
                w_ref[0, 0, rows, 128:] = jnp.where(left, t3, t4)
                w_ref[0, 1, rows, 128:] = jnp.concatenate([t3[:, 64:], t3[:, :64]], axis=1)
                w_ref[0, 2, rows, 128:] = t4

    x = x_ref[0]
    lane = lanes(L)
    raw = mm(x, w_ref[0, 0])
    u = raw[:, 128:].astype(BF)
    u = jnp.where(jnp.logical_and(lane >= DOWN0, lane < DOWN0 + 2 * RANK), u, jnp.zeros((), BF))
    u_ref[0] = u
    ua = jnp.where(lane == ATTN0, jnp.ones((), BF), u)
    q = (raw + mm(ua, upb_ref[0, 0])).astype(BF) * jnp.asarray(0.125, BF)
    k = mm(x, w_ref[0, 1]).astype(BF)
    v = (mm(x, w_ref[0, 2]) + mm(ua, upb_ref[0, 1])).astype(BF)
    live = meta[16 + 2 * i] + meta[17 + 2 * i]
    mask = jnp.where(lax.broadcasted_iota(jnp.int32, (1, L), 1) < live, 0.0, -1e30)
    left = lane < HD
    zero = jnp.zeros((), BF)
    one = jnp.ones((), BF)
    for t in range(2):
        c = slice(128 * t, 128 * t + 128)
        qp, kp, vp = q[:, c], k[:, c], v[:, c]
        q_ref[0, 0, t] = qp
        k_ref[0, 0, t] = kp
        v_ref[0, 0, t] = vp
        acc = None
        for h in range(2 * t, min(2 * t + 2, GH)):
            own = left if h % 2 == 0 else jnp.logical_not(left)
            s = mm_nt(qp, jnp.where(own, kp, zero)) + mask
            m = jnp.max(s, axis=1, keepdims=True)
            pb = jnp.exp(s - m).astype(BF)
            p_ref[0, 0, h] = pb
            rhs = jnp.concatenate([jnp.where(own, vp, zero), jnp.where(own, one, zero)], axis=1)
            part = mm(pb, rhs)
            acc = part if acc is None else acc + part
        total = acc[:, 128:]
        if 2 * t + 1 >= GH:
            total = jnp.where(left, total, 1.0)
        li = 1.0 / total
        li_ref[0, 0, t] = li
        o_ref[0, 0, t] = (acc[:, :128] * li).astype(BF)


def attn_fwd(group, meta, x, a, b, upb, kept):
    n = x.shape[0]
    shapes = [
        ((NR, 3, D, 256), BF),
        ((NR, n, 2, L, 128), BF),
        ((NR, n, 2, L, 128), BF),
        ((NR, n, 2, L, 128), BF),
        ((NR, n, GH, L, L), BF),
        ((NR, n, 2, L, 128), BF),
        ((NR, n, 2, L, 128), F32),
    ]
    specs = [pl.BlockSpec((1, 3, D, 256), lambda i, *_: (group, 0, 0, 0), pipeline_mode=pl.Buffered(1))]
    specs += [pl.BlockSpec((1, 1) + s[2:], lambda i, *_: (group, i, 0, 0, 0)) for s, _ in shapes[1:]]
    specs.append(pl.BlockSpec((1, L, 128), lambda i, *_: (i, 0, 0)))
    out_shape = [jax.ShapeDtypeStruct(s, d) for s, d in shapes] + [jax.ShapeDtypeStruct((n, L, 128), BF)]
    return pl.pallas_call(
        attn_fwd_body,
        grid_spec=pltpu.PrefetchScalarGridSpec(
            num_scalar_prefetch=1,
            grid=(n,),
            in_specs=[
                pl.BlockSpec((1, L, D), lambda i, *_: (i, 0, 0)),
                whole_spec(4, 5, FB, 128),
                whole_spec(4, 5, FB, 128),
                pl.BlockSpec((1, 2, 128, 256), lambda i, *_: (group, 0, 0, 0), pipeline_mode=pl.Buffered(1)),
            ]
            + [pl.BlockSpec(memory_space=pl.ANY)] * len(kept),
            out_specs=specs,
        ),
        out_shape=out_shape,
        input_output_aliases={5 + j: j for j in range(len(kept))},
        compiler_params=params(1),
        name="attn_fwd",
    )(meta, x, a, b, upb, *kept)


GP = 0.3275911 * math.sqrt(0.5)
GA = [0.5 * c for c in (0.254829592, -0.284496736, 1.421413741, -1.453152027, 1.061405429)]
GC = 1.0 / math.sqrt(2.0 * math.pi)


def gelu_pair(z):
    t = 1.0 / (1.0 + GP * jnp.abs(z))
    e = jnp.exp(-0.5 * z * z)
    tail = t * (GA[0] + t * (GA[1] + t * (GA[2] + t * (GA[3] + t * GA[4])))) * e
    cdf = jnp.where(z > 0, 1.0 - tail, tail)
    return z * cdf, cdf + z * (GC * e)


def ln_stats(v):
    c = v - jnp.mean(v, axis=-1, keepdims=True)
    r = lax.rsqrt(jnp.mean(c * c, axis=-1, keepdims=True) + 1e-5)
    return c * r, r


def ln_back(g, n, r, w):
    c = g * w
    return r * (c - jnp.mean(c, axis=-1, keepdims=True) - n * jnp.mean(c * n, axis=-1, keepdims=True))


TT = 256
FC = 512


def ffn_body(meta, x_ref, g_ref, o_ref, li_ref, r_ref, vec_ref, bi_ref, ho_ref, gf_ref, dm_ref,
             wo_scr, wi_scr, wb_scr, act_scr, dact_scr, gi_scr):
    @pl.when(jnp.logical_and(pl.program_id(0) == 0, pl.program_id(1) == 0))
    def _():
        z = meta[8]

        def block(f, carry):
            rows = pl.ds(pl.multiple_of(f * FB, 32), FB)
            tile = lambda r, j: r_ref[NR * f + r, j]
            left = lambda r, j: r_ref[NR * f + r, j, :, :64]
            right = lambda r, j: r_ref[NR * f + r, j, :, 64:]
            for r in range(NR):
                for j in range(6):
                    wi_scr[rows, pl.ds(D * r + 128 * j, 128)] = tile(r, j)
            slot = ((f // 2) ^ z) * 2 + f % 2
            wo_scr[pl.ds(pl.multiple_of(slot * FB, 32), FB), :] = jnp.concatenate(
                sum([[tile(r, 6), left(r, 11)] for r in range(NR)], []), axis=1
            )
            for j in range(4):
                half = (right if j % 2 == 0 else left)
                wb_scr[pl.ds(pl.multiple_of(f * 4 * FB + j * FB, 32), FB), :] = jnp.concatenate(
                    sum([[tile(r, 7 + j), half(r, 11 + (j + 1) // 2)] for r in range(NR)], []), axis=1
                )
            return carry

        lax.fori_loop(0, NF, block, 0)

    x = x_ref[0].astype(F32)
    mixed = jnp.concatenate(sum([[o_ref[g, 0, 0], o_ref[g, 0, 1][:, :64]] for g in range(NR)], []), axis=1)
    n1, r1 = ln_stats(x + mm(mixed, wo_scr[...]) + vec_ref[0:1])
    h1 = n1 * vec_ref[1:2] + vec_ref[2:3]
    h1b = h1.astype(BF)
    for c in range(FF // FC):
        s = pl.ds(c * FC, FC)
        a, d = gelu_pair(mm(h1b, wi_scr[:, s]) + bi_ref[0:1, s])
        act_scr[:, s] = a.astype(BF)
        dact_scr[:, s] = d.astype(BF)
    n2, r2 = ln_stats(h1 + mm(act_scr[...], wb_scr[...]) + vec_ref[3:4])
    ho_ref[0] = (n2 * vec_ref[4:5] + vec_ref[5:6]).astype(BF)
    gs = ln_back(g_ref[0].astype(F32), n2, r2, vec_ref[4:5])
    gsb = gs.astype(BF)
    for c in range(FF // FC):
        s = pl.ds(c * FC, FC)
        ga = mm_nt(gsb, wb_scr[s, :])
        gi_scr[:, s] = (ga * dact_scr[:, s].astype(F32)).astype(BF)
    gh = gs + mm_nt(gi_scr[...], wi_scr[...])
    gf = ln_back(gh, n1, r1, vec_ref[1:2])
    gf_ref[0] = gf
    gm = mm_nt(gf.astype(BF), wo_scr[...])
    for g in range(NR):
        part = gm[:, RB * g : RB * g + RB]
        dm_ref[g, 0, 0] = (part[:, :128] * li_ref[g, 0, 0]).astype(BF)
        tail = part[:, 128:] * li_ref[g, 0, 1][:, :64]
        dm_ref[g, 0, 1] = jnp.concatenate([tail, jnp.zeros((TT, 64), F32)], axis=1).astype(BF)


def ffn(meta, x, g, o, li, rest, vec, bi):
    n = x.shape[0]
    row = pl.BlockSpec((1, TT, D), lambda i, t, *_: (i, t, 0))
    prow = pl.BlockSpec((NR, 1, 2, TT, 128), lambda i, t, *_: (0, i, 0, t, 0))
    return pl.pallas_call(
        ffn_body,
        grid_spec=pltpu.PrefetchScalarGridSpec(
            num_scalar_prefetch=1,
            grid=(n, L // TT),
            in_specs=[row, row, prow, prow, whole_spec(NF * NR, 14, FB, 128), whole_spec(8, D), whole_spec(1, FF)],
            out_specs=[row, row, prow],
            scratch_shapes=[pltpu.VMEM((D, D), BF), pltpu.VMEM((D, FF), BF), pltpu.VMEM((FF, D), BF)]
            + [pltpu.VMEM((TT, FF), BF)] * 3,
        ),
        out_shape=[
            jax.ShapeDtypeStruct((n, L, D), BF),
            jax.ShapeDtypeStruct((n, L, D), F32),
            jax.ShapeDtypeStruct((NR, n, 2, L, 128), BF),
        ],
        compiler_params=params(2),
        name="ffn",
    )(meta, x, g, o, li, rest, vec, bi)


def attn_bwd_body(meta, q_ref, k_ref, v_ref, p_ref, o_ref, dm_ref, gf_ref, u_ref, w_ref, sm_ref, upb_ref,
                  hg_ref, ag_ref, w_scr, up_scr, acc_scr, dq_scr, dkt_scr, dvt_scr):
    i = pl.program_id(0)
    cat = lambda parts: jnp.concatenate(parts, axis=1)

    @pl.when(i == 0)
    def _():
        for k in range(3):
            w_scr[k] = cat([w_ref[g, k][:, :RB] for g in range(NR)])
        for k in range(2):
            up_scr[k] = cat([upb_ref[g, k][:, :RB] for g in range(NR)])
        acc_scr[...] = jnp.zeros_like(acc_scr)

    def group(g, carry):
        left = lanes(L) < HD
        zero = jnp.zeros((), BF)
        neg = jnp.asarray(-1.0, BF)
        for t in range(2):
            qp, kp, vp = q_ref[g, 0, t], k_ref[g, 0, t], v_ref[g, 0, t]
            dm = dm_ref[g, 0, t]
            lhs = jnp.concatenate([dm, dm * o_ref[g, 0, t]], axis=1)
            qt = qp.T
            dmt = dm.T
            dq = None
            for h in range(2 * t, min(2 * t + 2, GH)):
                own = left if h % 2 == 0 else jnp.logical_not(left)
                rhs = jnp.concatenate([jnp.where(own, vp, zero), jnp.where(own, neg, zero)], axis=1)
                p = p_ref[g, 0, h]
                ds = (p.astype(F32) * mm_nt(lhs, rhs)).astype(BF)
                part = mm(ds, jnp.where(own, kp, zero))
                dq = part if dq is None else dq + part
                src = slice(HD * (h % 2), HD * (h % 2) + HD)
                dst = slice(HD * h, HD * h + HD)
                dkt_scr[g, dst, :] = mm(qt[src, :], ds).astype(BF)
                dvt_scr[g, dst, :] = mm(dmt[src, :], p).astype(BF)
            dq_scr[g, t] = (dq * 0.125).astype(BF)
        return carry

    lax.fori_loop(0, NR, group, 0)
    dq = cat(sum([[dq_scr[g, 0], dq_scr[g, 1][:, :64]] for g in range(NR)], []))
    dk = cat([dkt_scr[g].T for g in range(NR)])
    dv = cat([dvt_scr[g].T for g in range(NR)])
    gu = (mm_nt(dq, up_scr[0]) + mm_nt(dv, up_scr[1])).astype(BF)
    hg = gf_ref[0] + mm_nt(dq, w_scr[0]) + mm_nt(dk, w_scr[1]) + mm_nt(dv, w_scr[2]) + mm_nt(gu, sm_ref[...])
    hg_ref[0] = hg.astype(BF)
    ut = u_ref[0].T
    acc_scr[0] += mm(ut[DOWN0 : DOWN0 + RANK], dq)
    acc_scr[1] += mm(ut[DOWN0 + RANK : DOWN0 + 2 * RANK], dv)

    @pl.when(i == pl.num_programs(0) - 1)
    def _():
        for g in range(NR):
            ag_ref[g ^ meta[8]] = acc_scr[:, :, RB * g : RB * g + RB]


def attn_bwd(meta, q, k, v, p, o, dm, gf, u, w, sm, upb):
    n = gf.shape[0]
    tile = pl.BlockSpec((NR, 1, 2, L, 128), lambda i, *_: (0, i, 0, 0, 0))
    return pl.pallas_call(
        attn_bwd_body,
        grid_spec=pltpu.PrefetchScalarGridSpec(
            num_scalar_prefetch=1,
            grid=(n,),
            in_specs=[tile] * 3
            + [pl.BlockSpec((NR, 1, GH, L, L), lambda i, *_: (0, i, 0, 0, 0))]
            + [tile] * 2
            + [
                pl.BlockSpec((1, L, D), lambda i, *_: (i, 0, 0)),
                pl.BlockSpec((1, L, 128), lambda i, *_: (i, 0, 0)),
                whole_spec(NR, 3, D, 256),
                whole_spec(D, 128),
                whole_spec(NR, 2, 128, 256),
            ],
            out_specs=[pl.BlockSpec((1, L, D), lambda i, *_: (i, 0, 0)), whole_spec(NR, 2, RANK, RB)],
            scratch_shapes=[
                pltpu.VMEM((3, D, D), BF),
                pltpu.VMEM((2, 128, D), BF),
                pltpu.VMEM((2, RANK, D), F32),
                pltpu.VMEM((NR, 2, L, 128), BF),
                pltpu.VMEM((NR, RB, L), BF),
                pltpu.VMEM((NR, RB, L), BF),
            ],
        ),
        out_shape=[jax.ShapeDtypeStruct((n, L, D), BF), jax.ShapeDtypeStruct((NR, 2, RANK, RB), F32)],
        compiler_params=params(1),
        name="attn_bwd",
    )(meta, q, k, v, p, o, dm, gf, u, w, sm, upb)


def layer(meta, x, g, up, firsts, rest):
    upb, sm, vec, inb = small_params(meta, firsts[0][0], firsts[0][1], up)
    kept = ()
    for group in range(NR):
        a, b = firsts[group]
        out = attn_fwd(group, meta, x, a, b, upb, kept)
        kept, u = out[:-1], out[-1]
    w, q, k, v, p, o, li = kept
    bi = inb.reshape(4, NF, FB).transpose(1, 0, 2).reshape(1, FF)
    ho, gf, dm = ffn(meta, x, g, o, li, rest, vec, bi)
    hg, ag = attn_bwd(meta, q, k, v, p, o, dm, gf, u, w, sm, upb)
    return ho, hg, ag


def finish(ag, tokens):
    return ag.transpose(1, 2, 0, 3).reshape(2, RANK, D) * (2.0 / math.sqrt(tokens))


def meta_of(y, x, c, z, lens):
    rows = []
    for core in (c, 1 - c):
        for dy in range(2):
            for dx in range(2):
                rows.append((((y ^ dy) * 2 + (x ^ dx)) * 2 + core) * FB)
    head = jnp.stack([jnp.asarray(v, jnp.int32) for v in rows + [z] + [0] * 7])
    return jnp.concatenate([head, lens.reshape(-1)])


def block_blocks(qkv, wo, wi, wb, attn, down, gain, shift, inb, backb):
    def first(f, r):
        rows, cols = slice(FB * f, FB * f + FB), slice(RB * r, RB * r + RB)
        wide = slice(4 * FB * f, 4 * FB * f + 4 * FB)
        return pack_first(
            qkv[:, rows, cols], attn[:, rows], down[:, rows], gain[:, rows], shift[:, rows], inb[wide], backb[rows]
        )

    def other(f, r):
        rows, cols = slice(FB * f, FB * f + FB), slice(RB * r, RB * r + RB)
        return pack_rest(
            wo[rows, cols], wi[rows, D * r : D * r + D], wb[4 * FB * f : 4 * FB * f + 4 * FB, cols]
        )

    firsts = [
        tuple(jnp.stack([first(2 * j + core, r) for j in range(4)]) for core in range(2)) for r in range(NR)
    ]
    return firsts, jnp.stack([other(f, r) for f in range(NF) for r in range(NR)])


def device_plain(x, lens, qkv, wo, attn, down, up, gain, shift, wi, inb, wb, backb, g):
    tokens = x.shape[0] * L * lax.axis_size("fsdp") * lax.axis_size("rep")
    gather = lambda a, axis, dim: lax.all_gather(a, axis, axis=dim, tiled=True)
    both = lambda a, row, col: gather(gather(a, "rep", col), "fsdp", row)
    firsts, rest = block_blocks(
        both(qkv, 1, 2), both(wo, 0, 1), both(wi, 0, 1), both(wb, 0, 1),
        gather(attn, "fsdp", 1), gather(down, "fsdp", 1), gather(gain, "fsdp", 1), gather(shift, "fsdp", 1),
        gather(inb, "fsdp", 0), gather(backb, "fsdp", 0),
    )
    ho, hg, ag = layer(meta_of(0, 0, 0, 0, lens), x, g, up, firsts, rest)
    return ho, hg, finish(lax.psum(ag, ("fsdp", "rep")), tokens)


AXES = ("y", "x", "c", "z")


def flip(value, dy=0, dx=0, dc=0, dz=0):
    pairs = []
    for i in range(32):
        y, x, c, z = i >> 4, (i >> 3) & 1, (i >> 2) & 1, i & 3
        pairs.append((i, ((y ^ dy) << 4) | ((x ^ dx) << 3) | ((c ^ dc) << 2) | (z ^ dz)))
    return lax.ppermute(value, AXES, pairs)


def device_block(x, lens, qkv, wo, attn, down, up, gain, shift, wi, inb, wb, backb, g):
    tokens = x.shape[0] * L * 32
    own = pack_first(qkv, attn, down, gain, shift, inb, backb)
    near = jnp.stack([own, flip(own, dx=1), flip(own, dy=1), flip(own, dy=1, dx=1)])
    firsts = [(near, flip(near, dc=1))]
    for k in range(1, NR):
        far = flip(near, dz=k)
        firsts.append((far, flip(far, dc=1)))
    rest = lax.all_gather(pack_rest(wo, wi, wb), AXES, axis=0)
    meta = meta_of(lax.axis_index("y"), lax.axis_index("x"), lax.axis_index("c"), lax.axis_index("z"), lens)
    ho, hg, ag = layer(meta, x, g, up, firsts, rest)
    for step in (dict(dc=1), dict(dx=1), dict(dy=1), dict(dz=1), dict(dz=2)):
        ag = ag + flip(ag, **step)
    return ho, hg, finish(ag, tokens)


def solution(mesh):
    if mesh.shape["fsdp"] == NF and mesh.shape["rep"] == NR:
        mesh = Mesh(mesh.devices.reshape(2, 2, 2, 4), AXES)
        body, f, r = device_block, ("y", "x", "c"), ("z",)
    else:
        body, f, r = device_plain, ("fsdp",), ("rep",)
    items = P(f + r, None, None)
    in_specs = (
        items,
        P(f + r, None),
        P(None, f, r),
        P(f, r),
        P(None, f),
        P(None, f, None),
        P(),
        P(None, f),
        P(None, f),
        P(f, r),
        P(f),
        P(f, r),
        P(f),
        items,
    )

    def call(layer_input, lens, qkv, wo, attn, down, up, gain, shift, wi, inb, wb, backb, g):
        return jax.shard_map(
            body, mesh=mesh, in_specs=in_specs, out_specs=(items, items, P()), check_vma=False
        )(layer_input, lens, qkv, wo, attn, down, up, gain, shift, wi, inb, wb, backb, g)

    return call
```

time: 784 us -> 322 us (0.41)
  matrix products: 345 us -> 0 us
  Pallas kernels: 0 us -> 193 us
  blocking collectives: 163 us -> 0 us
  local copies, waits for them, and re-layouts: 154 us -> 18.6 us
  other arithmetic: 101 us -> 1.35 us
  waiting for transfers between devices: 0.11 us -> 63.7 us
  starting transfers between devices: 0.16 us -> 30.7 us
    dot_general x32 -> x0, matrix products: 344 us -> none  [the longest x2 67.6 us: forward_sweep(): jnp.dot(hidden_one.astype(jnp.bfloat16), in_full, preferred_element_type=...]
    pallas_call x0 -> x7, Pallas kernels: none -> 193 us  [the longest x1 82.6 us: ffn(): pl.pallas_call(ffn_body, grid_spec=pltpu.PrefetchScalarGridSpec(num_scala...]
    all_gather x9 -> x0, blocking collectives: 113 us -> none  [the longest x1 21.9 us: collect_frozen(): lax.all_gather(qkv_part, 'rep', axis=2, tiled=True)]
    ppermute x0 -> x15, waiting for transfers between devices: none -> 63.7 us  [flip(): return lax.ppermute(value, AXES, pairs)]
    convert_element_type x9 -> x0, other arithmetic: 56.3 us -> none  [the longest x2 43.4 us: reverse_sweep(): grad_scores = (attn_weights * (grad_probs - row_inner)).astype(jnp.bfloat16)]
    psum x1 -> x0, blocking collectives: 38.5 us -> none  [adapter_sum(): return lax.psum(adapter_grad_term, ('fsdp', 'rep'))]
    ppermute x0 -> x15, starting transfers between devices: none -> 30.6 us  [flip(): return lax.ppermute(value, AXES, pairs)]
    reduce_sum x8 -> x0, other arithmetic: 28.8 us -> none  [the longest x2 24.1 us: forward_sweep(): jnp.sum(jnp.exp(scores - row_max), axis=-1, keepdims=True)]
  transfers between devices with their start and end apart: 4 -> 16, of which waited for: 0 -> 9; matrix products, arithmetic and copies ran while one was open for 34% -> 2% of each run, Pallas kernels for 0% -> 19%
where the time goes in v1:
time: 322 us; the launch traced here: 321 us
  Pallas kernels  193 us (60%)
  waiting for transfers between devices  63.7 us (20%)
  starting transfers between devices  30.7 us (10%)
  local copies, waits for them, and re-layouts  18.6 us (6%)
  between operations  14.2 us (4%)
    pallas_call x1, Pallas kernels, ffn(): pl.pallas_call(ffn_body, grid_spec=pltpu.PrefetchScalarGridSpec(num_scala...  82.6 us
    ppermute x15, waiting for transfers between devices, flip(): return lax.ppermute(value, AXES, pairs)  63.7 us
    pallas_call x4, Pallas kernels, attn_fwd(): pl.pallas_call(attn_fwd_body, grid_spec=pltpu.PrefetchScalarGridSpec(num_...  57.4 us
    pallas_call x1, Pallas kernels, attn_bwd(): pl.pallas_call(attn_bwd_body, grid_spec=pltpu.PrefetchScalarGridSpec(num_...  50 us
    ppermute x15, starting transfers between devices, flip(): return lax.ppermute(value, AXES, pairs)  30.6 us
    unnamed x26, local copies, waits for them, and re-layouts  10.1 us
  transfers between devices with their start and end apart: 16, of which 9 were waited for; matrix products, arithmetic and copies ran while one was open for 2% of the time, Pallas kernels for 19%

profile of v1, /device:TPU:0, one launch (start us, length us, event | category | flops | bytes accessed | tf_op | source)
XLA Modules:
  0.0 321.2 jit_solution(6785022631883816370)
XLA Ops:
  7.2 1.0 copy.68
  16.8 1.5 concatenate.23
  18.4 0.9 slice.64
  19.3 0.8 slice_bitcast_fusion.6
  20.2 3.0 collective-permute-start
  23.2 1.5 collective-permute-start.1
  24.8 2.2 collective-permute-done
  26.9 5.0 %collective-permute-done.1 = bf16[5,96,128]{2,1,0:T(8,128)(2,1)S(1)} collective-permute-done((bf16[5,96,128]{2,1,0:T(8,128)(2,1)S(1)}, bf16[5,96,128]{2,1,0:T(8,128)(2,1)S(1)}, u32[]{:S(2)}, u32[]{:S(2)}) %collective-permute-start.1) | collective-permute-done | bytes 122912 | tf_op jit(solution)/shard_map/ppermute | solution.py:489
  32.0 1.6 collective-permute-start.8
  33.7 2.6 collective-permute-start.6
  36.5 20.6 %collective-permute-done.8.a_ref = bf16[4,5,96,128]{3,2,1,0:T(8,128)(2,1)S(1)} collective-permute-done((bf16[4,5,96,128]{3,2,1,0:T(8,128)(2,1)S(1)}, bf16[4,5,96,128]{3,2,1,0:T(8,128)(2,1)S(1)}, u32[]{:S(2)}, u32[]{:S(2)}) %collective-permute-start.8) | collective-permute-done | bytes 491552 | tf_op jit(solution)/shard_map/ppermute | solution.py:489
  57.1 23.0 %collective-permute-done.6.a_ref = bf16[4,5,96,128]{3,2,1,0:T(8,128)(2,1)S(1)} collective-permute-done((bf16[4,5,96,128]{3,2,1,0:T(8,128)(2,1)S(1)}, bf16[4,5,96,128]{3,2,1,0:T(8,128)(2,1)S(1)}, u32[]{:S(2)}, u32[]{:S(2)}) %collective-permute-start.6) | collective-permute-done | bytes 491552 | tf_op jit(solution)/shard_map/ppermute | solution.py:489
  82.0 0.8 copy-done.1
  82.8 2.6 small_params.1
  85.5 0.8 reshape.27
  87.0 14.4 %attn_fwd.4 = (bf16[4,3,768,256]{3,2,1,0:T(8,128)(2,1)}, bf16[4,4,2,512,128]{4,3,2,1,0:T(8,128)(2,1)}, bf16[4,4,2,512,128]{4,3,2,1,0:T(8,128)(2,1)}, bf16[4,4,2,...) custom-call(s32[24]{0:T(128)} %concatenate.21.meta, ...), custom_call_target="tpu_custom_call" | custom-call | tf_op jit(solution)/shard_map/attn_fwd/pallas_call | solution.py:202
  101.3 14.4 %attn_fwd.5 = (bf16[4,3,768,256]{3,2,1,0:T(8,128)(2,1)}, bf16[4,4,2,512,128]{4,3,2,1,0:T(8,128)(2,1)}, bf16[4,4,2,512,128]{4,3,2,1,0:T(8,128)(2,1)}, bf16[4,4,2,...) custom-call(s32[24]{0:T(128)} %concatenate.21.meta, ...), custom_call_target="tpu_custom_call", output_to_operand_aliasing={{0}: (5, {}), {1}: (6, {}), {2}: (7, {}), {3}: (8, {}), {4}... | custom-call | tf_op jit(solution)/shard_map/attn_fwd/pallas_call | solution.py:202
  115.8 0.8 copy-done.6
  116.5 14.4 %attn_fwd.6 = (bf16[4,3,768,256]{3,2,1,0:T(8,128)(2,1)}, bf16[4,4,2,512,128]{4,3,2,1,0:T(8,128)(2,1)}, bf16[4,4,2,512,128]{4,3,2,1,0:T(8,128)(2,1)}, bf16[4,4,2,...) custom-call(s32[24]{0:T(128)} %concatenate.21.meta, ...), custom_call_target="tpu_custom_call", output_to_operand_aliasing={{0}: (5, {}), {1}: (6, {}), {2}: (7, {}), {3}: (8, {}), {4}... | custom-call | tf_op jit(solution)/shard_map/attn_fwd/pallas_call | solution.py:202
  130.9 0.8 copy-done.4
  131.7 14.3 %attn_fwd.7 = (bf16[4,3,768,256]{3,2,1,0:T(8,128)(2,1)}, bf16[4,4,2,512,128]{4,3,2,1,0:T(8,128)(2,1)}, bf16[4,4,2,512,128]{4,3,2,1,0:T(8,128)(2,1)}, bf16[4,4,2,...) custom-call(s32[24]{0:T(128)} %concatenate.21.meta, ...), custom_call_target="tpu_custom_call", output_to_operand_aliasing={{0}: (5, {}), {1}: (6, {}), {2}: (7, {}), {3}: (8, {}), {4}... | custom-call | tf_op jit(solution)/shard_map/attn_fwd/pallas_call | solution.py:202
  146.0 82.6 %ffn.1 = (bf16[4,512,768]{2,1,0:T(8,128)(2,1)}, f32[4,512,768]{2,1,0:T(8,128)}, bf16[4,4,2,512,128]{4,3,2,1,0:T(8,128)(2,1)}) custom-call(s32[24]{0:T(128)} %concatenate.21.meta, bf16[4,512,768]{2,1,0:T(8,128)(2,1)} %x_ref.9, bf16[4,512,768]{2,1,0:T(8,128)(2,1)} %g_ref.1, bf16[4,4,2,512,128]{4,3,2,1,0:T(8,128)(2,1)} %get-tuple-element.63.o_ref, ...), custom_call_target="tpu_custom_call" | custom-call | tf_op jit(solution)/shard_map/ffn/pallas_call | solution.py:311
  228.6 50.0 %attn_bwd.1 = (bf16[4,512,768]{2,1,0:T(8,128)(2,1)}, f32[4,2,8,192]{3,2,1,0:T(8,128)}) custom-call(s32[24]{0:T(128)} %concatenate.21.meta, bf16[4,4,2,512,128]{4,3,2,1,0:T(8,128)(2,1)} %get-tuple-element.68.q_ref, bf16[4,4,2,512,128]{4,3,2,1,0:T(8,128)(2,1)} %get-tuple-element.69.k_ref, bf16[4,4,2,512,128]{4,3,2,1,0:T(8,128)(2,1)} %get-tuple-element.70.v_ref, ...), custom_call_target="tpu_custom_call" | custom-call | tf_op jit(solution)/shard_map/attn_bwd/pallas_call | solution.py:389
  278.8 1.4 collective-permute-done.10
  280.2 0.9 add.69
  281.1 4.3 %collective-permute-done.11 = f32[4,2,8,192]{3,2,1,0:T(8,128)S(1)} collective-permute-done((f32[4,2,8,192]{3,2,1,0:T(8,128)S(1)}, f32[4,2,8,192]{3,2,1,0:T(8,128)S(1)}, u32[]{:S(2)}, u32[]{:S(2)}) %collective-permute-start.11) | collective-permute-done | bytes 49184 | tf_op jit(solution)/shard_map/ppermute | solution.py:489
  285.4 1.6 collective-permute-start.12
  287.0 2.7 collective-permute-done.12
  289.7 16.4 %collective-permute-start.13 = (f32[4,2,8,192]{3,2,1,0:T(8,128)S(1)}, f32[4,2,8,192]{3,2,1,0:T(8,128)S(1)}, u32[]{:S(2)}, u32[]{:S(2)}) collective-permute-start(f32[4,2,8,192]{3,2,1,0:T(8,128)S(1)} %add.71), channel_id=1, source_target_pairs={{0,1},{1,0},{2,3},{3,2},{4,5},{5,4},{6,7},{7,6},{8,9},{9,8},{10,11... | collective-permute-start | bytes 147464 | tf_op jit(solution)/shard_map/ppermute | solution.py:489
  306.1 2.2 collective-permute-done.13
  308.4 2.9 collective-permute-start.14
  311.3 2.3 collective-permute-done.14
  (62 shorter events, 12.8 us)
Async XLA Ops:
  7.2 138.8 %all-gather.3.cloned.1.call-start = ((), (), s32[]{:S(2)}) async-start(), calls=%async_computation | async-start | bytes 11354112 | tf_op jit(solution)/shard_map/all_gather | solution.py:500
  14.5 0.7 copy-start.7
  20.2 6.7 %collective-permute-start = (bf16[5,96,128]{2,1,0:T(8,128)(2,1)S(1)}, bf16[5,96,128]{2,1,0:T(8,128)(2,1)S(1)}, u32[]{:S(2)}, u32[]{:S(2)}) collective-permute-start(bf16[5,96,128]{2,1,0:T(8,128)(2,1)S(1)} %get-tuple-element.87), channel_id=1, source_target_pairs={{0,8},{1,9},{2,10},{3,11},{4,12},{5,13},{6,14},{7,15},{8,0},{9,1},... | collective-permute-start | bytes 368648 | tf_op jit(solution)/shard_map/ppermute | solution.py:489
  23.2 8.7 %collective-permute-start.1 = (bf16[5,96,128]{2,1,0:T(8,128)(2,1)S(1)}, bf16[5,96,128]{2,1,0:T(8,128)(2,1)S(1)}, u32[]{:S(2)}, u32[]{:S(2)}) collective-permute-start(bf16[5,96,128]{2,1,0:T(8,128)(2,1)S(1)} %get-tuple-element.87), channel_id=1, source_target_pairs={{0,16},{1,17},{2,18},{3,19},{4,20},{5,21},{6,22},{7,23},{8,24},{9,... | collective-permute-start | bytes 368648 | tf_op jit(solution)/shard_map/ppermute | solution.py:489
  24.8 7.2 %collective-permute-start.2 = (bf16[5,96,128]{2,1,0:T(8,128)(2,1)S(1)}, bf16[5,96,128]{2,1,0:T(8,128)(2,1)S(1)}, u32[]{:S(2)}, u32[]{:S(2)}) collective-permute-start(bf16[5,96,128]{2,1,0:T(8,128)(2,1)S(1)} %get-tuple-element.87), channel_id=1, source_target_pairs={{0,24},{1,25},{2,26},{3,27},{4,28},{5,29},{6,30},{7,31},{8,16},{9,... | collective-permute-start | bytes 368648 | tf_op jit(solution)/shard_map/ppermute | solution.py:489
  32.0 50.0 %copy-start = (bf16[4,5,96,128]{3,2,1,0:T(8,128)(2,1)}, bf16[4,5,96,128]{3,2,1,0:T(8,128)(2,1)S(1)}, u32[]{:S(2)}) copy-start(bf16[4,5,96,128]{3,2,1,0:T(8,128)(2,1)S(1)} %pad_maximum_fusion.a_ref) | copy-start | bytes 1474564
  32.0 25.1 %collective-permute-start.8 = (bf16[4,5,96,128]{3,2,1,0:T(8,128)(2,1)S(1)}, bf16[4,5,96,128]{3,2,1,0:T(8,128)(2,1)S(1)}, u32[]{:S(2)}, u32[]{:S(2)}) collective-permute-start(bf16[4,5,96,128]{3,2,1,0:T(8,128)(2,1)S(1)} %pad_maximum_fusion.a_ref), channel_id=1, source_target_pairs={{0,1},{1,0},{2,3},{3,2},{4,5},{5,4},{6,7},{7,6},{8,9},{9,8},{10,11... | collective-permute-start | bytes 1474568 | tf_op jit(solution)/shard_map/ppermute | solution.py:489
  33.7 46.4 %collective-permute-start.6 = (bf16[4,5,96,128]{3,2,1,0:T(8,128)(2,1)S(1)}, bf16[4,5,96,128]{3,2,1,0:T(8,128)(2,1)S(1)}, u32[]{:S(2)}, u32[]{:S(2)}) collective-permute-start(bf16[4,5,96,128]{3,2,1,0:T(8,128)(2,1)S(1)} %pad_maximum_fusion.a_ref), channel_id=1, source_target_pairs={{0,2},{1,3},{2,0},{3,1},{4,6},{5,7},{6,4},{7,5},{8,10},{9,11},{10,... | collective-permute-start | bytes 1474568 | tf_op jit(solution)/shard_map/ppermute | solution.py:489
  36.2 43.8 %collective-permute-start.3 = (bf16[4,5,96,128]{3,2,1,0:T(8,128)(2,1)S(1)}, bf16[4,5,96,128]{3,2,1,0:T(8,128)(2,1)S(1)}, u32[]{:S(2)}, u32[]{:S(2)}) collective-permute-start(bf16[4,5,96,128]{3,2,1,0:T(8,128)(2,1)S(1)} %pad_maximum_fusion.a_ref), channel_id=1, source_target_pairs={{0,3},{1,2},{2,1},{3,0},{4,7},{5,6},{6,5},{7,4},{8,11},{9,10},{10,... | collective-permute-start | bytes 1474568 | tf_op jit(solution)/shard_map/ppermute | solution.py:489
  36.5 45.6 %collective-permute-start.5 = (bf16[4,5,96,128]{3,2,1,0:T(8,128)(2,1)S(1)}, bf16[4,5,96,128]{3,2,1,0:T(8,128)(2,1)S(1)}, u32[]{:S(2)}, u32[]{:S(2)}) collective-permute-start(bf16[4,5,96,128]{3,2,1,0:T(8,128)(2,1)S(1)} %pad_maximum_fusion.a_ref), channel_id=1, source_target_pairs={{0,4},{1,5},{2,6},{3,7},{4,0},{5,1},{6,2},{7,3},{8,12},{9,13},{10,... | collective-permute-start | bytes 1474568 | tf_op jit(solution)/shard_map/ppermute | solution.py:489
  57.1 44.3 %copy-start.5 = (bf16[4,5,96,128]{3,2,1,0:T(8,128)(2,1)}, bf16[4,5,96,128]{3,2,1,0:T(8,128)(2,1)S(1)}, u32[]{:S(2)}) copy-start(bf16[4,5,96,128]{3,2,1,0:T(8,128)(2,1)S(1)} %collective-permute-done.8.a_ref) | copy-start | bytes 1474564
  57.1 44.3 %collective-permute-start.9 = (bf16[4,5,96,128]{3,2,1,0:T(8,128)(2,1)S(1)}, bf16[4,5,96,128]{3,2,1,0:T(8,128)(2,1)}, u32[]{:S(2)}, u32[]{:S(2)}) collective-permute-start(bf16[4,5,96,128]{3,2,1,0:T(8,128)(2,1)S(1)} %collective-permute-done.8.a_ref), channel_id=1, source_target_pairs={{0,4},{1,5},{2,6},{3,7},{4,0},{5,1},{6,2},{7,3},{8,12},{9,13},{10,... | collective-permute-start | bytes 1474568 | tf_op jit(solution)/shard_map/ppermute | solution.py:489
  80.0 35.7 %copy-start.3 = (bf16[4,5,96,128]{3,2,1,0:T(8,128)(2,1)}, bf16[4,5,96,128]{3,2,1,0:T(8,128)(2,1)S(1)}, u32[]{:S(2)}) copy-start(bf16[4,5,96,128]{3,2,1,0:T(8,128)(2,1)S(1)} %collective-permute-done.6.a_ref) | copy-start | bytes 1474564
  80.0 35.7 %collective-permute-start.7 = (bf16[4,5,96,128]{3,2,1,0:T(8,128)(2,1)S(1)}, bf16[4,5,96,128]{3,2,1,0:T(8,128)(2,1)S(1)}, u32[]{:S(2)}, u32[]{:S(2)}) collective-permute-start(bf16[4,5,96,128]{3,2,1,0:T(8,128)(2,1)S(1)} %collective-permute-done.6.a_ref), channel_id=1, source_target_pairs={{0,4},{1,5},{2,6},{3,7},{4,0},{5,1},{6,2},{7,3},{8,12},{9,13},{10,... | collective-permute-start | bytes 1474568 | tf_op jit(solution)/shard_map/ppermute | solution.py:489
  80.0 35.7 %copy-start.2 = (bf16[4,5,96,128]{3,2,1,0:T(8,128)(2,1)}, bf16[4,5,96,128]{3,2,1,0:T(8,128)(2,1)S(1)}, u32[]{:S(2)}) copy-start(bf16[4,5,96,128]{3,2,1,0:T(8,128)(2,1)S(1)} %collective-permute-done.3.a_ref) | copy-start | bytes 1474564
  80.1 50.8 %collective-permute-start.4 = (bf16[4,5,96,128]{3,2,1,0:T(8,128)(2,1)S(1)}, bf16[4,5,96,128]{3,2,1,0:T(8,128)(2,1)S(1)}, u32[]{:S(2)}, u32[]{:S(2)}) collective-permute-start(bf16[4,5,96,128]{3,2,1,0:T(8,128)(2,1)S(1)} %collective-permute-done.3.a_ref), channel_id=1, source_target_pairs={{0,4},{1,5},{2,6},{3,7},{4,0},{5,1},{6,2},{7,3},{8,12},{9,13},{10,... | collective-permute-start | bytes 1474568 | tf_op jit(solution)/shard_map/ppermute | solution.py:489
  82.0 0.8 copy-start.1
  115.7 0.8 copy-start.6
  130.9 0.8 copy-start.4
  278.7 1.5 collective-permute-start.10
  281.0 4.3 %collective-permute-start.11 = (f32[4,2,8,192]{3,2,1,0:T(8,128)S(1)}, f32[4,2,8,192]{3,2,1,0:T(8,128)S(1)}, u32[]{:S(2)}, u32[]{:S(2)}) collective-permute-start(f32[4,2,8,192]{3,2,1,0:T(8,128)S(1)} %add.69), channel_id=1, source_target_pairs={{0,8},{1,9},{2,10},{3,11},{4,12},{5,13},{6,14},{7,15},{8,0},{9,1},... | collective-permute-start | bytes 147464 | tf_op jit(solution)/shard_map/ppermute | solution.py:489
  285.4 4.3 %collective-permute-start.12 = (f32[4,2,8,192]{3,2,1,0:T(8,128)S(1)}, f32[4,2,8,192]{3,2,1,0:T(8,128)S(1)}, u32[]{:S(2)}, u32[]{:S(2)}) collective-permute-start(f32[4,2,8,192]{3,2,1,0:T(8,128)S(1)} %add.70), channel_id=1, source_target_pairs={{0,16},{1,17},{2,18},{3,19},{4,20},{5,21},{6,22},{7,23},{8,24},{9,... | collective-permute-start | bytes 147464 | tf_op jit(solution)/shard_map/ppermute | solution.py:489
  289.7 18.6 %collective-permute-start.13 = (f32[4,2,8,192]{3,2,1,0:T(8,128)S(1)}, f32[4,2,8,192]{3,2,1,0:T(8,128)S(1)}, u32[]{:S(2)}, u32[]{:S(2)}) collective-permute-start(f32[4,2,8,192]{3,2,1,0:T(8,128)S(1)} %add.71), channel_id=1, source_target_pairs={{0,1},{1,0},{2,3},{3,2},{4,5},{5,4},{6,7},{7,6},{8,9},{9,8},{10,11... | collective-permute-start | bytes 147464 | tf_op jit(solution)/shard_map/ppermute | solution.py:489
  308.4 5.2 %collective-permute-start.14 = (f32[4,2,8,192]{3,2,1,0:T(8,128)S(1)}, f32[4,2,8,192]{3,2,1,0:T(8,128)S(1)}, u32[]{:S(2)}, u32[]{:S(2)}) collective-permute-start(f32[4,2,8,192]{3,2,1,0:T(8,128)S(1)} %add.72), channel_id=1, source_target_pairs={{0,2},{1,3},{2,0},{3,1},{4,6},{5,7},{6,4},{7,5},{8,10},{9,11},{10,... | collective-permute-start | bytes 147464 | tf_op jit(solution)/shard_map/ppermute | solution.py:489
Sparse Core Ops, SparseCore 0:
  15.4 117.9 all-gather.2

commit v2 on v1

--- a/solution.py
+++ b/solution.py
@@ -50,30 +50,41 @@
     return pl.BlockSpec(shape, lambda *_: (0,) * len(shape), pipeline_mode=pl.Buffered(1))
 
 
-def pack_first(w, attn, down, gain, shift, in_bias, back_bias):
-    small = jnp.concatenate(
-        [down[0], down[1], attn.T, gain.T, shift.T, in_bias.reshape(FF // D, FB).T, back_bias[:, None]], axis=1
-    )
-    small = jnp.pad(small, ((0, 0), (0, 64 - small.shape[1])))
-    return jnp.stack(
-        [
-            w[0, :, :128],
-            w[1, :, :128],
-            w[2, :, :128],
-            jnp.concatenate([w[0, :, 128:], w[1, :, 128:]], axis=1),
-            jnp.concatenate([w[2, :, 128:], small], axis=1),
-        ]
-    )
-
-
-def pack_rest(wo, wi, wb):
-    b = wb.reshape(4, FB, RB)
-    tiles = [wi[:, 128 * j : 128 * j + 128] for j in range(6)]
-    tiles += [wo[:, :128]] + [b[j, :, :128] for j in range(4)]
-    halves = [wo[:, 128:]] + [b[j, :, 128:] for j in range(4)]
-    halves.append(halves[-1])
-    tiles += [jnp.concatenate(halves[2 * j : 2 * j + 2], axis=1) for j in range(3)]
-    return jnp.stack(tiles)
+def pack_body(qkv_ref, attn_ref, down_ref, gain_ref, shift_ref, inb_ref, backb_ref, wo_ref, wi_ref, wb_ref,
+              first_ref, rest_ref, scr):
+    scr[...] = jnp.zeros_like(scr)
+    up = lambda v: v.astype(F32)
+    for k in range(2):
+        scr[pl.ds(DOWN0 + RANK * k, RANK), :FB] = up(down_ref[k])
+    inb = up(inb_ref[...])
+    rows = [up(attn_ref[...]), up(gain_ref[...]), up(shift_ref[...])]
+    rows += [inb[:, FB * j : FB * j + FB] for j in range(FF // D)] + [up(backb_ref[...])]
+    at = ATTN0
+    for v in rows:
+        scr[pl.ds(at, v.shape[0]), :FB] = v
+        at += v.shape[0]
+    small = scr[...].T[:FB, 64:].astype(BF)
+    for k in range(3):
+        first_ref[k] = qkv_ref[k, :, :128]
+    first_ref[3] = jnp.concatenate([qkv_ref[0, :, 128:], qkv_ref[1, :, 128:]], axis=1)
+    first_ref[4] = jnp.concatenate([qkv_ref[2, :, 128:], small], axis=1)
+    for j in range(6):
+        rest_ref[j] = wi_ref[:, 128 * j : 128 * j + 128]
+    rest_ref[6] = wo_ref[:, :128]
+    rest_ref[7] = jnp.concatenate([wo_ref[:, 128:], wo_ref[:, 128:]], axis=1)
+    for h in range(2):
+        for j in range(3):
+            rest_ref[8 + 3 * h + j] = wb_ref[FB * h : FB * h + FB, 128 * j : 128 * j + 128]
+
+
+def pack(qkv, attn, down, gain, shift, inb, backb, wo, wi, wb):
+    return pl.pallas_call(
+        pack_body,
+        out_shape=[jax.ShapeDtypeStruct((5, FB, 128), BF), jax.ShapeDtypeStruct((14, FB, 128), BF)],
+        scratch_shapes=[pltpu.VMEM((128, 128), F32)],
+        compiler_params=pltpu.CompilerParams(vmem_limit_bytes=VMEM),
+        name="pack",
+    )(qkv, attn, down.transpose(0, 2, 1), gain, shift, inb[None], backb[None], wo, wi, wb.T)
 
 
 def small_body(meta, a_ref, b_ref, up_ref, upb_ref, sm_ref, vec_ref, inb_ref, scr):
@@ -89,7 +100,9 @@
     vec_ref[...] = jnp.concatenate(
         [row(ATTN0 + 2), row(GAIN0), row(SHIFT0), row(BACKB0), row(GAIN0 + 1), row(SHIFT0 + 1), zero, zero], axis=0
     )
-    inb_ref[...] = t[INB0 : INB0 + 4]
+    inb_ref[...] = jnp.concatenate(
+        [t[INB0 + j : INB0 + j + 1, FB * f : FB * f + FB] for f in range(NF) for j in range(4)], axis=1
+    )
     z = meta[8]
     zb = jnp.zeros((RANK, D), F32)
     for k in range(2):
@@ -102,7 +115,7 @@
         full = jnp.concatenate(body, axis=0).astype(BF)
         for r in range(NR):
             part = full[:, RB * r : RB * r + RB]
-            upb_ref[r ^ z, k] = jnp.concatenate([part, jnp.zeros((128, 256 - RB), BF)], axis=1)
+            upb_ref[(z + NR - r) % NR, k] = jnp.concatenate([part, jnp.zeros((128, 256 - RB), BF)], axis=1)
 
 
 def small_params(meta, a, b, up):
@@ -113,14 +126,14 @@
             num_scalar_prefetch=1,
             grid=(1,),
             in_specs=[tile, tile, whole_spec(2, RANK, D)],
-            out_specs=[whole_spec(NR, 2, 128, 256), whole_spec(D, 128), whole_spec(8, D), whole_spec(4, D)],
+            out_specs=[whole_spec(NR, 2, 128, 256), whole_spec(D, 128), whole_spec(8, D), whole_spec(1, FF)],
             scratch_shapes=[pltpu.VMEM((D, 128), BF)],
         ),
         out_shape=[
             jax.ShapeDtypeStruct((NR, 2, 128, 256), BF),
             jax.ShapeDtypeStruct((D, 128), BF),
             jax.ShapeDtypeStruct((8, D), F32),
-            jax.ShapeDtypeStruct((4, D), F32),
+            jax.ShapeDtypeStruct((1, FF), F32),
         ],
         compiler_params=params(1),
         name="small_params",
@@ -258,19 +271,18 @@
             rows = pl.ds(pl.multiple_of(f * FB, 32), FB)
             tile = lambda r, j: r_ref[NR * f + r, j]
             left = lambda r, j: r_ref[NR * f + r, j, :, :64]
-            right = lambda r, j: r_ref[NR * f + r, j, :, 64:]
             for r in range(NR):
                 for j in range(6):
                     wi_scr[rows, pl.ds(D * r + 128 * j, 128)] = tile(r, j)
-            slot = ((f // 2) ^ z) * 2 + f % 2
+            slot = ((z + NR - f // 2) % NR) * 2 + f % 2
             wo_scr[pl.ds(pl.multiple_of(slot * FB, 32), FB), :] = jnp.concatenate(
-                sum([[tile(r, 6), left(r, 11)] for r in range(NR)], []), axis=1
+                sum([[tile(r, 6), left(r, 7)] for r in range(NR)], []), axis=1
             )
-            for j in range(4):
-                half = (right if j % 2 == 0 else left)
-                wb_scr[pl.ds(pl.multiple_of(f * 4 * FB + j * FB, 32), FB), :] = jnp.concatenate(
-                    sum([[tile(r, 7 + j), half(r, 11 + (j + 1) // 2)] for r in range(NR)], []), axis=1
-                )
+            for r in range(NR):
+                for h in range(2):
+                    for j in range(3):
+                        cols = pl.ds(pl.multiple_of(f * 4 * FB + 128 * j, 128), 128)
+                        wb_scr[RB * r + FB * h : RB * r + FB * h + FB, cols] = tile(r, 8 + 3 * h + j)
             return carry
 
         lax.fori_loop(0, NF, block, 0)
@@ -285,13 +297,13 @@
         a, d = gelu_pair(mm(h1b, wi_scr[:, s]) + bi_ref[0:1, s])
         act_scr[:, s] = a.astype(BF)
         dact_scr[:, s] = d.astype(BF)
-    n2, r2 = ln_stats(h1 + mm(act_scr[...], wb_scr[...]) + vec_ref[3:4])
+    n2, r2 = ln_stats(h1 + mm_nt(act_scr[...], wb_scr[...]) + vec_ref[3:4])
     ho_ref[0] = (n2 * vec_ref[4:5] + vec_ref[5:6]).astype(BF)
     gs = ln_back(g_ref[0].astype(F32), n2, r2, vec_ref[4:5])
     gsb = gs.astype(BF)
     for c in range(FF // FC):
         s = pl.ds(c * FC, FC)
-        ga = mm_nt(gsb, wb_scr[s, :])
+        ga = mm(gsb, wb_scr[:, s])
         gi_scr[:, s] = (ga * dact_scr[:, s].astype(F32)).astype(BF)
     gh = gs + mm_nt(gi_scr[...], wi_scr[...])
     gf = ln_back(gh, n1, r1, vec_ref[1:2])
@@ -315,7 +327,7 @@
             grid=(n, L // TT),
             in_specs=[row, row, prow, prow, whole_spec(NF * NR, 14, FB, 128), whole_spec(8, D), whole_spec(1, FF)],
             out_specs=[row, row, prow],
-            scratch_shapes=[pltpu.VMEM((D, D), BF), pltpu.VMEM((D, FF), BF), pltpu.VMEM((FF, D), BF)]
+            scratch_shapes=[pltpu.VMEM((D, D), BF), pltpu.VMEM((D, FF), BF), pltpu.VMEM((D, FF), BF)]
             + [pltpu.VMEM((TT, FF), BF)] * 3,
         ),
         out_shape=[
@@ -380,7 +392,7 @@
     @pl.when(i == pl.num_programs(0) - 1)
     def _():
         for g in range(NR):
-            ag_ref[g ^ meta[8]] = acc_scr[:, :, RB * g : RB * g + RB]
+            ag_ref[(meta[8] + NR - g) % NR] = acc_scr[:, :, RB * g : RB * g + RB]
 
 
 def attn_bwd(meta, q, k, v, p, o, dm, gf, u, w, sm, upb):
@@ -417,15 +429,30 @@
     )(meta, q, k, v, p, o, dm, gf, u, w, sm, upb)
 
 
-def layer(meta, x, g, up, firsts, rest):
-    upb, sm, vec, inb = small_params(meta, firsts[0][0], firsts[0][1], up)
+def after(value, other):
+    return pl.pallas_call(
+        lambda *refs: None,
+        in_specs=[pl.BlockSpec(memory_space=pl.ANY)] * 2,
+        out_specs=pl.BlockSpec(memory_space=pl.ANY),
+        out_shape=jax.ShapeDtypeStruct(value.shape, value.dtype),
+        input_output_aliases={0: 0},
+        name="after",
+    )(value, other)
+
+
+def layer(meta, x, g, up, near, onward, rest):
+    a, b = near
+    upb, sm, vec, bi = small_params(meta, a, b, up)
     kept = ()
     for group in range(NR):
-        a, b = firsts[group]
+        last = group == NR - 1
+        nxt = None if last else onward[0](a)
         out = attn_fwd(group, meta, x, a, b, upb, kept)
         kept, u = out[:-1], out[-1]
+        if not last:
+            a = after(nxt, u)
+            b = onward[1](a, group)
     w, q, k, v, p, o, li = kept
-    bi = inb.reshape(4, NF, FB).transpose(1, 0, 2).reshape(1, FF)
     ho, gf, dm = ffn(meta, x, g, o, li, rest, vec, bi)
     hg, ag = attn_bwd(meta, q, k, v, p, o, dm, gf, u, w, sm, upb)
     return ho, hg, ag
@@ -445,63 +472,57 @@
     return jnp.concatenate([head, lens.reshape(-1)])
 
 
-def block_blocks(qkv, wo, wi, wb, attn, down, gain, shift, inb, backb):
-    def first(f, r):
-        rows, cols = slice(FB * f, FB * f + FB), slice(RB * r, RB * r + RB)
-        wide = slice(4 * FB * f, 4 * FB * f + 4 * FB)
-        return pack_first(
-            qkv[:, rows, cols], attn[:, rows], down[:, rows], gain[:, rows], shift[:, rows], inb[wide], backb[rows]
-        )
-
-    def other(f, r):
-        rows, cols = slice(FB * f, FB * f + FB), slice(RB * r, RB * r + RB)
-        return pack_rest(
-            wo[rows, cols], wi[rows, D * r : D * r + D], wb[4 * FB * f : 4 * FB * f + 4 * FB, cols]
-        )
-
-    firsts = [
-        tuple(jnp.stack([first(2 * j + core, r) for j in range(4)]) for core in range(2)) for r in range(NR)
-    ]
-    return firsts, jnp.stack([other(f, r) for f in range(NF) for r in range(NR)])
-
-
 def device_plain(x, lens, qkv, wo, attn, down, up, gain, shift, wi, inb, wb, backb, g):
     tokens = x.shape[0] * L * lax.axis_size("fsdp") * lax.axis_size("rep")
     gather = lambda a, axis, dim: lax.all_gather(a, axis, axis=dim, tiled=True)
     both = lambda a, row, col: gather(gather(a, "rep", col), "fsdp", row)
-    firsts, rest = block_blocks(
-        both(qkv, 1, 2), both(wo, 0, 1), both(wi, 0, 1), both(wb, 0, 1),
-        gather(attn, "fsdp", 1), gather(down, "fsdp", 1), gather(gain, "fsdp", 1), gather(shift, "fsdp", 1),
-        gather(inb, "fsdp", 0), gather(backb, "fsdp", 0),
+    qkv, wo, wi, wb = both(qkv, 1, 2), both(wo, 0, 1), both(wi, 0, 1), both(wb, 0, 1)
+    attn, down, gain, shift = (gather(a, "fsdp", 1) for a in (attn, down, gain, shift))
+    inb, backb = gather(inb, "fsdp", 0), gather(backb, "fsdp", 0)
+
+    def block(f, r):
+        rows, cols = slice(FB * f, FB * f + FB), slice(RB * r, RB * r + RB)
+        wide = slice(4 * FB * f, 4 * FB * f + 4 * FB)
+        return pack(
+            qkv[:, rows, cols], attn[:, rows], down[:, rows], gain[:, rows], shift[:, rows], inb[wide], backb[rows],
+            wo[rows, cols], wi[rows, D * r : D * r + D], wb[wide, cols],
+        )
+
+    blocks = [[block(f, r) for r in range(NR)] for f in range(NF)]
+    rest = jnp.stack([blocks[f][r][1] for f in range(NF) for r in range(NR)])
+    firsts = [
+        tuple(jnp.stack([blocks[2 * j + core][r][0] for j in range(4)]) for core in range(2)) for r in (0, 3, 2, 1)
+    ]
+    turn = iter(firsts[1:])
+    ho, hg, ag = layer(
+        meta_of(0, 0, 0, 0, lens), x, g, up, firsts[0],
+        (lambda a: next(turn)[0], lambda a, group: firsts[group + 1][1]), rest,
     )
-    ho, hg, ag = layer(meta_of(0, 0, 0, 0, lens), x, g, up, firsts, rest)
     return ho, hg, finish(lax.psum(ag, ("fsdp", "rep")), tokens)
 
 
 AXES = ("y", "x", "c", "z")
 
 
-def flip(value, dy=0, dx=0, dc=0, dz=0):
+def flip(value, dy=0, dx=0, dc=0, dz=0, shift=0):
     pairs = []
     for i in range(32):
         y, x, c, z = i >> 4, (i >> 3) & 1, (i >> 2) & 1, i & 3
-        pairs.append((i, ((y ^ dy) << 4) | ((x ^ dx) << 3) | ((c ^ dc) << 2) | (z ^ dz)))
+        pairs.append((i, ((y ^ dy) << 4) | ((x ^ dx) << 3) | ((c ^ dc) << 2) | (((z ^ dz) + shift) & 3)))
     return lax.ppermute(value, AXES, pairs)
 
 
 def device_block(x, lens, qkv, wo, attn, down, up, gain, shift, wi, inb, wb, backb, g):
     tokens = x.shape[0] * L * 32
-    own = pack_first(qkv, attn, down, gain, shift, inb, backb)
+    own, rest = pack(qkv, attn, down, gain, shift, inb, backb, wo, wi, wb)
+    rest = lax.all_gather(rest, AXES, axis=0)
+    meta = meta_of(lax.axis_index("y"), lax.axis_index("x"), lax.axis_index("c"), lax.axis_index("z"), lens)
     near = jnp.stack([own, flip(own, dx=1), flip(own, dy=1), flip(own, dy=1, dx=1)])
-    firsts = [(near, flip(near, dc=1))]
-    for k in range(1, NR):
-        far = flip(near, dz=k)
-        firsts.append((far, flip(far, dc=1)))
-    rest = lax.all_gather(pack_rest(wo, wi, wb), AXES, axis=0)
-    meta = meta_of(lax.axis_index("y"), lax.axis_index("x"), lax.axis_index("c"), lax.axis_index("z"), lens)
-    ho, hg, ag = layer(meta, x, g, up, firsts, rest)
-    for step in (dict(dc=1), dict(dx=1), dict(dy=1), dict(dz=1), dict(dz=2)):
-        ag = ag + flip(ag, **step)
+    onward = (lambda a: flip(a, shift=1), lambda a, group: flip(a, dc=1))
+    ho, hg, ag = layer(meta, x, g, up, (near, flip(near, dc=1)), onward, rest)
+    ag = ag + flip(ag, dc=1)
+    ag = (ag + flip(ag, dx=1)) + (flip(ag, dy=1) + flip(ag, dy=1, dx=1))
+    ag = (ag + flip(ag, dz=1)) + (flip(ag, dz=2) + flip(ag, dz=3))
     return ho, hg, finish(ag, tokens)
 
 

time: 322 us -> 282 us (0.88)
  waiting for transfers between devices: 63.7 us -> 44.6 us
  starting transfers between devices: 30.7 us -> 15.5 us
  local copies, waits for them, and re-layouts: 18.6 us -> 9 us
    ppermute x15 -> x17, waiting for transfers between devices: 63.7 us -> 36.7 us  [flip(): return lax.ppermute(value, AXES, pairs)]
    ppermute x15 -> x17, starting transfers between devices: 30.6 us -> 15.4 us  [flip(): return lax.ppermute(value, AXES, pairs)]
    all_gather x1, waiting for transfers between devices: 0.02 us -> 7.88 us  [device_block(): rest = lax.all_gather(rest, AXES, axis=0)]
    unnamed x26 -> x17, local copies, waits for them, and re-layouts: 10.1 us -> 6.24 us
  transfers between devices with their start and end apart: 16 -> 18, of which waited for: 9 -> 15; matrix products, arithmetic and copies ran while one was open for 2% -> 1% of each run, Pallas kernels for 19% -> 21%
where the time goes in v2:
time: 282 us; the launch traced here: 281 us
  Pallas kernels  196 us (70%)
  waiting for transfers between devices  44.6 us (16%)
  starting transfers between devices  15.5 us (5%)
  between operations  14.1 us (5%)
  local copies, waits for them, and re-layouts  9 us (3%)
    pallas_call x1, Pallas kernels, ffn(): pl.pallas_call(ffn_body, grid_spec=pltpu.PrefetchScalarGridSpec(num_scala...  84.1 us
    pallas_call x4, Pallas kernels, attn_fwd(): pl.pallas_call(attn_fwd_body, grid_spec=pltpu.PrefetchScalarGridSpec(num_...  57.4 us
    pallas_call x1, Pallas kernels, attn_bwd(): pl.pallas_call(attn_bwd_body, grid_spec=pltpu.PrefetchScalarGridSpec(num_...  50 us
    ppermute x17, waiting for transfers between devices, flip(): return lax.ppermute(value, AXES, pairs)  36.7 us
    ppermute x17, starting transfers between devices, flip(): return lax.ppermute(value, AXES, pairs)  15.4 us
    all_gather x1, waiting for transfers between devices, device_block(): rest = lax.all_gather(rest, AXES, axis=0)  7.88 us
    unnamed x17, local copies, waits for them, and re-layouts  6.24 us
  transfers between devices with their start and end apart: 18, of which 15 were waited for; matrix products, arithmetic and copies ran while one was open for 1% of the time, Pallas kernels for 21%

profile of v2, /device:TPU:0, one launch (start us, length us, event | category | flops | bytes accessed | tf_op | source)
XLA Modules:
  0.0 281.4 jit_solution(8725719936072701553)
XLA Ops:
  7.2 1.2 broadcast_in_dim.6.inb_ref
  8.5 2.1 pack.1
  10.5 3.0 %collective-permute-start = (bf16[5,96,128]{2,1,0:T(8,128)(2,1)}, bf16[5,96,128]{2,1,0:T(8,128)(2,1)S(1)}, u32[]{:S(2)}, u32[]{:S(2)}) collective-permute-start(bf16[5,96,128]{2,1,0:T(8,128)(2,1)} %get-tuple-element.46), channel_id=1, source_target_pairs={{0,8},{1,9},{2,10},{3,11},{4,12},{5,13},{6,14},{7,15},{8,0},{9,1},... | collective-permute-start | bytes 368648 | tf_op jit(solution)/shard_map/ppermute | solution.py:512
  13.6 1.5 collective-permute-start.1
  15.1 2.5 collective-permute-done
  17.6 3.7 %collective-permute-done.1 = bf16[5,96,128]{2,1,0:T(8,128)(2,1)S(1)} collective-permute-done((bf16[5,96,128]{2,1,0:T(8,128)(2,1)}, bf16[5,96,128]{2,1,0:T(8,128)(2,1)S(1)}, u32[]{:S(2)}, u32[]{:S(2)}) %collective-permute-start.1) | collective-permute-done | bytes 122912 | tf_op jit(solution)/shard_map/ppermute | solution.py:512
  21.3 1.0 pad_maximum_fusion.a_ref
  22.4 1.6 collective-permute-start.3
  26.3 2.7 small_params.1
  29.0 14.4 %attn_fwd.4 = (bf16[4,3,768,256]{3,2,1,0:T(8,128)(2,1)}, bf16[4,4,2,512,128]{4,3,2,1,0:T(8,128)(2,1)}, bf16[4,4,2,512,128]{4,3,2,1,0:T(8,128)(2,1)}, bf16[4,4,2,...) custom-call(s32[24]{0:T(128)} %concatenate.3.meta, ...), custom_call_target="tpu_custom_call" | custom-call | tf_op jit(solution)/shard_map/attn_fwd/pallas_call | solution.py:215
  43.3 1.4 collective-permute-done.3.refs_0_
  45.9 1.7 collective-permute-done.6.b_ref
  48.4 14.4 %attn_fwd.5 = (bf16[4,3,768,256]{3,2,1,0:T(8,128)(2,1)}, bf16[4,4,2,512,128]{4,3,2,1,0:T(8,128)(2,1)}, bf16[4,4,2,512,128]{4,3,2,1,0:T(8,128)(2,1)}, bf16[4,4,2,...) custom-call(s32[24]{0:T(128)} %concatenate.3.meta, ...), custom_call_target="tpu_custom_call", output_to_operand_aliasing={{0}: (5, {}), {1}: (6, {}), {2}: (7, {}), {3}: (8, {}), {4}... | custom-call | tf_op jit(solution)/shard_map/attn_fwd/pallas_call | solution.py:215
  62.8 9.2 %collective-permute-done.5.refs_0_ = bf16[4,5,96,128]{3,2,1,0:T(8,128)(2,1)S(1)} collective-permute-done((bf16[4,5,96,128]{3,2,1,0:T(8,128)(2,1)}, bf16[4,5,96,128]{3,2,1,0:T(8,128)(2,1)S(1)}, u32[]{:S(2)}, u32[]{:S(2)}) %collective-permute-start.5) | collective-permute-done | bytes 491552 | tf_op jit(solution)/shard_map/ppermute | solution.py:512
  73.3 1.6 collective-permute-done.8.b_ref
  75.6 14.3 %attn_fwd.6 = (bf16[4,3,768,256]{3,2,1,0:T(8,128)(2,1)}, bf16[4,4,2,512,128]{4,3,2,1,0:T(8,128)(2,1)}, bf16[4,4,2,512,128]{4,3,2,1,0:T(8,128)(2,1)}, bf16[4,4,2,...) custom-call(s32[24]{0:T(128)} %concatenate.3.meta, ...), custom_call_target="tpu_custom_call", output_to_operand_aliasing={{0}: (5, {}), {1}: (6, {}), {2}: (7, {}), {3}: (8, {}), {4}... | custom-call | tf_op jit(solution)/shard_map/attn_fwd/pallas_call | solution.py:215
  90.0 4.6 %collective-permute-done.7.refs_0_ = bf16[4,5,96,128]{3,2,1,0:T(8,128)(2,1)S(1)} collective-permute-done((bf16[4,5,96,128]{3,2,1,0:T(8,128)(2,1)}, bf16[4,5,96,128]{3,2,1,0:T(8,128)(2,1)S(1)}, u32[]{:S(2)}, u32[]{:S(2)}) %collective-permute-start.7) | collective-permute-done | bytes 491552 | tf_op jit(solution)/shard_map/ppermute | solution.py:512
  95.3 2.2 collective-permute-done.9.b_ref
  98.3 14.4 %attn_fwd.7 = (bf16[4,3,768,256]{3,2,1,0:T(8,128)(2,1)}, bf16[4,4,2,512,128]{4,3,2,1,0:T(8,128)(2,1)}, bf16[4,4,2,512,128]{4,3,2,1,0:T(8,128)(2,1)}, bf16[4,4,2,...) custom-call(s32[24]{0:T(128)} %concatenate.3.meta, ...), custom_call_target="tpu_custom_call", output_to_operand_aliasing={{0}: (5, {}), {1}: (6, {}), {2}: (7, {}), {3}: (8, {}), {4}... | custom-call | tf_op jit(solution)/shard_map/attn_fwd/pallas_call | solution.py:215
  112.7 7.9 %all-gather.3.cloned.1.call-done = bf16[448,96,128]{2,1,0:T(8,128)(2,1)} async-done(((bf16[14,96,128]{2,1,0:T(8,128)(2,1)}), bf16[448,96,128]{2,1,0:T(8,128)(2,1)}) %all-gather.3.cloned.1.call-update) | async-done | bytes 11010064 | tf_op jit(solution)/shard_map/all_gather | solution.py:518
  120.5 84.1 %ffn.1 = (bf16[4,512,768]{2,1,0:T(8,128)(2,1)}, f32[4,512,768]{2,1,0:T(8,128)}, bf16[4,4,2,512,128]{4,3,2,1,0:T(8,128)(2,1)}) custom-call(s32[24]{0:T(128)} %concatenate.3.meta, bf16[4,512,768]{2,1,0:T(8,128)(2,1)} %x_ref.9, bf16[4,512,768]{2,1,0:T(8,128)(2,1)} %g_ref.1, bf16[4,4,2,512,128]{4,3,2,1,0:T(8,128)(2,1)} %get-tuple-element.72.o_ref, ...), custom_call_target="tpu_custom_call" | custom-call | tf_op jit(solution)/shard_map/ffn/pallas_call | solution.py:323
  204.6 50.0 %attn_bwd.1 = (bf16[4,512,768]{2,1,0:T(8,128)(2,1)}, f32[4,2,8,192]{3,2,1,0:T(8,128)}) custom-call(s32[24]{0:T(128)} %concatenate.3.meta, bf16[4,4,2,512,128]{4,3,2,1,0:T(8,128)(2,1)} %get-tuple-element.78.q_ref, bf16[4,4,2,512,128]{4,3,2,1,0:T(8,128)(2,1)} %get-tuple-element.79.k_ref, bf16[4,4,2,512,128]{4,3,2,1,0:T(8,128)(2,1)} %get-tuple-element.80.v_ref, ...), custom_call_target="tpu_custom_call" | custom-call | tf_op jit(solution)/shard_map/attn_bwd/pallas_call | solution.py:401
  254.9 1.2 collective-permute-done.10
  257.0 1.5 collective-permute-start.11
  258.5 0.9 collective-permute-start.12
  259.4 1.2 collective-permute-start.13
  261.3 2.2 collective-permute-done.12
  263.5 1.1 collective-permute-done.13
  264.7 2.9 %collective-permute-start.15 = (f32[4,2,8,192]{3,2,1,0:T(8,128)S(1)}, f32[4,2,8,192]{3,2,1,0:T(8,128)S(1)}, u32[]{:S(2)}, u32[]{:S(2)}) collective-permute-start(f32[4,2,8,192]{3,2,1,0:T(8,128)S(1)} %add_add_fusion), channel_id=1, source_target_pairs={{0,2},{1,3},{2,0},{3,1},{4,6},{5,7},{6,4},{7,5},{8,10},{9,11},{10,... | collective-permute-start | bytes 147464 | tf_op jit(solution)/shard_map/ppermute | solution.py:512
  267.5 1.5 collective-permute-start.16
  269.0 2.4 collective-permute-done.15
  271.5 2.2 collective-permute-done.16
  (44 shorter events, 10.8 us)
Async XLA Ops:
  7.2 113.4 %all-gather.3.cloned.1.call-start = ((), (), s32[]{:S(2)}) async-start(), calls=%async_computation | async-start | bytes 11354112 | tf_op jit(solution)/shard_map/all_gather | solution.py:518
  10.5 7.1 %collective-permute-start = (bf16[5,96,128]{2,1,0:T(8,128)(2,1)}, bf16[5,96,128]{2,1,0:T(8,128)(2,1)S(1)}, u32[]{:S(2)}, u32[]{:S(2)}) collective-permute-start(bf16[5,96,128]{2,1,0:T(8,128)(2,1)} %get-tuple-element.46), channel_id=1, source_target_pairs={{0,8},{1,9},{2,10},{3,11},{4,12},{5,13},{6,14},{7,15},{8,0},{9,1},... | collective-permute-start | bytes 368648 | tf_op jit(solution)/shard_map/ppermute | solution.py:512
  13.6 7.7 %collective-permute-start.1 = (bf16[5,96,128]{2,1,0:T(8,128)(2,1)}, bf16[5,96,128]{2,1,0:T(8,128)(2,1)S(1)}, u32[]{:S(2)}, u32[]{:S(2)}) collective-permute-start(bf16[5,96,128]{2,1,0:T(8,128)(2,1)} %get-tuple-element.46), channel_id=1, source_target_pairs={{0,16},{1,17},{2,18},{3,19},{4,20},{5,21},{6,22},{7,23},{8,24},{9,... | collective-permute-start | bytes 368648 | tf_op jit(solution)/shard_map/ppermute | solution.py:512
  15.1 6.2 %collective-permute-start.2 = (bf16[5,96,128]{2,1,0:T(8,128)(2,1)}, bf16[5,96,128]{2,1,0:T(8,128)(2,1)S(1)}, u32[]{:S(2)}, u32[]{:S(2)}) collective-permute-start(bf16[5,96,128]{2,1,0:T(8,128)(2,1)} %get-tuple-element.46), channel_id=1, source_target_pairs={{0,24},{1,25},{2,26},{3,27},{4,28},{5,29},{6,30},{7,31},{8,16},{9,... | collective-permute-start | bytes 368648 | tf_op jit(solution)/shard_map/ppermute | solution.py:512
  22.3 3.3 %copy-start = (bf16[4,5,96,128]{3,2,1,0:T(8,128)(2,1)}, bf16[4,5,96,128]{3,2,1,0:T(8,128)(2,1)S(1)}, u32[]{:S(2)}) copy-start(bf16[4,5,96,128]{3,2,1,0:T(8,128)(2,1)S(1)} %pad_maximum_fusion.a_ref) | copy-start | bytes 1474564
  22.3 3.2 %collective-permute-start.4 = (bf16[4,5,96,128]{3,2,1,0:T(8,128)(2,1)S(1)}, bf16[4,5,96,128]{3,2,1,0:T(8,128)(2,1)S(1)}, u32[]{:S(2)}, u32[]{:S(2)}) collective-permute-start(bf16[4,5,96,128]{3,2,1,0:T(8,128)(2,1)S(1)} %pad_maximum_fusion.a_ref), channel_id=1, source_target_pairs={{0,4},{1,5},{2,6},{3,7},{4,0},{5,1},{6,2},{7,3},{8,12},{9,13},{10,... | collective-permute-start | bytes 1474568 | tf_op jit(solution)/shard_map/ppermute | solution.py:512
  22.4 22.4 %collective-permute-start.3 = (bf16[4,5,96,128]{3,2,1,0:T(8,128)(2,1)S(1)}, bf16[4,5,96,128]{3,2,1,0:T(8,128)(2,1)S(1)}, u32[]{:S(2)}, u32[]{:S(2)}) collective-permute-start(bf16[4,5,96,128]{3,2,1,0:T(8,128)(2,1)S(1)} %pad_maximum_fusion.a_ref), channel_id=1, source_target_pairs={{0,1},{1,2},{2,3},{3,0},{4,5},{5,6},{6,7},{7,4},{8,9},{9,10},{10,1... | collective-permute-start | bytes 1474568 | tf_op jit(solution)/shard_map/ppermute | solution.py:512
  25.5 0.8 copy-start.1
  44.8 0.8 copy-start.2
  45.5 2.1 collective-permute-start.6
  45.5 26.4 %collective-permute-start.5 = (bf16[4,5,96,128]{3,2,1,0:T(8,128)(2,1)}, bf16[4,5,96,128]{3,2,1,0:T(8,128)(2,1)S(1)}, u32[]{:S(2)}, u32[]{:S(2)}) collective-permute-start(bf16[4,5,96,128]{3,2,1,0:T(8,128)(2,1)} %after.3.a_ref), channel_id=1, source_target_pairs={{0,1},{1,2},{2,3},{3,0},{4,5},{5,6},{6,7},{7,4},{8,9},{9,10},{10,1... | collective-permute-start | bytes 1474568 | tf_op jit(solution)/shard_map/ppermute | solution.py:512
  47.6 0.8 copy-start.5
  72.0 0.8 copy-start.3
  72.8 2.1 collective-permute-start.8
  72.8 21.8 %collective-permute-start.7 = (bf16[4,5,96,128]{3,2,1,0:T(8,128)(2,1)}, bf16[4,5,96,128]{3,2,1,0:T(8,128)(2,1)S(1)}, u32[]{:S(2)}, u32[]{:S(2)}) collective-permute-start(bf16[4,5,96,128]{3,2,1,0:T(8,128)(2,1)} %after.4.a_ref), channel_id=1, source_target_pairs={{0,1},{1,2},{2,3},{3,0},{4,5},{5,6},{6,7},{7,4},{8,9},{9,10},{10,1... | collective-permute-start | bytes 1474568 | tf_op jit(solution)/shard_map/ppermute | solution.py:512
  74.8 0.8 copy-start.6
  94.5 0.8 copy-start.4
  95.3 2.2 collective-permute-start.9
  97.5 0.8 copy-start.7
  254.6 1.5 collective-permute-start.10
  257.0 4.3 %collective-permute-start.11 = (f32[4,2,8,192]{3,2,1,0:T(8,128)S(1)}, f32[4,2,8,192]{3,2,1,0:T(8,128)S(1)}, u32[]{:S(2)}, u32[]{:S(2)}) collective-permute-start(f32[4,2,8,192]{3,2,1,0:T(8,128)S(1)} %add.73), channel_id=1, source_target_pairs={{0,8},{1,9},{2,10},{3,11},{4,12},{5,13},{6,14},{7,15},{8,0},{9,1},... | collective-permute-start | bytes 147464 | tf_op jit(solution)/shard_map/ppermute | solution.py:512
  258.5 5.0 %collective-permute-start.12 = (f32[4,2,8,192]{3,2,1,0:T(8,128)S(1)}, f32[4,2,8,192]{3,2,1,0:T(8,128)S(1)}, u32[]{:S(2)}, u32[]{:S(2)}) collective-permute-start(f32[4,2,8,192]{3,2,1,0:T(8,128)S(1)} %add.73), channel_id=1, source_target_pairs={{0,16},{1,17},{2,18},{3,19},{4,20},{5,21},{6,22},{7,23},{8,24},{9,... | collective-permute-start | bytes 147464 | tf_op jit(solution)/shard_map/ppermute | solution.py:512
  259.4 5.2 %collective-permute-start.13 = (f32[4,2,8,192]{3,2,1,0:T(8,128)S(1)}, f32[4,2,8,192]{3,2,1,0:T(8,128)S(1)}, u32[]{:S(2)}, u32[]{:S(2)}) collective-permute-start(f32[4,2,8,192]{3,2,1,0:T(8,128)S(1)} %add.73), channel_id=1, source_target_pairs={{0,24},{1,25},{2,26},{3,27},{4,28},{5,29},{6,30},{7,31},{8,16},{9,... | collective-permute-start | bytes 147464 | tf_op jit(solution)/shard_map/ppermute | solution.py:512
  264.6 4.5 %collective-permute-start.14 = (f32[4,2,8,192]{3,2,1,0:T(8,128)S(1)}, f32[4,2,8,192]{3,2,1,0:T(8,128)S(1)}, u32[]{:S(2)}, u32[]{:S(2)}) collective-permute-start(f32[4,2,8,192]{3,2,1,0:T(8,128)S(1)} %add_add_fusion), channel_id=1, source_target_pairs={{0,1},{1,0},{2,3},{3,2},{4,5},{5,4},{6,7},{7,6},{8,9},{9,8},{10,11... | collective-permute-start | bytes 147464 | tf_op jit(solution)/shard_map/ppermute | solution.py:512
  264.7 6.8 %collective-permute-start.15 = (f32[4,2,8,192]{3,2,1,0:T(8,128)S(1)}, f32[4,2,8,192]{3,2,1,0:T(8,128)S(1)}, u32[]{:S(2)}, u32[]{:S(2)}) collective-permute-start(f32[4,2,8,192]{3,2,1,0:T(8,128)S(1)} %add_add_fusion), channel_id=1, source_target_pairs={{0,2},{1,3},{2,0},{3,1},{4,6},{5,7},{6,4},{7,5},{8,10},{9,11},{10,... | collective-permute-start | bytes 147464 | tf_op jit(solution)/shard_map/ppermute | solution.py:512
  267.5 6.2 %collective-permute-start.16 = (f32[4,2,8,192]{3,2,1,0:T(8,128)S(1)}, f32[4,2,8,192]{3,2,1,0:T(8,128)S(1)}, u32[]{:S(2)}, u32[]{:S(2)}) collective-permute-start(f32[4,2,8,192]{3,2,1,0:T(8,128)S(1)} %add_add_fusion), channel_id=1, source_target_pairs={{0,3},{1,2},{2,1},{3,0},{4,7},{5,6},{6,5},{7,4},{8,11},{9,10},{10,... | collective-permute-start | bytes 147464 | tf_op jit(solution)/shard_map/ppermute | solution.py:512
Sparse Core Ops, SparseCore 0:
  10.8 109.7 all-gather.2

commit v3 on v2

--- a/solution.py
+++ b/solution.py
@@ -233,17 +233,15 @@
     )(meta, x, a, b, upb, *kept)
 
 
-GP = 0.3275911 * math.sqrt(0.5)
-GA = [0.5 * c for c in (0.254829592, -0.284496736, 1.421413741, -1.453152027, 1.061405429)]
-GC = 1.0 / math.sqrt(2.0 * math.pi)
+def bf(v):
+    return jnp.asarray(v, BF)
 
 
 def gelu_pair(z):
-    t = 1.0 / (1.0 + GP * jnp.abs(z))
-    e = jnp.exp(-0.5 * z * z)
-    tail = t * (GA[0] + t * (GA[1] + t * (GA[2] + t * (GA[3] + t * GA[4])))) * e
-    cdf = jnp.where(z > 0, 1.0 - tail, tail)
-    return z * cdf, cdf + z * (GC * e)
+    cdf = 0.5 + 0.5 * lax.erf(z * math.sqrt(0.5))
+    zb = z.astype(BF)
+    pdf = jnp.exp2(zb * zb * bf(-0.5 * math.log2(math.e))) * bf(1.0 / math.sqrt(2.0 * math.pi))
+    return (z * cdf).astype(BF), cdf.astype(BF) + zb * pdf
 
 
 def ln_stats(v):
@@ -295,8 +293,8 @@
     for c in range(FF // FC):
         s = pl.ds(c * FC, FC)
         a, d = gelu_pair(mm(h1b, wi_scr[:, s]) + bi_ref[0:1, s])
-        act_scr[:, s] = a.astype(BF)
-        dact_scr[:, s] = d.astype(BF)
+        act_scr[:, s] = a
+        dact_scr[:, s] = d
     n2, r2 = ln_stats(h1 + mm_nt(act_scr[...], wb_scr[...]) + vec_ref[3:4])
     ho_ref[0] = (n2 * vec_ref[4:5] + vec_ref[5:6]).astype(BF)
     gs = ln_back(g_ref[0].astype(F32), n2, r2, vec_ref[4:5])
@@ -304,7 +302,7 @@
     for c in range(FF // FC):
         s = pl.ds(c * FC, FC)
         ga = mm(gsb, wb_scr[:, s])
-        gi_scr[:, s] = (ga * dact_scr[:, s].astype(F32)).astype(BF)
+        gi_scr[:, s] = ga.astype(BF) * dact_scr[:, s]
     gh = gs + mm_nt(gi_scr[...], wi_scr[...])
     gf = ln_back(gh, n1, r1, vec_ref[1:2])
     gf_ref[0] = gf

time: 282 us -> 270 us (0.957)
  Pallas kernels: 196 us -> 185 us
    pallas_call x1, Pallas kernels: 84.1 us -> 72.8 us  [ffn(): pl.pallas_call(ffn_body, grid_spec=pltpu.PrefetchScalarGridSpec(num_scala...]
  transfers between devices with their start and end apart: 18 -> 18, of which waited for: 15 -> 15; matrix products, arithmetic and copies ran while one was open for 1% -> 1% of each run, Pallas kernels for 21% -> 22%
where the time goes in v3:
time: 270 us
  Pallas kernels  185 us (69%)
  waiting for transfers between devices  44.6 us (17%)
  starting transfers between devices  15.5 us (6%)
  between operations  14.1 us (5%)
  local copies, waits for them, and re-layouts  9 us (3%)
    pallas_call x1, Pallas kernels, ffn(): pl.pallas_call(ffn_body, grid_spec=pltpu.PrefetchScalarGridSpec(num_scala...  72.8 us
    pallas_call x4, Pallas kernels, attn_fwd(): pl.pallas_call(attn_fwd_body, grid_spec=pltpu.PrefetchScalarGridSpec(num_...  57.4 us
    pallas_call x1, Pallas kernels, attn_bwd(): pl.pallas_call(attn_bwd_body, grid_spec=pltpu.PrefetchScalarGridSpec(num_...  49.8 us
    ppermute x17, waiting for transfers between devices, flip(): return lax.ppermute(value, AXES, pairs)  36.7 us
    ppermute x17, starting transfers between devices, flip(): return lax.ppermute(value, AXES, pairs)  15.4 us
    all_gather x1, waiting for transfers between devices, device_block(): rest = lax.all_gather(rest, AXES, axis=0)  7.88 us
    unnamed x17, local copies, waits for them, and re-layouts  6.24 us
  transfers between devices with their start and end apart: 18, of which 15 were waited for; matrix products, arithmetic and copies ran while one was open for 1% of the time, Pallas kernels for 22%

profile of v3, /device:TPU:0, one launch (start us, length us, event | category | flops | bytes accessed | tf_op | source)
XLA Modules:
  0.0 269.9 jit_solution(13051990636318318199)
XLA Ops:
  7.2 1.2 broadcast_in_dim.6.inb_ref
  8.5 2.1 pack.1
  10.5 3.0 %collective-permute-start = (bf16[5,96,128]{2,1,0:T(8,128)(2,1)}, bf16[5,96,128]{2,1,0:T(8,128)(2,1)S(1)}, u32[]{:S(2)}, u32[]{:S(2)}) collective-permute-start(bf16[5,96,128]{2,1,0:T(8,128)(2,1)} %get-tuple-element.46), channel_id=1, source_target_pairs={{0,8},{1,9},{2,10},{3,11},{4,12},{5,13},{6,14},{7,15},{8,0},{9,1},... | collective-permute-start | bytes 368648 | tf_op jit(solution)/shard_map/ppermute | solution.py:510
  13.6 1.5 collective-permute-start.1
  15.1 2.5 collective-permute-done
  17.6 3.7 %collective-permute-done.1 = bf16[5,96,128]{2,1,0:T(8,128)(2,1)S(1)} collective-permute-done((bf16[5,96,128]{2,1,0:T(8,128)(2,1)}, bf16[5,96,128]{2,1,0:T(8,128)(2,1)S(1)}, u32[]{:S(2)}, u32[]{:S(2)}) %collective-permute-start.1) | collective-permute-done | bytes 122912 | tf_op jit(solution)/shard_map/ppermute | solution.py:510
  21.3 1.0 pad_maximum_fusion.a_ref
  22.4 1.6 collective-permute-start.3
  26.3 2.7 small_params.1
  29.0 14.4 %attn_fwd.4 = (bf16[4,3,768,256]{3,2,1,0:T(8,128)(2,1)}, bf16[4,4,2,512,128]{4,3,2,1,0:T(8,128)(2,1)}, bf16[4,4,2,512,128]{4,3,2,1,0:T(8,128)(2,1)}, bf16[4,4,2,...) custom-call(s32[24]{0:T(128)} %concatenate.3.meta, ...), custom_call_target="tpu_custom_call" | custom-call | tf_op jit(solution)/shard_map/attn_fwd/pallas_call | solution.py:215
  43.3 1.4 collective-permute-done.3.refs_0_
  45.9 1.7 collective-permute-done.6.b_ref
  48.4 14.4 %attn_fwd.5 = (bf16[4,3,768,256]{3,2,1,0:T(8,128)(2,1)}, bf16[4,4,2,512,128]{4,3,2,1,0:T(8,128)(2,1)}, bf16[4,4,2,512,128]{4,3,2,1,0:T(8,128)(2,1)}, bf16[4,4,2,...) custom-call(s32[24]{0:T(128)} %concatenate.3.meta, ...), custom_call_target="tpu_custom_call", output_to_operand_aliasing={{0}: (5, {}), {1}: (6, {}), {2}: (7, {}), {3}: (8, {}), {4}... | custom-call | tf_op jit(solution)/shard_map/attn_fwd/pallas_call | solution.py:215
  62.8 9.2 %collective-permute-done.5.refs_0_ = bf16[4,5,96,128]{3,2,1,0:T(8,128)(2,1)S(1)} collective-permute-done((bf16[4,5,96,128]{3,2,1,0:T(8,128)(2,1)}, bf16[4,5,96,128]{3,2,1,0:T(8,128)(2,1)S(1)}, u32[]{:S(2)}, u32[]{:S(2)}) %collective-permute-start.5) | collective-permute-done | bytes 491552 | tf_op jit(solution)/shard_map/ppermute | solution.py:510
  73.3 1.6 collective-permute-done.8.b_ref
  75.6 14.3 %attn_fwd.6 = (bf16[4,3,768,256]{3,2,1,0:T(8,128)(2,1)}, bf16[4,4,2,512,128]{4,3,2,1,0:T(8,128)(2,1)}, bf16[4,4,2,512,128]{4,3,2,1,0:T(8,128)(2,1)}, bf16[4,4,2,...) custom-call(s32[24]{0:T(128)} %concatenate.3.meta, ...), custom_call_target="tpu_custom_call", output_to_operand_aliasing={{0}: (5, {}), {1}: (6, {}), {2}: (7, {}), {3}: (8, {}), {4}... | custom-call | tf_op jit(solution)/shard_map/attn_fwd/pallas_call | solution.py:215
  90.0 4.6 %collective-permute-done.7.refs_0_ = bf16[4,5,96,128]{3,2,1,0:T(8,128)(2,1)S(1)} collective-permute-done((bf16[4,5,96,128]{3,2,1,0:T(8,128)(2,1)}, bf16[4,5,96,128]{3,2,1,0:T(8,128)(2,1)S(1)}, u32[]{:S(2)}, u32[]{:S(2)}) %collective-permute-start.7) | collective-permute-done | bytes 491552 | tf_op jit(solution)/shard_map/ppermute | solution.py:510
  95.3 2.2 collective-permute-done.9.b_ref
  98.3 14.4 %attn_fwd.7 = (bf16[4,3,768,256]{3,2,1,0:T(8,128)(2,1)}, bf16[4,4,2,512,128]{4,3,2,1,0:T(8,128)(2,1)}, bf16[4,4,2,512,128]{4,3,2,1,0:T(8,128)(2,1)}, bf16[4,4,2,...) custom-call(s32[24]{0:T(128)} %concatenate.3.meta, ...), custom_call_target="tpu_custom_call", output_to_operand_aliasing={{0}: (5, {}), {1}: (6, {}), {2}: (7, {}), {3}: (8, {}), {4}... | custom-call | tf_op jit(solution)/shard_map/attn_fwd/pallas_call | solution.py:215
  112.7 7.9 %all-gather.3.cloned.1.call-done = bf16[448,96,128]{2,1,0:T(8,128)(2,1)} async-done(((bf16[14,96,128]{2,1,0:T(8,128)(2,1)}), bf16[448,96,128]{2,1,0:T(8,128)(2,1)}) %all-gather.3.cloned.1.call-update) | async-done | bytes 11010064 | tf_op jit(solution)/shard_map/all_gather | solution.py:516
  120.5 72.8 %ffn.1 = (bf16[4,512,768]{2,1,0:T(8,128)(2,1)}, f32[4,512,768]{2,1,0:T(8,128)}, bf16[4,4,2,512,128]{4,3,2,1,0:T(8,128)(2,1)}) custom-call(s32[24]{0:T(128)} %concatenate.3.meta, bf16[4,512,768]{2,1,0:T(8,128)(2,1)} %x_ref.9, bf16[4,512,768]{2,1,0:T(8,128)(2,1)} %g_ref.1, bf16[4,4,2,512,128]{4,3,2,1,0:T(8,128)(2,1)} %get-tuple-element.72.o_ref, ...), custom_call_target="tpu_custom_call" | custom-call | tf_op jit(solution)/shard_map/ffn/pallas_call | solution.py:321
  193.3 49.8 %attn_bwd.1 = (bf16[4,512,768]{2,1,0:T(8,128)(2,1)}, f32[4,2,8,192]{3,2,1,0:T(8,128)}) custom-call(s32[24]{0:T(128)} %concatenate.3.meta, bf16[4,4,2,512,128]{4,3,2,1,0:T(8,128)(2,1)} %get-tuple-element.78.q_ref, bf16[4,4,2,512,128]{4,3,2,1,0:T(8,128)(2,1)} %get-tuple-element.79.k_ref, bf16[4,4,2,512,128]{4,3,2,1,0:T(8,128)(2,1)} %get-tuple-element.80.v_ref, ...), custom_call_target="tpu_custom_call" | custom-call | tf_op jit(solution)/shard_map/attn_bwd/pallas_call | solution.py:399
  243.5 1.2 collective-permute-done.10
  245.5 1.5 collective-permute-start.11
  247.1 0.9 collective-permute-start.12
  247.9 1.2 collective-permute-start.13
  249.9 2.2 collective-permute-done.12
  252.0 1.1 collective-permute-done.13
  253.2 2.9 %collective-permute-start.15 = (f32[4,2,8,192]{3,2,1,0:T(8,128)S(1)}, f32[4,2,8,192]{3,2,1,0:T(8,128)S(1)}, u32[]{:S(2)}, u32[]{:S(2)}) collective-permute-start(f32[4,2,8,192]{3,2,1,0:T(8,128)S(1)} %add_add_fusion), channel_id=1, source_target_pairs={{0,2},{1,3},{2,0},{3,1},{4,6},{5,7},{6,4},{7,5},{8,10},{9,11},{10,... | collective-permute-start | bytes 147464 | tf_op jit(solution)/shard_map/ppermute | solution.py:510
  256.1 1.5 collective-permute-start.16
  257.6 2.4 collective-permute-done.15
  260.0 2.2 collective-permute-done.16
  (44 shorter events, 10.8 us)
Async XLA Ops:
  7.2 113.4 %all-gather.3.cloned.1.call-start = ((), (), s32[]{:S(2)}) async-start(), calls=%async_computation | async-start | bytes 11354112 | tf_op jit(solution)/shard_map/all_gather | solution.py:516
  10.5 7.1 %collective-permute-start = (bf16[5,96,128]{2,1,0:T(8,128)(2,1)}, bf16[5,96,128]{2,1,0:T(8,128)(2,1)S(1)}, u32[]{:S(2)}, u32[]{:S(2)}) collective-permute-start(bf16[5,96,128]{2,1,0:T(8,128)(2,1)} %get-tuple-element.46), channel_id=1, source_target_pairs={{0,8},{1,9},{2,10},{3,11},{4,12},{5,13},{6,14},{7,15},{8,0},{9,1},... | collective-permute-start | bytes 368648 | tf_op jit(solution)/shard_map/ppermute | solution.py:510
  13.6 7.7 %collective-permute-start.1 = (bf16[5,96,128]{2,1,0:T(8,128)(2,1)}, bf16[5,96,128]{2,1,0:T(8,128)(2,1)S(1)}, u32[]{:S(2)}, u32[]{:S(2)}) collective-permute-start(bf16[5,96,128]{2,1,0:T(8,128)(2,1)} %get-tuple-element.46), channel_id=1, source_target_pairs={{0,16},{1,17},{2,18},{3,19},{4,20},{5,21},{6,22},{7,23},{8,24},{9,... | collective-permute-start | bytes 368648 | tf_op jit(solution)/shard_map/ppermute | solution.py:510
  15.1 6.2 %collective-permute-start.2 = (bf16[5,96,128]{2,1,0:T(8,128)(2,1)}, bf16[5,96,128]{2,1,0:T(8,128)(2,1)S(1)}, u32[]{:S(2)}, u32[]{:S(2)}) collective-permute-start(bf16[5,96,128]{2,1,0:T(8,128)(2,1)} %get-tuple-element.46), channel_id=1, source_target_pairs={{0,24},{1,25},{2,26},{3,27},{4,28},{5,29},{6,30},{7,31},{8,16},{9,... | collective-permute-start | bytes 368648 | tf_op jit(solution)/shard_map/ppermute | solution.py:510
  22.3 3.3 %copy-start = (bf16[4,5,96,128]{3,2,1,0:T(8,128)(2,1)}, bf16[4,5,96,128]{3,2,1,0:T(8,128)(2,1)S(1)}, u32[]{:S(2)}) copy-start(bf16[4,5,96,128]{3,2,1,0:T(8,128)(2,1)S(1)} %pad_maximum_fusion.a_ref) | copy-start | bytes 1474564
  22.3 3.2 %collective-permute-start.4 = (bf16[4,5,96,128]{3,2,1,0:T(8,128)(2,1)S(1)}, bf16[4,5,96,128]{3,2,1,0:T(8,128)(2,1)S(1)}, u32[]{:S(2)}, u32[]{:S(2)}) collective-permute-start(bf16[4,5,96,128]{3,2,1,0:T(8,128)(2,1)S(1)} %pad_maximum_fusion.a_ref), channel_id=1, source_target_pairs={{0,4},{1,5},{2,6},{3,7},{4,0},{5,1},{6,2},{7,3},{8,12},{9,13},{10,... | collective-permute-start | bytes 1474568 | tf_op jit(solution)/shard_map/ppermute | solution.py:510
  22.4 22.4 %collective-permute-start.3 = (bf16[4,5,96,128]{3,2,1,0:T(8,128)(2,1)S(1)}, bf16[4,5,96,128]{3,2,1,0:T(8,128)(2,1)S(1)}, u32[]{:S(2)}, u32[]{:S(2)}) collective-permute-start(bf16[4,5,96,128]{3,2,1,0:T(8,128)(2,1)S(1)} %pad_maximum_fusion.a_ref), channel_id=1, source_target_pairs={{0,1},{1,2},{2,3},{3,0},{4,5},{5,6},{6,7},{7,4},{8,9},{9,10},{10,1... | collective-permute-start | bytes 1474568 | tf_op jit(solution)/shard_map/ppermute | solution.py:510
  25.5 0.8 copy-start.1
  44.8 0.8 copy-start.2
  45.5 2.1 collective-permute-start.6
  45.5 26.4 %collective-permute-start.5 = (bf16[4,5,96,128]{3,2,1,0:T(8,128)(2,1)}, bf16[4,5,96,128]{3,2,1,0:T(8,128)(2,1)S(1)}, u32[]{:S(2)}, u32[]{:S(2)}) collective-permute-start(bf16[4,5,96,128]{3,2,1,0:T(8,128)(2,1)} %after.3.a_ref), channel_id=1, source_target_pairs={{0,1},{1,2},{2,3},{3,0},{4,5},{5,6},{6,7},{7,4},{8,9},{9,10},{10,1... | collective-permute-start | bytes 1474568 | tf_op jit(solution)/shard_map/ppermute | solution.py:510
  47.6 0.8 copy-start.5
  72.0 0.8 copy-start.3
  72.8 2.1 collective-permute-start.8
  72.8 21.8 %collective-permute-start.7 = (bf16[4,5,96,128]{3,2,1,0:T(8,128)(2,1)}, bf16[4,5,96,128]{3,2,1,0:T(8,128)(2,1)S(1)}, u32[]{:S(2)}, u32[]{:S(2)}) collective-permute-start(bf16[4,5,96,128]{3,2,1,0:T(8,128)(2,1)} %after.4.a_ref), channel_id=1, source_target_pairs={{0,1},{1,2},{2,3},{3,0},{4,5},{5,6},{6,7},{7,4},{8,9},{9,10},{10,1... | collective-permute-start | bytes 1474568 | tf_op jit(solution)/shard_map/ppermute | solution.py:510
  74.8 0.8 copy-start.6
  94.5 0.8 copy-start.4
  95.3 2.2 collective-permute-start.9
  97.5 0.8 copy-start.7
  243.2 1.5 collective-permute-start.10
  245.5 4.3 %collective-permute-start.11 = (f32[4,2,8,192]{3,2,1,0:T(8,128)S(1)}, f32[4,2,8,192]{3,2,1,0:T(8,128)S(1)}, u32[]{:S(2)}, u32[]{:S(2)}) collective-permute-start(f32[4,2,8,192]{3,2,1,0:T(8,128)S(1)} %add.73), channel_id=1, source_target_pairs={{0,8},{1,9},{2,10},{3,11},{4,12},{5,13},{6,14},{7,15},{8,0},{9,1},... | collective-permute-start | bytes 147464 | tf_op jit(solution)/shard_map/ppermute | solution.py:510
  247.1 5.0 %collective-permute-start.12 = (f32[4,2,8,192]{3,2,1,0:T(8,128)S(1)}, f32[4,2,8,192]{3,2,1,0:T(8,128)S(1)}, u32[]{:S(2)}, u32[]{:S(2)}) collective-permute-start(f32[4,2,8,192]{3,2,1,0:T(8,128)S(1)} %add.73), channel_id=1, source_target_pairs={{0,16},{1,17},{2,18},{3,19},{4,20},{5,21},{6,22},{7,23},{8,24},{9,... | collective-permute-start | bytes 147464 | tf_op jit(solution)/shard_map/ppermute | solution.py:510
  247.9 5.2 %collective-permute-start.13 = (f32[4,2,8,192]{3,2,1,0:T(8,128)S(1)}, f32[4,2,8,192]{3,2,1,0:T(8,128)S(1)}, u32[]{:S(2)}, u32[]{:S(2)}) collective-permute-start(f32[4,2,8,192]{3,2,1,0:T(8,128)S(1)} %add.73), channel_id=1, source_target_pairs={{0,24},{1,25},{2,26},{3,27},{4,28},{5,29},{6,30},{7,31},{8,16},{9,... | collective-permute-start | bytes 147464 | tf_op jit(solution)/shard_map/ppermute | solution.py:510
  253.1 4.5 %collective-permute-start.14 = (f32[4,2,8,192]{3,2,1,0:T(8,128)S(1)}, f32[4,2,8,192]{3,2,1,0:T(8,128)S(1)}, u32[]{:S(2)}, u32[]{:S(2)}) collective-permute-start(f32[4,2,8,192]{3,2,1,0:T(8,128)S(1)} %add_add_fusion), channel_id=1, source_target_pairs={{0,1},{1,0},{2,3},{3,2},{4,5},{5,4},{6,7},{7,6},{8,9},{9,8},{10,11... | collective-permute-start | bytes 147464 | tf_op jit(solution)/shard_map/ppermute | solution.py:510
  253.2 6.8 %collective-permute-start.15 = (f32[4,2,8,192]{3,2,1,0:T(8,128)S(1)}, f32[4,2,8,192]{3,2,1,0:T(8,128)S(1)}, u32[]{:S(2)}, u32[]{:S(2)}) collective-permute-start(f32[4,2,8,192]{3,2,1,0:T(8,128)S(1)} %add_add_fusion), channel_id=1, source_target_pairs={{0,2},{1,3},{2,0},{3,1},{4,6},{5,7},{6,4},{7,5},{8,10},{9,11},{10,... | collective-permute-start | bytes 147464 | tf_op jit(solution)/shard_map/ppermute | solution.py:510
  256.1 6.2 %collective-permute-start.16 = (f32[4,2,8,192]{3,2,1,0:T(8,128)S(1)}, f32[4,2,8,192]{3,2,1,0:T(8,128)S(1)}, u32[]{:S(2)}, u32[]{:S(2)}) collective-permute-start(f32[4,2,8,192]{3,2,1,0:T(8,128)S(1)} %add_add_fusion), channel_id=1, source_target_pairs={{0,3},{1,2},{2,1},{3,0},{4,7},{5,6},{6,5},{7,4},{8,11},{9,10},{10,... | collective-permute-start | bytes 147464 | tf_op jit(solution)/shard_map/ppermute | solution.py:510
Sparse Core Ops, SparseCore 0:
  10.8 109.7 all-gather.2

commit v4 on v3

v4 whole, which is shorter than its diff:
```python
import math

import jax
import jax.numpy as jnp
from jax import lax
from jax.experimental import pallas as pl
from jax.experimental.pallas import tpu as pltpu
from jax.sharding import Mesh, PartitionSpec as P

D = 768
HD = 64
RANK = 8
L = 512
FF = 3072
F32 = jnp.float32
BF = jnp.bfloat16

NF = 8
NR = 4
FB = D // NF
RB = D // NR
NP = D // 128
NH = 2 * NP
STEPS = 2
SP = NP // STEPS
SW = 128 * SP
VMEM = 60 << 20

DOWN0 = 64
ATTN0 = 80
GAIN0 = 83
SHIFT0 = 85
INB0 = 87
BACKB0 = 91


def mm(a, b):
    return jnp.dot(a, b, preferred_element_type=F32)


def mm_nt(a, b):
    return lax.dot_general(a, b, (((1,), (1,)), ((), ())), preferred_element_type=F32)


def lanes(rows):
    return lax.broadcasted_iota(jnp.int32, (rows, 128), 1)


def params(n):
    return pltpu.CompilerParams(dimension_semantics=("arbitrary",) * n, vmem_limit_bytes=VMEM)


def whole_spec(*shape):
    return pl.BlockSpec(shape, lambda *_: (0,) * len(shape), pipeline_mode=pl.Buffered(1))


def pack_body(qkv_ref, attn_ref, down_ref, gain_ref, shift_ref, inb_ref, backb_ref, wo_ref, wi_ref, wb_ref,
              first_ref, rest_ref, again_ref, scr):
    scr[...] = jnp.zeros_like(scr)
    up = lambda v: v.astype(F32)
    for k in range(2):
        scr[pl.ds(DOWN0 + RANK * k, RANK), :FB] = up(down_ref[k])
    inb = up(inb_ref[...])
    rows = [up(attn_ref[...]), up(gain_ref[...]), up(shift_ref[...])]
    rows += [inb[:, FB * j : FB * j + FB] for j in range(FF // D)] + [up(backb_ref[...])]
    at = ATTN0
    for v in rows:
        scr[pl.ds(at, v.shape[0]), :FB] = v
        at += v.shape[0]
    small = scr[...].T[:FB, 64:].astype(BF)
    for k in range(3):
        first_ref[k] = qkv_ref[k, :, :128]
    first_ref[3] = jnp.concatenate([qkv_ref[0, :, 128:], qkv_ref[1, :, 128:]], axis=1)
    first_ref[4] = jnp.concatenate([qkv_ref[2, :, 128:], small], axis=1)
    for j in range(6):
        rest_ref[j] = wi_ref[:, 128 * j : 128 * j + 128]
    rest_ref[6] = wo_ref[:, :128]
    rest_ref[7] = jnp.concatenate([wo_ref[:, 128:], wo_ref[:, 128:]], axis=1)
    for h in range(2):
        for j in range(3):
            rest_ref[8 + 3 * h + j] = wb_ref[FB * h : FB * h + FB, 128 * j : 128 * j + 128]
    again_ref[...] = rest_ref[...]


def pack(qkv, attn, down, gain, shift, inb, backb, wo, wi, wb):
    return pl.pallas_call(
        pack_body,
        out_shape=[jax.ShapeDtypeStruct((5, FB, 128), BF), jax.ShapeDtypeStruct((14, FB, 128), BF),
                   jax.ShapeDtypeStruct((14, FB, 128), BF)],
        scratch_shapes=[pltpu.VMEM((128, 128), F32)],
        compiler_params=pltpu.CompilerParams(vmem_limit_bytes=VMEM),
        name="pack",
    )(qkv, attn, down.transpose(0, 2, 1), gain, shift, inb[None], backb[None], wo, wi, wb.T)


def assemble(meta, src, up_ref, w_ref, sm_ref, upb_ref, vec_ref, bi_ref, scr):
    z = meta[8]
    for s in range(NF):
        rows = pl.ds(pl.multiple_of(meta[s], 32), FB)
        parts = [[], [], []]
        for r in range(NR):
            slot = z ^ r
            t3, t4 = src[s][slot, 3], src[s][slot, 4]
            parts[0] += [src[s][slot, 0], t3[:, :64]]
            parts[1] += [src[s][slot, 1], t3[:, 64:]]
            parts[2] += [src[s][slot, 2], t4[:, :64]]
        for k in range(3):
            w_ref[k, rows, :] = jnp.concatenate(parts[k], axis=1)
        scr[rows, :] = src[s][0, 4]
    sm = scr[...]
    lane = lanes(D)
    sm_ref[...] = jnp.where(jnp.logical_and(lane >= DOWN0, lane < DOWN0 + 2 * RANK), sm, jnp.zeros((), BF))
    t = sm.astype(F32).T
    row = lambda i: t[i : i + 1]
    zero = jnp.zeros((1, D), F32)
    vec_ref[...] = jnp.concatenate(
        [row(ATTN0 + 2), row(GAIN0), row(SHIFT0), row(BACKB0), row(GAIN0 + 1), row(SHIFT0 + 1), zero, zero], axis=0
    )
    bi_ref[...] = jnp.concatenate(
        [t[INB0 + j : INB0 + j + 1, FB * f : FB * f + FB] for f in range(NF) for j in range(4)], axis=1
    )
    zb = jnp.zeros((RANK, D), F32)
    for k in range(2):
        b = up_ref[k].astype(F32) * 2.0
        body = [jnp.zeros((DOWN0, D), F32)] + ([b, zb] if k == 0 else [zb, b])
        bias = jnp.broadcast_to(row(ATTN0 + k), (RANK, D))
        keep = lax.broadcasted_iota(jnp.int32, (RANK, D), 0) == 0
        body.append(jnp.where(keep, bias, 0.0))
        body.append(jnp.zeros((128 - DOWN0 - 3 * RANK, D), F32))
        upb_ref[k] = jnp.concatenate(body, axis=0).astype(BF)


def attn_fwd_body(meta, x_ref, up_ref, *refs):
    src = refs[:NF]
    w_ref, sm_ref, upb_ref, vec_ref, bi_ref, q_ref, k_ref, v_ref, p_ref, o_ref, li_ref, u_ref, scr = refs[NF:]
    i, step = pl.program_id(0), pl.program_id(1)

    @pl.when(jnp.logical_and(i == 0, step == 0))
    def _():
        assemble(meta, src, up_ref, w_ref, sm_ref, upb_ref, vec_ref, bi_ref, scr)

    lane = lanes(L)

    @pl.when(step == 0)
    def _():
        x = x_ref[0]
        u = mm(x, sm_ref[...]).astype(BF)
        u_ref[0] = u
        ua = jnp.where(lane == ATTN0, jnp.ones((), BF), u)
        for c in range(D // 256):
            s = slice(256 * c, 256 * c + 256)
            q = mm(x, w_ref[0, :, s]) + mm(ua, upb_ref[0, :, s])
            q_ref[0, :, s] = q.astype(BF) * jnp.asarray(0.125, BF)
            k_ref[0, :, s] = mm(x, w_ref[1, :, s]).astype(BF)
            v_ref[0, :, s] = (mm(x, w_ref[2, :, s]) + mm(ua, upb_ref[1, :, s])).astype(BF)

    live = meta[16 + 2 * i] + meta[17 + 2 * i]
    mask = jnp.where(lax.broadcasted_iota(jnp.int32, (1, L), 1) < live, 0.0, -1e30)
    left = lane < HD
    zero = jnp.zeros((), BF)
    one = jnp.ones((), BF)
    for j in range(SP):
        tile = pl.ds(pl.multiple_of(step * SW + 128 * j, 128), 128)
        qp, kp, vp = q_ref[0, :, tile], k_ref[0, :, tile], v_ref[0, :, tile]
        acc = None
        for h in range(2):
            own = left if h == 0 else jnp.logical_not(left)
            s = mm_nt(qp, jnp.where(own, kp, zero)) + mask
            m = jnp.max(s, axis=1, keepdims=True)
            pb = jnp.exp(s - m).astype(BF)
            p_ref[0, 2 * j + h] = pb
            rhs = jnp.concatenate([jnp.where(own, vp, zero), jnp.where(own, one, zero)], axis=1)
            part = mm(pb, rhs)
            acc = part if acc is None else acc + part
        li = 1.0 / acc[:, 128:]
        c = slice(128 * j, 128 * j + 128)
        li_ref[0, :, c] = li
        o_ref[0, :, c] = (acc[:, :128] * li).astype(BF)


def item_spec(*shape):
    return pl.BlockSpec((1,) + shape, lambda i, *_: (i,) + (0,) * len(shape))


def step_spec():
    return pl.BlockSpec((1, L, SW), lambda i, t, *_: (i, 0, t))


def probs_spec():
    return pl.BlockSpec((1, 2 * SP, L, L), lambda i, t, *_: (i, t, 0, 0))


def attn_fwd(meta, x, up, firsts):
    n = x.shape[0]
    wide = lambda d: jax.ShapeDtypeStruct((n, L, D), d)
    consts = [((3, D, D), BF), ((D, 128), BF), ((2, 128, D), BF), ((8, D), F32), ((1, FF), F32)]
    return pl.pallas_call(
        attn_fwd_body,
        grid_spec=pltpu.PrefetchScalarGridSpec(
            num_scalar_prefetch=1,
            grid=(n, STEPS),
            in_specs=[item_spec(L, D), whole_spec(2, RANK, D)] + [whole_spec(NR, 5, FB, 128)] * NF,
            out_specs=[whole_spec(*s) for s, _ in consts]
            + [item_spec(L, D)] * 3
            + [probs_spec(), step_spec(), step_spec(), item_spec(L, 128)],
            scratch_shapes=[pltpu.VMEM((D, 128), BF)],
        ),
        out_shape=[jax.ShapeDtypeStruct(s, d) for s, d in consts]
        + [wide(BF)] * 3
        + [jax.ShapeDtypeStruct((n, NH, L, L), BF), wide(BF), wide(F32), jax.ShapeDtypeStruct((n, L, 128), BF)],
        compiler_params=params(2),
        name="attn_fwd",
    )(meta, x, up, *firsts)


def bf(v):
    return jnp.asarray(v, BF)


def gelu_pair(z):
    cdf = 0.5 + 0.5 * lax.erf(z * math.sqrt(0.5))
    zb = z.astype(BF)
    pdf = jnp.exp2(zb * zb * bf(-0.5 * math.log2(math.e))) * bf(1.0 / math.sqrt(2.0 * math.pi))
    return (z * cdf).astype(BF), cdf.astype(BF) + zb * pdf


def ln_stats(v):
    c = v - jnp.mean(v, axis=-1, keepdims=True)
    r = lax.rsqrt(jnp.mean(c * c, axis=-1, keepdims=True) + 1e-5)
    return c * r, r


def ln_back(g, n, r, w):
    c = g * w
    return r * (c - jnp.mean(c, axis=-1, keepdims=True) - n * jnp.mean(c * n, axis=-1, keepdims=True))


TT = 256
FC = 512


def ffn_body(meta, x_ref, g_ref, o_ref, li_ref, vec_ref, bi_ref, *refs):
    near, far = refs[:NF], refs[NF : 2 * NF]
    ho_ref, gf_ref, dm_ref, wo_scr, wi_scr, wb_scr, act_scr, dact_scr, gi_scr = refs[2 * NF :]

    @pl.when(jnp.logical_and(pl.program_id(0) == 0, pl.program_id(1) == 0))
    def _():
        z = meta[8]
        for s in range(NF):
            rows = pl.ds(pl.multiple_of(meta[s], 32), FB)
            for k in range(NR):
                tile = lambda i: near[s][i] if k == 0 else far[s][k - 1, i]
                r = z ^ k
                for i in range(6):
                    wi_scr[rows, pl.ds(pl.multiple_of(r * D + 128 * i, 128), 128)] = tile(i)
                for h in range(2):
                    down = pl.ds(pl.multiple_of(r * RB + FB * h, 32), FB)
                    for i in range(3):
                        cols = pl.ds(pl.multiple_of(meta[s] * 4 + 128 * i, 128), 128)
                        wb_scr[down, cols] = tile(8 + 3 * h + i)
            blocks = []
            for r in range(NR):
                slot = z ^ r
                for i, width in ((6, 128), (7, 64)):
                    blocks.append(jnp.where(slot == 0, near[s][i], far[s][jnp.maximum(slot - 1, 0), i])[:, :width])
            wo_scr[rows, :] = jnp.concatenate(blocks, axis=1)

    x = x_ref[0].astype(F32)
    n1, r1 = ln_stats(x + mm(o_ref[0], wo_scr[...]) + vec_ref[0:1])
    h1 = n1 * vec_ref[1:2] + vec_ref[2:3]
    h1b = h1.astype(BF)
    for c in range(FF // FC):
        s = pl.ds(c * FC, FC)
        a, d = gelu_pair(mm(h1b, wi_scr[:, s]) + bi_ref[0:1, s])
        act_scr[:, s] = a
        dact_scr[:, s] = d
    n2, r2 = ln_stats(h1 + mm_nt(act_scr[...], wb_scr[...]) + vec_ref[3:4])
    ho_ref[0] = (n2 * vec_ref[4:5] + vec_ref[5:6]).astype(BF)
    gs = ln_back(g_ref[0].astype(F32), n2, r2, vec_ref[4:5])
    gsb = gs.astype(BF)
    for c in range(FF // FC):
        s = pl.ds(c * FC, FC)
        ga = mm(gsb, wb_scr[:, s])
        gi_scr[:, s] = ga.astype(BF) * dact_scr[:, s]
    gh = gs + mm_nt(gi_scr[...], wi_scr[...])
    gf = ln_back(gh, n1, r1, vec_ref[1:2])
    gf_ref[0] = gf
    gm = mm_nt(gf.astype(BF), wo_scr[...])
    dm_ref[0] = (gm * li_ref[0]).astype(BF)


def ffn(meta, x, g, o, li, vec, bi, near, far):
    n = x.shape[0]
    row = pl.BlockSpec((1, TT, D), lambda i, t, *_: (i, t, 0))
    return pl.pallas_call(
        ffn_body,
        grid_spec=pltpu.PrefetchScalarGridSpec(
            num_scalar_prefetch=1,
            grid=(n, L // TT),
            in_specs=[row] * 4
            + [whole_spec(8, D), whole_spec(1, FF)]
            + [whole_spec(14, FB, 128)] * NF
            + [whole_spec(NR - 1, 14, FB, 128)] * NF,
            out_specs=[row] * 3,
            scratch_shapes=[pltpu.VMEM((D, D), BF), pltpu.VMEM((D, FF), BF), pltpu.VMEM((D, FF), BF)]
            + [pltpu.VMEM((TT, FF), BF)] * 3,
        ),
        out_shape=[jax.ShapeDtypeStruct((n, L, D), d) for d in (BF, F32, BF)],
        compiler_params=params(2),
        name="ffn",
    )(meta, x, g, o, li, vec, bi, *near, *far)


def attn_bwd_body(meta, q_ref, k_ref, v_ref, p_ref, o_ref, dm_ref, gf_ref, u_ref, w_ref, sm_ref, upb_ref,
                  hg_ref, ag_ref, dq_scr, dkt_scr, dvt_scr):
    i, step = pl.program_id(0), pl.program_id(1)

    @pl.when(jnp.logical_and(i == 0, step == 0))
    def _():
        ag_ref[...] = jnp.zeros_like(ag_ref)

    left = lanes(L) < HD
    zero = jnp.zeros((), BF)
    neg = jnp.asarray(-1.0, BF)
    for j in range(SP):
        c = slice(128 * j, 128 * j + 128)
        at = step * SW + 128 * j
        kp, vp, dm = k_ref[0, :, c], v_ref[0, :, c], dm_ref[0, :, c]
        lhs = jnp.concatenate([dm, dm * o_ref[0, :, c]], axis=1)
        qt = q_ref[0, :, c].T
        dmt = dm.T
        dq = None
        for h in range(2):
            own = left if h == 0 else jnp.logical_not(left)
            rhs = jnp.concatenate([jnp.where(own, vp, zero), jnp.where(own, neg, zero)], axis=1)
            p = p_ref[0, 2 * j + h]
            ds = (p.astype(F32) * mm_nt(lhs, rhs)).astype(BF)
            part = mm(ds, jnp.where(own, kp, zero))
            dq = part if dq is None else dq + part
            src = slice(HD * h, HD * h + HD)
            dst = pl.ds(pl.multiple_of(at + HD * h, HD), HD)
            dkt_scr[dst, :] = mm(qt[src, :], ds).astype(BF)
            dvt_scr[dst, :] = mm(dmt[src, :], p).astype(BF)
        dq_scr[:, pl.ds(pl.multiple_of(at, 128), 128)] = (dq * 0.125).astype(BF)

    @pl.when(step == STEPS - 1)
    def _():
        dq = dq_scr[...]
        dk = dkt_scr[...].T
        dv = dvt_scr[...].T
        gu = (mm_nt(dq, upb_ref[0]) + mm_nt(dv, upb_ref[1])).astype(BF)
        hg = gf_ref[0] + mm_nt(dq, w_ref[0]) + mm_nt(dk, w_ref[1]) + mm_nt(dv, w_ref[2]) + mm_nt(gu, sm_ref[...])
        hg_ref[0] = hg.astype(BF)
        ut = u_ref[0].T
        ag_ref[0] += mm(ut[DOWN0 : DOWN0 + RANK], dq)
        ag_ref[1] += mm(ut[DOWN0 + RANK : DOWN0 + 2 * RANK], dv)


def attn_bwd(meta, q, k, v, p, o, dm, gf, u, w, sm, upb):
    n = gf.shape[0]
    return pl.pallas_call(
        attn_bwd_body,
        grid_spec=pltpu.PrefetchScalarGridSpec(
            num_scalar_prefetch=1,
            grid=(n, STEPS),
            in_specs=[step_spec()] * 3
            + [probs_spec()]
            + [step_spec()] * 2
            + [item_spec(L, D), item_spec(L, 128), whole_spec(3, D, D), whole_spec(D, 128), whole_spec(2, 128, D)],
            out_specs=[item_spec(L, D), whole_spec(2, RANK, D)],
            scratch_shapes=[pltpu.VMEM((L, D), BF), pltpu.VMEM((D, L), BF), pltpu.VMEM((D, L), BF)],
        ),
        out_shape=[jax.ShapeDtypeStruct((n, L, D), BF), jax.ShapeDtypeStruct((2, RANK, D), F32)],
        compiler_params=params(2),
        name="attn_bwd",
    )(meta, q, k, v, p, o, dm, gf, u, w, sm, upb)


def after(value, *others):
    return pl.pallas_call(
        lambda *refs: None,
        in_specs=[pl.BlockSpec(memory_space=pl.ANY)] * (1 + len(others)),
        out_specs=pl.BlockSpec(memory_space=pl.ANY),
        out_shape=jax.ShapeDtypeStruct(value.shape, value.dtype),
        input_output_aliases={0: 0},
        name="after",
    )(value, *others)


def layer(meta, x, g, up, firsts, near, far):
    w, sm, upb, vec, bi, q, k, v, p, o, li, u = attn_fwd(meta, x, up, firsts)
    ho, gf, dm = ffn(meta, x, g, o, li, vec, bi, near, far(u))
    hg, ag = attn_bwd(meta, q, k, v, p, o, dm, gf, u, w, sm, upb)
    return ho, hg, ag


def finish(ag, tokens):
    return ag * (2.0 / math.sqrt(tokens))


def meta_of(y, x, c, z, lens):
    rows = []
    for core in (c, 1 - c):
        for dy in range(2):
            for dx in range(2):
                rows.append((((y ^ dy) * 2 + (x ^ dx)) * 2 + core) * FB)
    head = jnp.stack([jnp.asarray(v, jnp.int32) for v in rows + [z] + [0] * 7])
    return jnp.concatenate([head, lens.reshape(-1)])


def device_plain(x, lens, qkv, wo, attn, down, up, gain, shift, wi, inb, wb, backb, g):
    tokens = x.shape[0] * L * lax.axis_size("fsdp") * lax.axis_size("rep")
    gather = lambda a, axis, dim: lax.all_gather(a, axis, axis=dim, tiled=True)
    both = lambda a, row, col: gather(gather(a, "rep", col), "fsdp", row)
    qkv, wo, wi, wb = both(qkv, 1, 2), both(wo, 0, 1), both(wi, 0, 1), both(wb, 0, 1)
    attn, down, gain, shift = (gather(a, "fsdp", 1) for a in (attn, down, gain, shift))
    inb, backb = gather(inb, "fsdp", 0), gather(backb, "fsdp", 0)

    def block(f, r):
        rows, cols = slice(FB * f, FB * f + FB), slice(RB * r, RB * r + RB)
        wide = slice(4 * FB * f, 4 * FB * f + 4 * FB)
        return pack(
            qkv[:, rows, cols], attn[:, rows], down[:, rows], gain[:, rows], shift[:, rows], inb[wide], backb[rows],
            wo[rows, cols], wi[rows, D * r : D * r + D], wb[wide, cols],
        )

    blocks = [[block(f, r) for r in range(NR)] for f in range(NF)]
    order = [2 * j + core for core in range(2) for j in range(NF // 2)]
    firsts = [jnp.stack([blocks[f][r][0] for r in range(NR)]) for f in order]
    near = [blocks[f][0][1] for f in order]
    far = [jnp.stack([blocks[f][r][1] for r in range(1, NR)]) for f in order]
    ho, hg, ag = layer(meta_of(0, 0, 0, 0, lens), x, g, up, firsts, near, lambda u: far)
    return ho, hg, finish(lax.psum(ag, ("fsdp", "rep")), tokens)


AXES = ("y", "x", "c", "z")


def flip(value, dy=0, dx=0, dc=0, dz=0):
    pairs = []
    for i in range(32):
        y, x, c, z = i >> 4, (i >> 3) & 1, (i >> 2) & 1, i & 3
        pairs.append((i, ((y ^ dy) << 4) | ((x ^ dx) << 3) | ((c ^ dc) << 2) | (z ^ dz)))
    return lax.ppermute(value, AXES, pairs)


def along_z(value):
    return [flip(value, dz=k) for k in range(1, NR)]


def across(value):
    return [flip(value, dx=1), flip(value, dy=1), flip(value, dy=1, dx=1)]


def both_cores(values):
    return values + [flip(v, dc=1) for v in values]


def device_block(x, lens, qkv, wo, attn, down, up, gain, shift, wi, inb, wb, backb, g):
    tokens = x.shape[0] * L * 32
    own, rest, rest_again = pack(qkv, attn, down, gain, shift, inb, backb, wo, wi, wb)
    line = jnp.stack([own] + along_z(own))
    sides = across(rest)
    rest_line = jnp.stack(along_z(after(rest_again, line)))
    near = both_cores([rest] + sides)
    first_sides = across(after(line, *sides))
    firsts = both_cores([line] + first_sides)
    rest_line = after(rest_line, *first_sides)
    rest_far = across(rest_line)

    def far(u):
        return both_cores([rest_line] + [after(v, u) for v in rest_far])

    meta = meta_of(lax.axis_index("y"), lax.axis_index("x"), lax.axis_index("c"), lax.axis_index("z"), lens)
    meta = after(meta, rest_line, *near)
    ho, hg, ag = layer(meta, x, g, up, firsts, near, far)
    ag = ag + flip(ag, dc=1)
    a, b, c = across(ag)
    ag = (ag + a) + (b + c)
    a, b, c = along_z(ag)
    ag = (ag + a) + (b + c)
    return ho, hg, finish(ag, tokens)


def solution(mesh):
    if mesh.shape["fsdp"] == NF and mesh.shape["rep"] == NR:
        mesh = Mesh(mesh.devices.reshape(2, 2, 2, 4), AXES)
        body, f, r = device_block, ("y", "x", "c"), ("z",)
    else:
        body, f, r = device_plain, ("fsdp",), ("rep",)
    items = P(f + r, None, None)
    in_specs = (
        items,
        P(f + r, None),
        P(None, f, r),
        P(f, r),
        P(None, f),
        P(None, f, None),
        P(),
        P(None, f),
        P(None, f),
        P(f, r),
        P(f),
        P(f, r),
        P(f),
        items,
    )

    def call(layer_input, lens, qkv, wo, attn, down, up, gain, shift, wi, inb, wb, backb, g):
        return jax.shard_map(
            body, mesh=mesh, in_specs=in_specs, out_specs=(items, items, P()), check_vma=False
        )(layer_input, lens, qkv, wo, attn, down, up, gain, shift, wi, inb, wb, backb, g)

    return call
```

time: 270 us -> 253 us (0.937)
  Pallas kernels: 185 us -> 164 us
  starting transfers between devices: 15.5 us -> 35.9 us
  between operations: 14.1 us -> 0.77 us
  waiting for transfers between devices: 44.6 us -> 37.2 us
    ppermute x17 -> x34, starting transfers between devices: 15.4 us -> 35.9 us  [flip(): return lax.ppermute(value, AXES, pairs)]
    pallas_call x4 -> x1, Pallas kernels: 57.4 us -> 44 us  [attn_fwd(): pl.pallas_call(attn_fwd_body, grid_spec=pltpu.PrefetchScalarGridSpec(num_...]
    all_gather x1 -> x0, waiting for transfers between devices: 7.88 us -> none  [device_block(): rest = lax.all_gather(rest, AXES, axis=0)]
    pallas_call x1, Pallas kernels: 49.8 us -> 46.1 us  [attn_bwd(): pl.pallas_call(attn_bwd_body, grid_spec=pltpu.PrefetchScalarGridSpec(num_...]
    unnamed x17 -> x34, local copies, waits for them, and re-layouts: 6.24 us -> 7.97 us
    ppermute x17 -> x34, waiting for transfers between devices: 36.7 us -> 37.2 us  [flip(): return lax.ppermute(value, AXES, pairs)]
  transfers between devices with their start and end apart: 18 -> 34, of which waited for: 15 -> 19; matrix products, arithmetic and copies ran while one was open for 1% -> 2% of each run, Pallas kernels for 22% -> 17%
where the time goes in v4:
time: 253 us
  Pallas kernels  164 us (65%)
  waiting for transfers between devices  37.2 us (15%)
  starting transfers between devices  35.9 us (14%)
  local copies, waits for them, and re-layouts  9.98 us (4%)
  other arithmetic  4.27 us (2%)
    pallas_call x1, Pallas kernels, ffn(): pl.pallas_call(ffn_body, grid_spec=pltpu.PrefetchScalarGridSpec(num_scala...  72.2 us
    pallas_call x1, Pallas kernels, attn_bwd(): pl.pallas_call(attn_bwd_body, grid_spec=pltpu.PrefetchScalarGridSpec(num_...  46.1 us
    pallas_call x1, Pallas kernels, attn_fwd(): pl.pallas_call(attn_fwd_body, grid_spec=pltpu.PrefetchScalarGridSpec(num_...  44 us
    ppermute x34, waiting for transfers between devices, flip(): return lax.ppermute(value, AXES, pairs)  37.2 us
    ppermute x34, starting transfers between devices, flip(): return lax.ppermute(value, AXES, pairs)  35.9 us
    unnamed x34, local copies, waits for them, and re-layouts  7.97 us
  transfers between devices with their start and end apart: 34, of which 19 were waited for; matrix products, arithmetic and copies ran while one was open for 2% of the time, Pallas kernels for 17%

profile of v4, /device:TPU:0, one launch (start us, length us, event | category | flops | bytes accessed | tf_op | source)
XLA Modules:
  0.0 252.5 jit_solution(10603827823668402573)
XLA Ops:
  0.6 1.2 broadcast_in_dim.6.inb_ref
  1.9 2.2 pack.1
  4.0 5.1 %collective-permute-start.2 = (bf16[5,96,128]{2,1,0:T(8,128)(2,1)}, bf16[5,96,128]{2,1,0:T(8,128)(2,1)S(1)}, u32[]{:S(2)}, u32[]{:S(2)}) collective-permute-start(bf16[5,96,128]{2,1,0:T(8,128)(2,1)} %get-tuple-element.24), channel_id=1, source_target_pairs={{0,3},{1,2},{2,1},{3,0},{4,7},{5,6},{6,5},{7,4},{8,11},{9,10},{10,... | collective-permute-start | bytes 368648 | tf_op jit(solution)/shard_map/ppermute | solution.py:444
  9.1 2.4 collective-permute-start.8
  12.8 4.1 %collective-permute-start = (bf16[5,96,128]{2,1,0:T(8,128)(2,1)}, bf16[5,96,128]{2,1,0:T(8,128)(2,1)S(1)}, u32[]{:S(2)}, u32[]{:S(2)}) collective-permute-start(bf16[5,96,128]{2,1,0:T(8,128)(2,1)} %get-tuple-element.24), channel_id=1, source_target_pairs={{0,1},{1,0},{2,3},{3,2},{4,5},{5,4},{6,7},{7,6},{8,9},{9,8},{10,11... | collective-permute-start | bytes 368648 | tf_op jit(solution)/shard_map/ppermute | solution.py:444
  16.9 2.8 %collective-permute-done.1 = bf16[5,96,128]{2,1,0:T(8,128)(2,1)S(1)} collective-permute-done((bf16[5,96,128]{2,1,0:T(8,128)(2,1)}, bf16[5,96,128]{2,1,0:T(8,128)(2,1)S(1)}, u32[]{:S(2)}, u32[]{:S(2)}) %collective-permute-start.1) | collective-permute-done | bytes 122912 | tf_op jit(solution)/shard_map/ppermute | solution.py:444
  19.7 1.2 collective-permute-done
  20.9 1.7 pad_maximum_fusion.1.refs_1_.refs_0_
  22.7 2.8 %collective-permute-start.5 = (bf16[14,96,128]{2,1,0:T(8,128)(2,1)}, bf16[14,96,128]{2,1,0:T(8,128)(2,1)S(1)}, u32[]{:S(2)}, u32[]{:S(2)}) collective-permute-start(bf16[14,96,128]{2,1,0:T(8,128)(2,1)} %after.7), channel_id=1, source_target_pairs={{0,3},{1,2},{2,1},{3,0},{4,7},{5,6},{6,5},{7,4},{8,11},{9,10},{10,... | collective-permute-start | bytes 1032200 | tf_op jit(solution)/shard_map/ppermute | solution.py:444
  26.0 1.8 copy.27.refs_0_
  29.5 2.4 collective-permute-start.11
  32.0 1.0 collective-permute-start.3
  33.5 2.2 collective-permute-done.5
  35.7 1.5 collective-permute-start.9
  37.1 15.5 %collective-permute-done.4 = bf16[14,96,128]{2,1,0:T(8,128)(2,1)S(1)} collective-permute-done((bf16[14,96,128]{2,1,0:T(8,128)(2,1)}, bf16[14,96,128]{2,1,0:T(8,128)(2,1)S(1)}, u32[]{:S(2)}, u32[]{:S(2)}) %collective-permute-start.4) | collective-permute-done | bytes 344096 | tf_op jit(solution)/shard_map/ppermute | solution.py:444
  53.7 1.1 pad_maximum_fusion.refs_0_
  55.5 1.5 collective-permute-start.20
  57.0 1.5 collective-permute-start.21
  59.5 2.0 collective-permute-done.13.refs_7_.refs_5_
  65.2 44.0 %attn_fwd.1 = (bf16[3,768,768]{2,1,0:T(8,128)(2,1)}, bf16[768,128]{1,0:T(8,128)(2,1)}, bf16[2,128,768]{2,1,0:T(8,128)(2,1)}, f32[8,768]{1,0:T(8,128)}, f32[1,307...) custom-call(s32[24]{0:T(128)} %after.10.meta, ...), custom_call_target="tpu_custom_call" | custom-call | tf_op jit(solution)/shard_map/attn_fwd/pallas_call | solution.py:197
  110.8 1.0 copy-done.2
  112.3 1.3 collective-permute-done.25.refs_14_
  113.6 1.5 collective-permute-done.26.refs_15_
  116.0 72.2 %ffn.1 = (bf16[4,512,768]{2,1,0:T(8,128)(2,1)}, f32[4,512,768]{2,1,0:T(8,128)}, bf16[4,512,768]{2,1,0:T(8,128)(2,1)}) custom-call(s32[24]{0:T(128)} %after.10.meta, bf16[4,512,768]{2,1,0:T(8,128)(2,1)} %x_ref.3, bf16[4,512,768]{2,1,0:T(8,128)(2,1)} %g_ref.1, bf16[4,512,768]{2,1,0:T(8,128)(2,1)} %get-tuple-element.26.o_ref, ...), custom_call_target="tpu_custom_call" | custom-call | tf_op jit(solution)/shard_map/ffn/pallas_call | solution.py:295
  188.3 46.1 %attn_bwd.1 = (bf16[4,512,768]{2,1,0:T(8,128)(2,1)}, f32[2,8,768]{2,1,0:T(8,128)}) custom-call(s32[24]{0:T(128)} %after.10.meta, bf16[4,512,768]{2,1,0:T(8,128)(2,1)} %get-tuple-element.32.q_ref, bf16[4,512,768]{2,1,0:T(8,128)(2,1)} %get-tuple-element.33.k_ref, bf16[4,512,768]{2,1,0:T(8,128)(2,1)} %get-tuple-element.34.v_ref, ...), custom_call_target="tpu_custom_call" | custom-call | tf_op jit(solution)/shard_map/attn_bwd/pallas_call | solution.py:361
  234.6 1.3 collective-permute-done.27
  236.7 2.5 collective-permute-start.30
  240.2 1.5 collective-permute-done.30
  241.7 1.6 collective-permute-done.29
  243.8 2.0 collective-permute-start.33
  245.8 2.1 collective-permute-start.32
  248.3 2.0 collective-permute-done.33
  (91 shorter events, 18.5 us)
Async XLA Ops:
  4.0 8.7 %collective-permute-start.2 = (bf16[5,96,128]{2,1,0:T(8,128)(2,1)}, bf16[5,96,128]{2,1,0:T(8,128)(2,1)S(1)}, u32[]{:S(2)}, u32[]{:S(2)}) collective-permute-start(bf16[5,96,128]{2,1,0:T(8,128)(2,1)} %get-tuple-element.24), channel_id=1, source_target_pairs={{0,3},{1,2},{2,1},{3,0},{4,7},{5,6},{6,5},{7,4},{8,11},{9,10},{10,... | collective-permute-start | bytes 368648 | tf_op jit(solution)/shard_map/ppermute | solution.py:444
  9.1 18.8 %collective-permute-start.8 = (bf16[14,96,128]{2,1,0:T(8,128)(2,1)}, bf16[14,96,128]{2,1,0:T(8,128)(2,1)S(1)}, u32[]{:S(2)}, u32[]{:S(2)}) collective-permute-start(bf16[14,96,128]{2,1,0:T(8,128)(2,1)} %get-tuple-element.25.refs_2_.refs_0_), channel_id=1, source_target_pairs={{0,24},{1,25},{2,26},{3,27},{4,28},{5,29},{6,30},{7,31},{8,16},{9,... | collective-permute-start | bytes 1032200 | tf_op jit(solution)/shard_map/ppermute | solution.py:444
  11.6 16.3 %collective-permute-start.7 = (bf16[14,96,128]{2,1,0:T(8,128)(2,1)}, bf16[14,96,128]{2,1,0:T(8,128)(2,1)S(1)}, u32[]{:S(2)}, u32[]{:S(2)}) collective-permute-start(bf16[14,96,128]{2,1,0:T(8,128)(2,1)} %get-tuple-element.25.refs_2_.refs_0_), channel_id=1, source_target_pairs={{0,16},{1,17},{2,18},{3,19},{4,20},{5,21},{6,22},{7,23},{8,24},{9,... | collective-permute-start | bytes 1032200 | tf_op jit(solution)/shard_map/ppermute | solution.py:444
  12.1 15.8 %collective-permute-start.6 = (bf16[14,96,128]{2,1,0:T(8,128)(2,1)}, bf16[14,96,128]{2,1,0:T(8,128)(2,1)S(1)}, u32[]{:S(2)}, u32[]{:S(2)}) collective-permute-start(bf16[14,96,128]{2,1,0:T(8,128)(2,1)} %get-tuple-element.25.refs_2_.refs_0_), channel_id=1, source_target_pairs={{0,8},{1,9},{2,10},{3,11},{4,12},{5,13},{6,14},{7,15},{8,0},{9,1},... | collective-permute-start | bytes 1032200 | tf_op jit(solution)/shard_map/ppermute | solution.py:444
  12.6 7.1 %collective-permute-start.1 = (bf16[5,96,128]{2,1,0:T(8,128)(2,1)}, bf16[5,96,128]{2,1,0:T(8,128)(2,1)S(1)}, u32[]{:S(2)}, u32[]{:S(2)}) collective-permute-start(bf16[5,96,128]{2,1,0:T(8,128)(2,1)} %get-tuple-element.24), channel_id=1, source_target_pairs={{0,2},{1,3},{2,0},{3,1},{4,6},{5,7},{6,4},{7,5},{8,10},{9,11},{10,... | collective-permute-start | bytes 368648 | tf_op jit(solution)/shard_map/ppermute | solution.py:444
  12.8 8.2 %collective-permute-start = (bf16[5,96,128]{2,1,0:T(8,128)(2,1)}, bf16[5,96,128]{2,1,0:T(8,128)(2,1)S(1)}, u32[]{:S(2)}, u32[]{:S(2)}) collective-permute-start(bf16[5,96,128]{2,1,0:T(8,128)(2,1)} %get-tuple-element.24), channel_id=1, source_target_pairs={{0,1},{1,0},{2,3},{3,2},{4,5},{5,4},{6,7},{7,6},{8,9},{9,8},{10,11... | collective-permute-start | bytes 368648 | tf_op jit(solution)/shard_map/ppermute | solution.py:444
  22.7 13.0 %collective-permute-start.5 = (bf16[14,96,128]{2,1,0:T(8,128)(2,1)}, bf16[14,96,128]{2,1,0:T(8,128)(2,1)S(1)}, u32[]{:S(2)}, u32[]{:S(2)}) collective-permute-start(bf16[14,96,128]{2,1,0:T(8,128)(2,1)} %after.7), channel_id=1, source_target_pairs={{0,3},{1,2},{2,1},{3,0},{4,7},{5,6},{6,5},{7,4},{8,11},{9,10},{10,... | collective-permute-start | bytes 1032200 | tf_op jit(solution)/shard_map/ppermute | solution.py:444
  25.5 27.1 %collective-permute-start.4 = (bf16[14,96,128]{2,1,0:T(8,128)(2,1)}, bf16[14,96,128]{2,1,0:T(8,128)(2,1)S(1)}, u32[]{:S(2)}, u32[]{:S(2)}) collective-permute-start(bf16[14,96,128]{2,1,0:T(8,128)(2,1)} %after.7), channel_id=1, source_target_pairs={{0,2},{1,3},{2,0},{3,1},{4,6},{5,7},{6,4},{7,5},{8,10},{9,11},{10,... | collective-permute-start | bytes 1032200 | tf_op jit(solution)/shard_map/ppermute | solution.py:444
  29.5 23.6 %collective-permute-start.11 = (bf16[4,5,96,128]{3,2,1,0:T(8,128)(2,1)}, bf16[4,5,96,128]{3,2,1,0:T(8,128)(2,1)S(1)}, u32[]{:S(2)}, u32[]{:S(2)}) collective-permute-start(bf16[4,5,96,128]{3,2,1,0:T(8,128)(2,1)} %after.8), channel_id=1, source_target_pairs={{0,24},{1,25},{2,26},{3,27},{4,28},{5,29},{6,30},{7,31},{8,16},{9,... | collective-permute-start | bytes 1474568 | tf_op jit(solution)/shard_map/ppermute | solution.py:444
  32.0 20.7 %collective-permute-start.3 = (bf16[14,96,128]{2,1,0:T(8,128)(2,1)}, bf16[14,96,128]{2,1,0:T(8,128)(2,1)S(1)}, u32[]{:S(2)}, u32[]{:S(2)}) collective-permute-start(bf16[14,96,128]{2,1,0:T(8,128)(2,1)} %after.7), channel_id=1, source_target_pairs={{0,1},{1,0},{2,3},{3,2},{4,5},{5,4},{6,7},{7,6},{8,9},{9,8},{10,11... | collective-permute-start | bytes 1032200 | tf_op jit(solution)/shard_map/ppermute | solution.py:444
  33.0 20.4 %collective-permute-start.10 = (bf16[4,5,96,128]{3,2,1,0:T(8,128)(2,1)}, bf16[4,5,96,128]{3,2,1,0:T(8,128)(2,1)S(1)}, u32[]{:S(2)}, u32[]{:S(2)}) collective-permute-start(bf16[4,5,96,128]{3,2,1,0:T(8,128)(2,1)} %after.8), channel_id=1, source_target_pairs={{0,16},{1,17},{2,18},{3,19},{4,20},{5,21},{6,22},{7,23},{8,24},{9,... | collective-permute-start | bytes 1474568 | tf_op jit(solution)/shard_map/ppermute | solution.py:444
  35.7 19.1 %collective-permute-start.9 = (bf16[4,5,96,128]{3,2,1,0:T(8,128)(2,1)}, bf16[4,5,96,128]{3,2,1,0:T(8,128)(2,1)S(1)}, u32[]{:S(2)}, u32[]{:S(2)}) collective-permute-start(bf16[4,5,96,128]{3,2,1,0:T(8,128)(2,1)} %after.8), channel_id=1, source_target_pairs={{0,8},{1,9},{2,10},{3,11},{4,12},{5,13},{6,14},{7,15},{8,0},{9,1},... | collective-permute-start | bytes 1474568 | tf_op jit(solution)/shard_map/ppermute | solution.py:444
  52.6 5.9 %collective-permute-start.16 = (bf16[4,5,96,128]{3,2,1,0:T(8,128)(2,1)S(1)}, bf16[4,5,96,128]{3,2,1,0:T(8,128)(2,1)}, u32[]{:S(2)}, u32[]{:S(2)}) collective-permute-start(bf16[4,5,96,128]{3,2,1,0:T(8,128)(2,1)S(1)} %copy-done.1), channel_id=1, source_target_pairs={{0,4},{1,5},{2,6},{3,7},{4,0},{5,1},{6,2},{7,3},{8,12},{9,13},{10,... | collective-permute-start | bytes 1474568 | tf_op jit(solution)/shard_map/ppermute | solution.py:444
  52.6 4.4 %collective-permute-start.12 = (bf16[14,96,128]{2,1,0:T(8,128)(2,1)S(1)}, bf16[14,96,128]{2,1,0:T(8,128)(2,1)}, u32[]{:S(2)}, u32[]{:S(2)}) collective-permute-start(bf16[14,96,128]{2,1,0:T(8,128)(2,1)S(1)} %copy-done.11), channel_id=1, source_target_pairs={{0,4},{1,5},{2,6},{3,7},{4,0},{5,1},{6,2},{7,3},{8,12},{9,13},{10,... | collective-permute-start | bytes 1032200 | tf_op jit(solution)/shard_map/ppermute | solution.py:444
  53.1 5.9 %collective-permute-start.15 = (bf16[14,96,128]{2,1,0:T(8,128)(2,1)}, bf16[14,96,128]{2,1,0:T(8,128)(2,1)}, u32[]{:S(2)}, u32[]{:S(2)}) collective-permute-start(bf16[14,96,128]{2,1,0:T(8,128)(2,1)} %copy-done.4), channel_id=1, source_target_pairs={{0,4},{1,5},{2,6},{3,7},{4,0},{5,1},{6,2},{7,3},{8,12},{9,13},{10,... | collective-permute-start | bytes 1032200 | tf_op jit(solution)/shard_map/ppermute | solution.py:444
  53.4 5.6 %collective-permute-start.14 = (bf16[14,96,128]{2,1,0:T(8,128)(2,1)}, bf16[14,96,128]{2,1,0:T(8,128)(2,1)}, u32[]{:S(2)}, u32[]{:S(2)}) collective-permute-start(bf16[14,96,128]{2,1,0:T(8,128)(2,1)} %copy-done.5), channel_id=1, source_target_pairs={{0,4},{1,5},{2,6},{3,7},{4,0},{5,1},{6,2},{7,3},{8,12},{9,13},{10,... | collective-permute-start | bytes 1032200 | tf_op jit(solution)/shard_map/ppermute | solution.py:444
  55.5 53.7 %collective-permute-start.20 = (bf16[3,14,96,128]{3,2,1,0:T(8,128)(2,1)}, bf16[3,14,96,128]{3,2,1,0:T(8,128)(2,1)}, u32[]{:S(2)}, u32[]{:S(2)}) collective-permute-start(bf16[3,14,96,128]{3,2,1,0:T(8,128)(2,1)} %after.9.refs_1_.refs_8_), channel_id=1, source_target_pairs={{0,8},{1,9},{2,10},{3,11},{4,12},{5,13},{6,14},{7,15},{8,0},{9,1},... | collective-permute-start | bytes 3096584 | tf_op jit(solution)/shard_map/ppermute | solution.py:444
  57.0 52.4 %collective-permute-start.21 = (bf16[3,14,96,128]{3,2,1,0:T(8,128)(2,1)}, bf16[3,14,96,128]{3,2,1,0:T(8,128)(2,1)S(1)}, u32[]{:S(2)}, u32[]{:S(2)}) collective-permute-start(bf16[3,14,96,128]{3,2,1,0:T(8,128)(2,1)} %after.9.refs_1_.refs_8_), channel_id=1, source_target_pairs={{0,16},{1,17},{2,18},{3,19},{4,20},{5,21},{6,22},{7,23},{8,24},{9,... | collective-permute-start | bytes 3096584 | tf_op jit(solution)/shard_map/ppermute | solution.py:444
  58.5 52.2 %collective-permute-start.22 = (bf16[3,14,96,128]{3,2,1,0:T(8,128)(2,1)}, bf16[3,14,96,128]{3,2,1,0:T(8,128)(2,1)S(1)}, u32[]{:S(2)}, u32[]{:S(2)}) collective-permute-start(bf16[3,14,96,128]{3,2,1,0:T(8,128)(2,1)} %after.9.refs_1_.refs_8_), channel_id=1, source_target_pairs={{0,24},{1,25},{2,26},{3,27},{4,28},{5,29},{6,30},{7,31},{8,16},{9,... | collective-permute-start | bytes 3096584 | tf_op jit(solution)/shard_map/ppermute | solution.py:444
  59.0 3.5 %collective-permute-start.19 = (bf16[4,5,96,128]{3,2,1,0:T(8,128)(2,1)}, bf16[4,5,96,128]{3,2,1,0:T(8,128)(2,1)}, u32[]{:S(2)}, u32[]{:S(2)}) collective-permute-start(bf16[4,5,96,128]{3,2,1,0:T(8,128)(2,1)} %copy-done.8), channel_id=1, source_target_pairs={{0,4},{1,5},{2,6},{3,7},{4,0},{5,1},{6,2},{7,3},{8,12},{9,13},{10,... | collective-permute-start | bytes 1474568 | tf_op jit(solution)/shard_map/ppermute | solution.py:444
  59.0 2.5 %collective-permute-start.13 = (bf16[14,96,128]{2,1,0:T(8,128)(2,1)S(1)}, bf16[14,96,128]{2,1,0:T(8,128)(2,1)S(1)}, u32[]{:S(2)}, u32[]{:S(2)}) collective-permute-start(bf16[14,96,128]{2,1,0:T(8,128)(2,1)S(1)} %copy-done.7), channel_id=1, source_target_pairs={{0,4},{1,5},{2,6},{3,7},{4,0},{5,1},{6,2},{7,3},{8,12},{9,13},{10,... | collective-permute-start | bytes 1032200 | tf_op jit(solution)/shard_map/ppermute | solution.py:444
  62.5 2.8 %collective-permute-start.17 = (bf16[4,5,96,128]{3,2,1,0:T(8,128)(2,1)}, bf16[4,5,96,128]{3,2,1,0:T(8,128)(2,1)}, u32[]{:S(2)}, u32[]{:S(2)}) collective-permute-start(bf16[4,5,96,128]{3,2,1,0:T(8,128)(2,1)} %copy-done.10), channel_id=1, source_target_pairs={{0,4},{1,5},{2,6},{3,7},{4,0},{5,1},{6,2},{7,3},{8,12},{9,13},{10,... | collective-permute-start | bytes 1474568 | tf_op jit(solution)/shard_map/ppermute | solution.py:444
  64.5 47.4 %collective-permute-start.23 = (bf16[3,14,96,128]{3,2,1,0:T(8,128)(2,1)S(1)}, bf16[3,14,96,128]{3,2,1,0:T(8,128)(2,1)}, u32[]{:S(2)}, u32[]{:S(2)}) collective-permute-start(bf16[3,14,96,128]{3,2,1,0:T(8,128)(2,1)S(1)} %copy-done), channel_id=1, source_target_pairs={{0,4},{1,5},{2,6},{3,7},{4,0},{5,1},{6,2},{7,3},{8,12},{9,13},{10,... | collective-permute-start | bytes 3096584 | tf_op jit(solution)/shard_map/ppermute | solution.py:444
  109.2 3.0 %collective-permute-start.24 = (bf16[3,14,96,128]{3,2,1,0:T(8,128)(2,1)}, bf16[3,14,96,128]{3,2,1,0:T(8,128)(2,1)}, u32[]{:S(2)}, u32[]{:S(2)}) collective-permute-start(bf16[3,14,96,128]{3,2,1,0:T(8,128)(2,1)} %after.11.refs_9_), channel_id=1, source_target_pairs={{0,4},{1,5},{2,6},{3,7},{4,0},{5,1},{6,2},{7,3},{8,12},{9,13},{10,... | collective-permute-start | bytes 3096584 | tf_op jit(solution)/shard_map/ppermute | solution.py:444
  110.4 3.2 %collective-permute-start.25 = (bf16[3,14,96,128]{3,2,1,0:T(8,128)(2,1)}, bf16[3,14,96,128]{3,2,1,0:T(8,128)(2,1)S(1)}, u32[]{:S(2)}, u32[]{:S(2)}) collective-permute-start(bf16[3,14,96,128]{3,2,1,0:T(8,128)(2,1)} %after.12.refs_10_), channel_id=1, source_target_pairs={{0,4},{1,5},{2,6},{3,7},{4,0},{5,1},{6,2},{7,3},{8,12},{9,13},{10,... | collective-permute-start | bytes 3096584 | tf_op jit(solution)/shard_map/ppermute | solution.py:444
  111.8 3.3 %collective-permute-start.26 = (bf16[3,14,96,128]{3,2,1,0:T(8,128)(2,1)}, bf16[3,14,96,128]{3,2,1,0:T(8,128)(2,1)S(1)}, u32[]{:S(2)}, u32[]{:S(2)}) collective-permute-start(bf16[3,14,96,128]{3,2,1,0:T(8,128)(2,1)} %after.13.refs_11_), channel_id=1, source_target_pairs={{0,4},{1,5},{2,6},{3,7},{4,0},{5,1},{6,2},{7,3},{8,12},{9,13},{10,... | collective-permute-start | bytes 3096584 | tf_op jit(solution)/shard_map/ppermute | solution.py:444
  236.7 5.0 %collective-permute-start.30 = (f32[2,8,768]{2,1,0:T(8,128)S(1)}, f32[2,8,768]{2,1,0:T(8,128)S(1)}, u32[]{:S(2)}, u32[]{:S(2)}) collective-permute-start(f32[2,8,768]{2,1,0:T(8,128)S(1)} %add.73), channel_id=1, source_target_pairs={{0,24},{1,25},{2,26},{3,27},{4,28},{5,29},{6,30},{7,31},{8,16},{9,... | collective-permute-start | bytes 147464 | tf_op jit(solution)/shard_map/ppermute | solution.py:444
  239.2 4.1 %collective-permute-start.29 = (f32[2,8,768]{2,1,0:T(8,128)S(1)}, f32[2,8,768]{2,1,0:T(8,128)S(1)}, u32[]{:S(2)}, u32[]{:S(2)}) collective-permute-start(f32[2,8,768]{2,1,0:T(8,128)S(1)} %add.73), channel_id=1, source_target_pairs={{0,16},{1,17},{2,18},{3,19},{4,20},{5,21},{6,22},{7,23},{8,24},{9,... | collective-permute-start | bytes 147464 | tf_op jit(solution)/shard_map/ppermute | solution.py:444
  239.7 4.1 %collective-permute-start.28 = (f32[2,8,768]{2,1,0:T(8,128)S(1)}, f32[2,8,768]{2,1,0:T(8,128)S(1)}, u32[]{:S(2)}, u32[]{:S(2)}) collective-permute-start(f32[2,8,768]{2,1,0:T(8,128)S(1)} %add.73), channel_id=1, source_target_pairs={{0,8},{1,9},{2,10},{3,11},{4,12},{5,13},{6,14},{7,15},{8,0},{9,1},... | collective-permute-start | bytes 147464 | tf_op jit(solution)/shard_map/ppermute | solution.py:444
  243.8 6.5 %collective-permute-start.33 = (f32[2,8,768]{2,1,0:T(8,128)S(1)}, f32[2,8,768]{2,1,0:T(8,128)S(1)}, u32[]{:S(2)}, u32[]{:S(2)}) collective-permute-start(f32[2,8,768]{2,1,0:T(8,128)S(1)} %add_add_fusion), channel_id=1, source_target_pairs={{0,3},{1,2},{2,1},{3,0},{4,7},{5,6},{6,5},{7,4},{8,11},{9,10},{10,... | collective-permute-start | bytes 147464 | tf_op jit(solution)/shard_map/ppermute | solution.py:444
  245.8 5.5 %collective-permute-start.32 = (f32[2,8,768]{2,1,0:T(8,128)S(1)}, f32[2,8,768]{2,1,0:T(8,128)S(1)}, u32[]{:S(2)}, u32[]{:S(2)}) collective-permute-start(f32[2,8,768]{2,1,0:T(8,128)S(1)} %add_add_fusion), channel_id=1, source_target_pairs={{0,2},{1,3},{2,0},{3,1},{4,6},{5,7},{6,4},{7,5},{8,10},{9,11},{10,... | collective-permute-start | bytes 147464 | tf_op jit(solution)/shard_map/ppermute | solution.py:444
  247.8 4.1 %collective-permute-start.31 = (f32[2,8,768]{2,1,0:T(8,128)S(1)}, f32[2,8,768]{2,1,0:T(8,128)S(1)}, u32[]{:S(2)}, u32[]{:S(2)}) collective-permute-start(f32[2,8,768]{2,1,0:T(8,128)S(1)} %add_add_fusion), channel_id=1, source_target_pairs={{0,1},{1,0},{2,3},{3,2},{4,5},{5,4},{6,7},{7,6},{8,9},{9,8},{10,11... | collective-permute-start | bytes 147464 | tf_op jit(solution)/shard_map/ppermute | solution.py:444
  (18 other events, 165.3 us)

commit v5 on v4

--- a/solution.py
+++ b/solution.py
@@ -235,7 +235,7 @@
     return r * (c - jnp.mean(c, axis=-1, keepdims=True) - n * jnp.mean(c * n, axis=-1, keepdims=True))
 
 
-TT = 256
+TT = 512
 FC = 512
 
 
@@ -461,9 +461,11 @@
     own, rest, rest_again = pack(qkv, attn, down, gain, shift, inb, backb, wo, wi, wb)
     line = jnp.stack([own] + along_z(own))
     sides = across(rest)
-    rest_line = jnp.stack(along_z(after(rest_again, line)))
+    rest_again = after(rest_again, line)
+    rest_line = jnp.stack(along_z(rest_again))
     near = both_cores([rest] + sides)
-    first_sides = across(after(line, *sides))
+    line = after(line, rest_again, *sides)
+    first_sides = across(line)
     firsts = both_cores([line] + first_sides)
     rest_line = after(rest_line, *first_sides)
     rest_far = across(rest_line)

time: 253 us -> 249 us (0.984)
  Pallas kernels: 164 us -> 161 us
  waiting for transfers between devices: 37.2 us -> 40.2 us
  local copies, waits for them, and re-layouts: 9.98 us -> 6.99 us
    pallas_call x1, Pallas kernels: 72.2 us -> 68.6 us  [ffn(): pl.pallas_call(ffn_body, grid_spec=pltpu.PrefetchScalarGridSpec(num_scala...]
    unnamed x34 -> x31, local copies, waits for them, and re-layouts: 7.97 us -> 5 us
    ppermute x34, waiting for transfers between devices: 37.2 us -> 40.2 us  [flip(): return lax.ppermute(value, AXES, pairs)]
  transfers between devices with their start and end apart: 34 -> 34, of which waited for: 19 -> 20; matrix products, arithmetic and copies ran while one was open for 2% -> 1% of each run, Pallas kernels for 17% -> 18%
where the time goes in v5:
time: 249 us; the launch traced here: 248 us
  Pallas kernels  161 us (65%)
  waiting for transfers between devices  40.2 us (16%)
  starting transfers between devices  35.5 us (14%)
  local copies, waits for them, and re-layouts  6.99 us (3%)
  other arithmetic  4.27 us (2%)
    pallas_call x1, Pallas kernels, ffn(): pl.pallas_call(ffn_body, grid_spec=pltpu.PrefetchScalarGridSpec(num_scala...  68.6 us
    pallas_call x1, Pallas kernels, attn_bwd(): pl.pallas_call(attn_bwd_body, grid_spec=pltpu.PrefetchScalarGridSpec(num_...  45.9 us
    pallas_call x1, Pallas kernels, attn_fwd(): pl.pallas_call(attn_fwd_body, grid_spec=pltpu.PrefetchScalarGridSpec(num_...  44 us
    ppermute x34, waiting for transfers between devices, flip(): return lax.ppermute(value, AXES, pairs)  40.2 us
    ppermute x34, starting transfers between devices, flip(): return lax.ppermute(value, AXES, pairs)  35.5 us
    unnamed x31, local copies, waits for them, and re-layouts  5 us
  transfers between devices with their start and end apart: 34, of which 20 were waited for; matrix products, arithmetic and copies ran while one was open for 1% of the time, Pallas kernels for 18%

profile of v5, /device:TPU:0, one launch (start us, length us, event | category | flops | bytes accessed | tf_op | source)
XLA Modules:
  0.0 248.4 jit_solution(16943553116012332389)
XLA Ops:
  0.6 1.2 broadcast_in_dim.6.inb_ref
  1.9 2.2 pack.1
  4.0 5.1 %collective-permute-start.2 = (bf16[5,96,128]{2,1,0:T(8,128)(2,1)}, bf16[5,96,128]{2,1,0:T(8,128)(2,1)S(1)}, u32[]{:S(2)}, u32[]{:S(2)}) collective-permute-start(bf16[5,96,128]{2,1,0:T(8,128)(2,1)} %get-tuple-element.24), channel_id=1, source_target_pairs={{0,3},{1,2},{2,1},{3,0},{4,7},{5,6},{6,5},{7,4},{8,11},{9,10},{10,... | collective-permute-start | bytes 368648 | tf_op jit(solution)/shard_map/ppermute | solution.py:444
  9.1 2.4 collective-permute-start.8
  12.8 4.1 %collective-permute-start = (bf16[5,96,128]{2,1,0:T(8,128)(2,1)}, bf16[5,96,128]{2,1,0:T(8,128)(2,1)S(1)}, u32[]{:S(2)}, u32[]{:S(2)}) collective-permute-start(bf16[5,96,128]{2,1,0:T(8,128)(2,1)} %get-tuple-element.24), channel_id=1, source_target_pairs={{0,1},{1,0},{2,3},{3,2},{4,5},{5,4},{6,7},{7,6},{8,9},{9,8},{10,11... | collective-permute-start | bytes 368648 | tf_op jit(solution)/shard_map/ppermute | solution.py:444
  16.9 2.8 %collective-permute-done.1 = bf16[5,96,128]{2,1,0:T(8,128)(2,1)S(1)} collective-permute-done((bf16[5,96,128]{2,1,0:T(8,128)(2,1)}, bf16[5,96,128]{2,1,0:T(8,128)(2,1)S(1)}, u32[]{:S(2)}, u32[]{:S(2)}) %collective-permute-start.1) | collective-permute-done | bytes 122912 | tf_op jit(solution)/shard_map/ppermute | solution.py:444
  19.7 1.2 collective-permute-done
  20.9 1.7 pad_maximum_fusion.1.refs_1_.refs_0_
  22.7 2.8 %collective-permute-start.5 = (bf16[14,96,128]{2,1,0:T(8,128)(2,1)}, bf16[14,96,128]{2,1,0:T(8,128)(2,1)S(1)}, u32[]{:S(2)}, u32[]{:S(2)}) collective-permute-start(bf16[14,96,128]{2,1,0:T(8,128)(2,1)} %after.7.refs_1_), channel_id=1, source_target_pairs={{0,3},{1,2},{2,1},{3,0},{4,7},{5,6},{6,5},{7,4},{8,11},{9,10},{10,... | collective-permute-start | bytes 1032200 | tf_op jit(solution)/shard_map/ppermute | solution.py:444
  25.5 1.7 collective-permute-done.7.refs_3_.refs_4_.refs_2_
  28.6 1.7 collective-permute-start.11
  30.4 1.2 collective-permute-start.10
  32.5 1.5 collective-permute-start.9
  34.0 18.6 %collective-permute-done.4 = bf16[14,96,128]{2,1,0:T(8,128)(2,1)S(1)} collective-permute-done((bf16[14,96,128]{2,1,0:T(8,128)(2,1)}, bf16[14,96,128]{2,1,0:T(8,128)(2,1)S(1)}, u32[]{:S(2)}, u32[]{:S(2)}) %collective-permute-start.4) | collective-permute-done | bytes 344096 | tf_op jit(solution)/shard_map/ppermute | solution.py:444
  53.7 1.1 pad_maximum_fusion.refs_0_
  55.5 1.5 collective-permute-start.20
  57.0 1.5 collective-permute-start.21
  59.8 1.3 collective-permute-done.16.refs_4_
  64.8 44.0 %attn_fwd.1 = (bf16[3,768,768]{2,1,0:T(8,128)(2,1)}, bf16[768,128]{1,0:T(8,128)(2,1)}, bf16[2,128,768]{2,1,0:T(8,128)(2,1)}, f32[8,768]{1,0:T(8,128)}, f32[1,307...) custom-call(s32[24]{0:T(128)} %after.10.meta, ...), custom_call_target="tpu_custom_call" | custom-call | tf_op jit(solution)/shard_map/attn_fwd/pallas_call | solution.py:197
  110.6 1.3 collective-permute-done.24.refs_13_
  111.9 1.5 collective-permute-done.25.refs_14_
  113.4 1.3 collective-permute-done.26.refs_15_
  115.7 68.6 %ffn.1 = (bf16[4,512,768]{2,1,0:T(8,128)(2,1)}, f32[4,512,768]{2,1,0:T(8,128)}, bf16[4,512,768]{2,1,0:T(8,128)(2,1)}) custom-call(s32[24]{0:T(128)} %after.10.meta, bf16[4,512,768]{2,1,0:T(8,128)(2,1)} %x_ref.3, bf16[4,512,768]{2,1,0:T(8,128)(2,1)} %g_ref.1, bf16[4,512,768]{2,1,0:T(8,128)(2,1)} %get-tuple-element.26.o_ref, ...), custom_call_target="tpu_custom_call" | custom-call | tf_op jit(solution)/shard_map/ffn/pallas_call | solution.py:295
  184.3 45.9 %attn_bwd.1 = (bf16[4,512,768]{2,1,0:T(8,128)(2,1)}, f32[2,8,768]{2,1,0:T(8,128)}) custom-call(s32[24]{0:T(128)} %after.10.meta, bf16[4,512,768]{2,1,0:T(8,128)(2,1)} %get-tuple-element.32.q_ref, bf16[4,512,768]{2,1,0:T(8,128)(2,1)} %get-tuple-element.33.k_ref, bf16[4,512,768]{2,1,0:T(8,128)(2,1)} %get-tuple-element.34.v_ref, ...), custom_call_target="tpu_custom_call" | custom-call | tf_op jit(solution)/shard_map/attn_bwd/pallas_call | solution.py:361
  230.4 1.3 collective-permute-done.27
  232.5 2.2 collective-permute-start.30
  235.9 1.5 collective-permute-done.30
  237.5 1.3 collective-permute-done.29
  239.6 2.0 collective-permute-start.33
  241.5 2.1 collective-permute-start.32
  244.1 1.7 collective-permute-done.33
  245.9 1.2 collective-permute-done.32
  (88 shorter events, 17.8 us)
Async XLA Ops:
  4.0 8.7 %collective-permute-start.2 = (bf16[5,96,128]{2,1,0:T(8,128)(2,1)}, bf16[5,96,128]{2,1,0:T(8,128)(2,1)S(1)}, u32[]{:S(2)}, u32[]{:S(2)}) collective-permute-start(bf16[5,96,128]{2,1,0:T(8,128)(2,1)} %get-tuple-element.24), channel_id=1, source_target_pairs={{0,3},{1,2},{2,1},{3,0},{4,7},{5,6},{6,5},{7,4},{8,11},{9,10},{10,... | collective-permute-start | bytes 368648 | tf_op jit(solution)/shard_map/ppermute | solution.py:444
  9.1 16.3 %collective-permute-start.8 = (bf16[14,96,128]{2,1,0:T(8,128)(2,1)}, bf16[14,96,128]{2,1,0:T(8,128)(2,1)S(1)}, u32[]{:S(2)}, u32[]{:S(2)}) collective-permute-start(bf16[14,96,128]{2,1,0:T(8,128)(2,1)} %get-tuple-element.25.refs_2_.refs_0_), channel_id=1, source_target_pairs={{0,24},{1,25},{2,26},{3,27},{4,28},{5,29},{6,30},{7,31},{8,16},{9,... | collective-permute-start | bytes 1032200 | tf_op jit(solution)/shard_map/ppermute | solution.py:444
  11.6 15.6 %collective-permute-start.7 = (bf16[14,96,128]{2,1,0:T(8,128)(2,1)}, bf16[14,96,128]{2,1,0:T(8,128)(2,1)S(1)}, u32[]{:S(2)}, u32[]{:S(2)}) collective-permute-start(bf16[14,96,128]{2,1,0:T(8,128)(2,1)} %get-tuple-element.25.refs_2_.refs_0_), channel_id=1, source_target_pairs={{0,16},{1,17},{2,18},{3,19},{4,20},{5,21},{6,22},{7,23},{8,24},{9,... | collective-permute-start | bytes 1032200 | tf_op jit(solution)/shard_map/ppermute | solution.py:444
  12.1 15.2 %collective-permute-start.6 = (bf16[14,96,128]{2,1,0:T(8,128)(2,1)}, bf16[14,96,128]{2,1,0:T(8,128)(2,1)S(1)}, u32[]{:S(2)}, u32[]{:S(2)}) collective-permute-start(bf16[14,96,128]{2,1,0:T(8,128)(2,1)} %get-tuple-element.25.refs_2_.refs_0_), channel_id=1, source_target_pairs={{0,8},{1,9},{2,10},{3,11},{4,12},{5,13},{6,14},{7,15},{8,0},{9,1},... | collective-permute-start | bytes 1032200 | tf_op jit(solution)/shard_map/ppermute | solution.py:444
  12.6 7.1 %collective-permute-start.1 = (bf16[5,96,128]{2,1,0:T(8,128)(2,1)}, bf16[5,96,128]{2,1,0:T(8,128)(2,1)S(1)}, u32[]{:S(2)}, u32[]{:S(2)}) collective-permute-start(bf16[5,96,128]{2,1,0:T(8,128)(2,1)} %get-tuple-element.24), channel_id=1, source_target_pairs={{0,2},{1,3},{2,0},{3,1},{4,6},{5,7},{6,4},{7,5},{8,10},{9,11},{10,... | collective-permute-start | bytes 368648 | tf_op jit(solution)/shard_map/ppermute | solution.py:444
  12.8 8.2 %collective-permute-start = (bf16[5,96,128]{2,1,0:T(8,128)(2,1)}, bf16[5,96,128]{2,1,0:T(8,128)(2,1)S(1)}, u32[]{:S(2)}, u32[]{:S(2)}) collective-permute-start(bf16[5,96,128]{2,1,0:T(8,128)(2,1)} %get-tuple-element.24), channel_id=1, source_target_pairs={{0,1},{1,0},{2,3},{3,2},{4,5},{5,4},{6,7},{7,6},{8,9},{9,8},{10,11... | collective-permute-start | bytes 368648 | tf_op jit(solution)/shard_map/ppermute | solution.py:444
  22.7 9.8 %collective-permute-start.5 = (bf16[14,96,128]{2,1,0:T(8,128)(2,1)}, bf16[14,96,128]{2,1,0:T(8,128)(2,1)S(1)}, u32[]{:S(2)}, u32[]{:S(2)}) collective-permute-start(bf16[14,96,128]{2,1,0:T(8,128)(2,1)} %after.7.refs_1_), channel_id=1, source_target_pairs={{0,3},{1,2},{2,1},{3,0},{4,7},{5,6},{6,5},{7,4},{8,11},{9,10},{10,... | collective-permute-start | bytes 1032200 | tf_op jit(solution)/shard_map/ppermute | solution.py:444
  28.6 24.5 %collective-permute-start.11 = (bf16[4,5,96,128]{3,2,1,0:T(8,128)(2,1)}, bf16[4,5,96,128]{3,2,1,0:T(8,128)(2,1)S(1)}, u32[]{:S(2)}, u32[]{:S(2)}) collective-permute-start(bf16[4,5,96,128]{3,2,1,0:T(8,128)(2,1)} %after.8.refs_0_), channel_id=1, source_target_pairs={{0,24},{1,25},{2,26},{3,27},{4,28},{5,29},{6,30},{7,31},{8,16},{9,... | collective-permute-start | bytes 1474568 | tf_op jit(solution)/shard_map/ppermute | solution.py:444
  30.4 23.0 %collective-permute-start.10 = (bf16[4,5,96,128]{3,2,1,0:T(8,128)(2,1)}, bf16[4,5,96,128]{3,2,1,0:T(8,128)(2,1)S(1)}, u32[]{:S(2)}, u32[]{:S(2)}) collective-permute-start(bf16[4,5,96,128]{3,2,1,0:T(8,128)(2,1)} %after.8.refs_0_), channel_id=1, source_target_pairs={{0,16},{1,17},{2,18},{3,19},{4,20},{5,21},{6,22},{7,23},{8,24},{9,... | collective-permute-start | bytes 1474568 | tf_op jit(solution)/shard_map/ppermute | solution.py:444
  31.6 21.0 %collective-permute-start.4 = (bf16[14,96,128]{2,1,0:T(8,128)(2,1)}, bf16[14,96,128]{2,1,0:T(8,128)(2,1)S(1)}, u32[]{:S(2)}, u32[]{:S(2)}) collective-permute-start(bf16[14,96,128]{2,1,0:T(8,128)(2,1)} %after.7.refs_1_), channel_id=1, source_target_pairs={{0,2},{1,3},{2,0},{3,1},{4,6},{5,7},{6,4},{7,5},{8,10},{9,11},{10,... | collective-permute-start | bytes 1032200 | tf_op jit(solution)/shard_map/ppermute | solution.py:444
  31.6 21.0 %collective-permute-start.3 = (bf16[14,96,128]{2,1,0:T(8,128)(2,1)}, bf16[14,96,128]{2,1,0:T(8,128)(2,1)S(1)}, u32[]{:S(2)}, u32[]{:S(2)}) collective-permute-start(bf16[14,96,128]{2,1,0:T(8,128)(2,1)} %after.7.refs_1_), channel_id=1, source_target_pairs={{0,1},{1,0},{2,3},{3,2},{4,5},{5,4},{6,7},{7,6},{8,9},{9,8},{10,11... | collective-permute-start | bytes 1032200 | tf_op jit(solution)/shard_map/ppermute | solution.py:444
  32.5 22.2 %collective-permute-start.9 = (bf16[4,5,96,128]{3,2,1,0:T(8,128)(2,1)}, bf16[4,5,96,128]{3,2,1,0:T(8,128)(2,1)S(1)}, u32[]{:S(2)}, u32[]{:S(2)}) collective-permute-start(bf16[4,5,96,128]{3,2,1,0:T(8,128)(2,1)} %after.8.refs_0_), channel_id=1, source_target_pairs={{0,8},{1,9},{2,10},{3,11},{4,12},{5,13},{6,14},{7,15},{8,0},{9,1},... | collective-permute-start | bytes 1474568 | tf_op jit(solution)/shard_map/ppermute | solution.py:444
  52.6 4.4 %collective-permute-start.12 = (bf16[14,96,128]{2,1,0:T(8,128)(2,1)S(1)}, bf16[14,96,128]{2,1,0:T(8,128)(2,1)S(1)}, u32[]{:S(2)}, u32[]{:S(2)}) collective-permute-start(bf16[14,96,128]{2,1,0:T(8,128)(2,1)S(1)} %copy-done.9), channel_id=1, source_target_pairs={{0,4},{1,5},{2,6},{3,7},{4,0},{5,1},{6,2},{7,3},{8,12},{9,13},{10,... | collective-permute-start | bytes 1032200 | tf_op jit(solution)/shard_map/ppermute | solution.py:444
  52.6 5.9 %collective-permute-start.15 = (bf16[14,96,128]{2,1,0:T(8,128)(2,1)}, bf16[14,96,128]{2,1,0:T(8,128)(2,1)}, u32[]{:S(2)}, u32[]{:S(2)}) collective-permute-start(bf16[14,96,128]{2,1,0:T(8,128)(2,1)} %copy-done.3), channel_id=1, source_target_pairs={{0,4},{1,5},{2,6},{3,7},{4,0},{5,1},{6,2},{7,3},{8,12},{9,13},{10,... | collective-permute-start | bytes 1032200 | tf_op jit(solution)/shard_map/ppermute | solution.py:444
  53.1 6.1 %collective-permute-start.14 = (bf16[14,96,128]{2,1,0:T(8,128)(2,1)}, bf16[14,96,128]{2,1,0:T(8,128)(2,1)}, u32[]{:S(2)}, u32[]{:S(2)}) collective-permute-start(bf16[14,96,128]{2,1,0:T(8,128)(2,1)} %copy-done.4), channel_id=1, source_target_pairs={{0,4},{1,5},{2,6},{3,7},{4,0},{5,1},{6,2},{7,3},{8,12},{9,13},{10,... | collective-permute-start | bytes 1032200 | tf_op jit(solution)/shard_map/ppermute | solution.py:444
  53.4 5.9 %collective-permute-start.13 = (bf16[14,96,128]{2,1,0:T(8,128)(2,1)}, bf16[14,96,128]{2,1,0:T(8,128)(2,1)}, u32[]{:S(2)}, u32[]{:S(2)}) collective-permute-start(bf16[14,96,128]{2,1,0:T(8,128)(2,1)} %copy-done.5), channel_id=1, source_target_pairs={{0,4},{1,5},{2,6},{3,7},{4,0},{5,1},{6,2},{7,3},{8,12},{9,13},{10,... | collective-permute-start | bytes 1032200 | tf_op jit(solution)/shard_map/ppermute | solution.py:444
  55.5 53.3 %collective-permute-start.20 = (bf16[3,14,96,128]{3,2,1,0:T(8,128)(2,1)}, bf16[3,14,96,128]{3,2,1,0:T(8,128)(2,1)}, u32[]{:S(2)}, u32[]{:S(2)}) collective-permute-start(bf16[3,14,96,128]{3,2,1,0:T(8,128)(2,1)} %after.9.refs_1_.refs_8_), channel_id=1, source_target_pairs={{0,8},{1,9},{2,10},{3,11},{4,12},{5,13},{6,14},{7,15},{8,0},{9,1},... | collective-permute-start | bytes 3096584 | tf_op jit(solution)/shard_map/ppermute | solution.py:444
  57.0 52.1 %collective-permute-start.21 = (bf16[3,14,96,128]{3,2,1,0:T(8,128)(2,1)}, bf16[3,14,96,128]{3,2,1,0:T(8,128)(2,1)}, u32[]{:S(2)}, u32[]{:S(2)}) collective-permute-start(bf16[3,14,96,128]{3,2,1,0:T(8,128)(2,1)} %after.9.refs_1_.refs_8_), channel_id=1, source_target_pairs={{0,16},{1,17},{2,18},{3,19},{4,20},{5,21},{6,22},{7,23},{8,24},{9,... | collective-permute-start | bytes 3096584 | tf_op jit(solution)/shard_map/ppermute | solution.py:444
  58.5 50.9 %collective-permute-start.22 = (bf16[3,14,96,128]{3,2,1,0:T(8,128)(2,1)}, bf16[3,14,96,128]{3,2,1,0:T(8,128)(2,1)S(1)}, u32[]{:S(2)}, u32[]{:S(2)}) collective-permute-start(bf16[3,14,96,128]{3,2,1,0:T(8,128)(2,1)} %after.9.refs_1_.refs_8_), channel_id=1, source_target_pairs={{0,24},{1,25},{2,26},{3,27},{4,28},{5,29},{6,30},{7,31},{8,16},{9,... | collective-permute-start | bytes 3096584 | tf_op jit(solution)/shard_map/ppermute | solution.py:444
  59.3 2.8 %collective-permute-start.19 = (bf16[4,5,96,128]{3,2,1,0:T(8,128)(2,1)}, bf16[4,5,96,128]{3,2,1,0:T(8,128)(2,1)}, u32[]{:S(2)}, u32[]{:S(2)}) collective-permute-start(bf16[4,5,96,128]{3,2,1,0:T(8,128)(2,1)} %copy-done.6), channel_id=1, source_target_pairs={{0,4},{1,5},{2,6},{3,7},{4,0},{5,1},{6,2},{7,3},{8,12},{9,13},{10,... | collective-permute-start | bytes 1474568 | tf_op jit(solution)/shard_map/ppermute | solution.py:444
  61.9 2.2 collective-permute-start.18
  62.1 2.8 %collective-permute-start.17 = (bf16[4,5,96,128]{3,2,1,0:T(8,128)(2,1)}, bf16[4,5,96,128]{3,2,1,0:T(8,128)(2,1)}, u32[]{:S(2)}, u32[]{:S(2)}) collective-permute-start(bf16[4,5,96,128]{3,2,1,0:T(8,128)(2,1)} %copy-done.8), channel_id=1, source_target_pairs={{0,4},{1,5},{2,6},{3,7},{4,0},{5,1},{6,2},{7,3},{8,12},{9,13},{10,... | collective-permute-start | bytes 1474568 | tf_op jit(solution)/shard_map/ppermute | solution.py:444
  64.1 46.5 %collective-permute-start.23 = (bf16[3,14,96,128]{3,2,1,0:T(8,128)(2,1)S(1)}, bf16[3,14,96,128]{3,2,1,0:T(8,128)(2,1)S(1)}, u32[]{:S(2)}, u32[]{:S(2)}) collective-permute-start(bf16[3,14,96,128]{3,2,1,0:T(8,128)(2,1)S(1)} %copy-done), channel_id=1, source_target_pairs={{0,4},{1,5},{2,6},{3,7},{4,0},{5,1},{6,2},{7,3},{8,12},{9,13},{10,... | collective-permute-start | bytes 3096584 | tf_op jit(solution)/shard_map/ppermute | solution.py:444
  108.9 3.0 %collective-permute-start.24 = (bf16[3,14,96,128]{3,2,1,0:T(8,128)(2,1)}, bf16[3,14,96,128]{3,2,1,0:T(8,128)(2,1)}, u32[]{:S(2)}, u32[]{:S(2)}) collective-permute-start(bf16[3,14,96,128]{3,2,1,0:T(8,128)(2,1)} %after.11.refs_9_), channel_id=1, source_target_pairs={{0,4},{1,5},{2,6},{3,7},{4,0},{5,1},{6,2},{7,3},{8,12},{9,13},{10,... | collective-permute-start | bytes 3096584 | tf_op jit(solution)/shard_map/ppermute | solution.py:444
  109.1 4.3 %collective-permute-start.25 = (bf16[3,14,96,128]{3,2,1,0:T(8,128)(2,1)}, bf16[3,14,96,128]{3,2,1,0:T(8,128)(2,1)}, u32[]{:S(2)}, u32[]{:S(2)}) collective-permute-start(bf16[3,14,96,128]{3,2,1,0:T(8,128)(2,1)} %after.12.refs_10_), channel_id=1, source_target_pairs={{0,4},{1,5},{2,6},{3,7},{4,0},{5,1},{6,2},{7,3},{8,12},{9,13},{10,... | collective-permute-start | bytes 3096584 | tf_op jit(solution)/shard_map/ppermute | solution.py:444
  110.5 4.3 %collective-permute-start.26 = (bf16[3,14,96,128]{3,2,1,0:T(8,128)(2,1)}, bf16[3,14,96,128]{3,2,1,0:T(8,128)(2,1)S(1)}, u32[]{:S(2)}, u32[]{:S(2)}) collective-permute-start(bf16[3,14,96,128]{3,2,1,0:T(8,128)(2,1)} %after.13.refs_11_), channel_id=1, source_target_pairs={{0,4},{1,5},{2,6},{3,7},{4,0},{5,1},{6,2},{7,3},{8,12},{9,13},{10,... | collective-permute-start | bytes 3096584 | tf_op jit(solution)/shard_map/ppermute | solution.py:444
  232.5 5.0 %collective-permute-start.30 = (f32[2,8,768]{2,1,0:T(8,128)S(1)}, f32[2,8,768]{2,1,0:T(8,128)S(1)}, u32[]{:S(2)}, u32[]{:S(2)}) collective-permute-start(f32[2,8,768]{2,1,0:T(8,128)S(1)} %add.73), channel_id=1, source_target_pairs={{0,24},{1,25},{2,26},{3,27},{4,28},{5,29},{6,30},{7,31},{8,16},{9,... | collective-permute-start | bytes 147464 | tf_op jit(solution)/shard_map/ppermute | solution.py:444
  234.7 4.1 %collective-permute-start.29 = (f32[2,8,768]{2,1,0:T(8,128)S(1)}, f32[2,8,768]{2,1,0:T(8,128)S(1)}, u32[]{:S(2)}, u32[]{:S(2)}) collective-permute-start(f32[2,8,768]{2,1,0:T(8,128)S(1)} %add.73), channel_id=1, source_target_pairs={{0,16},{1,17},{2,18},{3,19},{4,20},{5,21},{6,22},{7,23},{8,24},{9,... | collective-permute-start | bytes 147464 | tf_op jit(solution)/shard_map/ppermute | solution.py:444
  235.5 4.1 %collective-permute-start.28 = (f32[2,8,768]{2,1,0:T(8,128)S(1)}, f32[2,8,768]{2,1,0:T(8,128)S(1)}, u32[]{:S(2)}, u32[]{:S(2)}) collective-permute-start(f32[2,8,768]{2,1,0:T(8,128)S(1)} %add.73), channel_id=1, source_target_pairs={{0,8},{1,9},{2,10},{3,11},{4,12},{5,13},{6,14},{7,15},{8,0},{9,1},... | collective-permute-start | bytes 147464 | tf_op jit(solution)/shard_map/ppermute | solution.py:444
  239.6 6.3 %collective-permute-start.33 = (f32[2,8,768]{2,1,0:T(8,128)S(1)}, f32[2,8,768]{2,1,0:T(8,128)S(1)}, u32[]{:S(2)}, u32[]{:S(2)}) collective-permute-start(f32[2,8,768]{2,1,0:T(8,128)S(1)} %add_add_fusion), channel_id=1, source_target_pairs={{0,3},{1,2},{2,1},{3,0},{4,7},{5,6},{6,5},{7,4},{8,11},{9,10},{10,... | collective-permute-start | bytes 147464 | tf_op jit(solution)/shard_map/ppermute | solution.py:444
  241.5 5.6 %collective-permute-start.32 = (f32[2,8,768]{2,1,0:T(8,128)S(1)}, f32[2,8,768]{2,1,0:T(8,128)S(1)}, u32[]{:S(2)}, u32[]{:S(2)}) collective-permute-start(f32[2,8,768]{2,1,0:T(8,128)S(1)} %add_add_fusion), channel_id=1, source_target_pairs={{0,2},{1,3},{2,0},{3,1},{4,6},{5,7},{6,4},{7,5},{8,10},{9,11},{10,... | collective-permute-start | bytes 147464 | tf_op jit(solution)/shard_map/ppermute | solution.py:444
  243.6 4.1 %collective-permute-start.31 = (f32[2,8,768]{2,1,0:T(8,128)S(1)}, f32[2,8,768]{2,1,0:T(8,128)S(1)}, u32[]{:S(2)}, u32[]{:S(2)}) collective-permute-start(f32[2,8,768]{2,1,0:T(8,128)S(1)} %add_add_fusion), channel_id=1, source_target_pairs={{0,1},{1,0},{2,3},{3,2},{4,5},{5,4},{6,7},{7,6},{8,9},{9,8},{10,11... | collective-permute-start | bytes 147464 | tf_op jit(solution)/shard_map/ppermute | solution.py:444
  (17 other events, 140.3 us)
